TPU v7x, 32 devices: a whole 2x2x4 slice. The times are simulated.
32 devices in a mesh: dp: 4 (over x, core), fsdp: 8 (over z, y).
Axes of the slice: x: 2, y: 2, z: 4, core: 2. Of those that a mesh axis runs over, the one named last changes fastest.
Arguments:
- inputs: bfloat16 [8192, 2048], P(('dp', 'fsdp')), may hold values from -18 to 18
- kv_input: bfloat16 [8192, 2048], P(('dp', 'fsdp')), may hold values from -6 to 6
- segment_ids: int32 [8192], P(('dp', 'fsdp')), may hold values from 0 to 15, never falling along the last dimension, each value on 1 to 1024 neighbouring positions
- valid_mask: int32 [8192], P(('dp', 'fsdp')), may hold values from 0 to 1, as said below
- w_query: bfloat16 [2048, 2048], P(('dp', 'fsdp')), may hold values from -0.125 to 0.125
- w_key: bfloat16 [2048, 2048], P(('dp', 'fsdp')), may hold values from -0.125 to 0.125
- w_value: bfloat16 [2048, 2048], P(('dp', 'fsdp')), may hold values from -0.125 to 0.125
- w_out: bfloat16 [2048, 2048], P(('dp', 'fsdp')), may hold values from -1 to 1
- w_gate: bfloat16 [2048, 5504], P(('dp', 'fsdp')), may hold values from -0.125 to 0.125
- w_up: bfloat16 [2048, 5504], P(('dp', 'fsdp')), may hold values from -0.125 to 0.125
- w_down: bfloat16 [5504, 2048], P(('dp', 'fsdp')), may hold values from -0.078125 to 0.078125
- gain_attn: bfloat16 [2048], P(('dp', 'fsdp')), may hold values from 0.099609375 to 1.8984375
- gain_ffn: bfloat16 [2048], P(('dp', 'fsdp')), may hold values from 0.099609375 to 1.8984375
- cotangent: bfloat16 [8192, 2048], P(('dp', 'fsdp')), may hold values from -6 to 6
Outputs:
- output: bfloat16 [8192, 2048], P(('dp', 'fsdp'))
- grad_inputs: float32 [8192, 2048], P(('dp', 'fsdp'))
- grad_kv_input: float32 [8192, 2048], P(('dp', 'fsdp'))
- grad_w_query: float32 [2048, 2048], P(('dp', 'fsdp'))
- grad_w_key: float32 [2048, 2048], P(('dp', 'fsdp'))
- grad_w_value: float32 [2048, 2048], P(('dp', 'fsdp'))
- grad_w_out: float32 [2048, 2048], P(('dp', 'fsdp'))
- grad_w_gate: float32 [2048, 5504], P(('dp', 'fsdp'))
- grad_w_up: float32 [2048, 5504], P(('dp', 'fsdp'))
- grad_w_down: float32 [5504, 2048], P(('dp', 'fsdp'))
- grad_gain_attn: float32 [2048], P(('dp', 'fsdp'))
- grad_gain_ffn: float32 [2048], P(('dp', 'fsdp'))
- rms_in: float32 [], replicated
- rms_mid: float32 [], replicated
- rms_out: float32 [], replicated
Inputs may be any that keep to these rules, and one draw needn't show every extreme that they name: `valid_mask`: 1 for real tokens; padding fills the last 0 to 256 tokens of each block of 2048. `segment_ids`: never falling along the tokens; each id covers 1 to 1024 consecutive tokens.
All inputs are finite; a program needn't handle non-finite values.
Results may differ from a plain program's by a relative error of at most 0.017.
Values may be sent and summed in bfloat16 or wider, within the bound.
No kernel may reach another device: no remote copies, remote signals or barrier semaphores. Data moves between devices by JAX's collectives and lax.ppermute only.
A program may use at most 576 MiB of HBM per device.

v0:
```python
import math

import jax
import jax.numpy as jnp
from jax import lax
from jax.sharding import PartitionSpec as P

HEADS = 16
HEAD_DIM = 128
SEQ_LEN = 4096


EPSILON = 1e-06


def unit_rows(values):
    factor = lax.rsqrt(jnp.mean(values * values, axis=-1, keepdims=True) + EPSILON)
    return (values * factor, factor)


def unit_back(grad_normed, unit_vals, factor, gains):
    grad_gain = jnp.sum(grad_normed * unit_vals, axis=0)
    inner = grad_normed * gains
    grad_in = factor * (inner - unit_vals * jnp.mean(inner * unit_vals, axis=-1, keepdims=True))
    return (grad_in, grad_gain)


def forward_dot(left_side, right_side):
    return jnp.dot(left_side, right_side, preferred_element_type=jnp.float32)


def right_trans(left_side, right_side):
    return lax.dot_general(
        left_side, right_side, (((1,), (1,)), ((), ())), preferred_element_type=jnp.float32
    )


def left_trans(left_side, right_side):
    return lax.dot_general(
        left_side, right_side, (((0,), (0,)), ((), ())), preferred_element_type=jnp.float32
    )


def attention_weights(w_query, w_key, w_value, gain_attn):
    return (
        lax.all_gather(w_query, ("dp", "fsdp"), axis=0, tiled=True),
        lax.all_gather(w_key, ("dp", "fsdp"), axis=0, tiled=True),
        lax.all_gather(w_value, ("dp", "fsdp"), axis=0, tiled=True),
        lax.all_gather(gain_attn, ("dp", "fsdp"), axis=0, tiled=True),
    )


def output_weight(w_out):
    return lax.all_gather(w_out, ("dp", "fsdp"), axis=0, tiled=True)


def feed_weights(w_gate, w_up, gain_ffn):
    return (
        lax.all_gather(w_gate, ("dp", "fsdp"), axis=0, tiled=True),
        lax.all_gather(w_up, ("dp", "fsdp"), axis=0, tiled=True),
        lax.all_gather(gain_ffn, ("dp", "fsdp"), axis=0, tiled=True),
    )


def down_weight(w_down):
    return lax.all_gather(w_down, ("dp", "fsdp"), axis=0, tiled=True)


def shared_keys(key_proj, value_proj, segment_ids, valid_mask):
    return (
        lax.all_gather(key_proj, "fsdp", axis=0, tiled=True),
        lax.all_gather(value_proj, "fsdp", axis=0, tiled=True),
        lax.all_gather(segment_ids, "fsdp", axis=0, tiled=True),
        lax.all_gather(valid_mask, "fsdp", axis=0, tiled=True),
    )


def key_block(
    query_heads,
    key_all,
    segment_all,
    valid_all,
    segment_mine,
    query_pos,
    seq_length,
    block_start,
    block_rows,
):
    score_scale = 1.0 / math.sqrt(HEAD_DIM)
    key_heads = lax.dynamic_slice_in_dim(key_all, block_start, block_rows, 0).reshape(
        block_rows, HEADS, HEAD_DIM
    )
    segment_keys = lax.dynamic_slice_in_dim(segment_all, block_start, block_rows, 0)
    valid_keys = lax.dynamic_slice_in_dim(valid_all, block_start, block_rows, 0)
    key_pos = block_start + jnp.arange(block_rows, dtype=jnp.int32)
    allowed = (segment_mine[:, None] == segment_keys[None, :]) & (
        (query_pos // seq_length)[:, None] == (key_pos // seq_length)[None, :]
    )
    allowed = allowed & (key_pos[None, :] <= query_pos[:, None])
    allowed = allowed & ((valid_keys[None, :] == 1) | (key_pos[None, :] == query_pos[:, None]))
    scores = (
        jnp.einsum("qhd,khd->hqk", query_heads, key_heads, preferred_element_type=jnp.float32)
        * score_scale
    )
    weights = jnp.where(allowed[None, :, :], jnp.exp(scores), 0.0)
    return (weights, key_heads)


def attend_forward(
    queries, key_all, value_all, segment_all, valid_all, segment_mine, first_query, seq_length
):
    rows_here = queries.shape[0]
    key_count = key_all.shape[0]
    block_rows = min(512, key_count)
    query_heads = queries.reshape(rows_here, HEADS, HEAD_DIM)
    query_pos = first_query + jnp.arange(rows_here, dtype=jnp.int32)
    seq_start = first_query // seq_length * seq_length
    last_query = first_query + rows_here - 1

    def one_step(block_index, state):
        block_start = block_index * block_rows

        def accumulate(inner):
            summed, totals = inner
            weights, key_heads = key_block(
                query_heads,
                key_all,
                segment_all,
                valid_all,
                segment_mine,
                query_pos,
                seq_length,
                block_start,
                block_rows,
            )
            value_heads = lax.dynamic_slice_in_dim(value_all, block_start, block_rows, 0).reshape(
                block_rows, HEADS, HEAD_DIM
            )
            totals = totals + jnp.sum(weights, axis=-1)
            summed = summed + jnp.einsum(
                "hqk,khd->qhd",
                weights.astype(jnp.bfloat16),
                value_heads,
                preferred_element_type=jnp.float32,
            )
            return (summed, totals)

        needed = (block_start <= last_query) & (block_start + block_rows - 1 >= seq_start)
        return lax.cond(needed, accumulate, lambda inner: inner, state)

    start_state = (
        jnp.zeros((rows_here, HEADS, HEAD_DIM), jnp.float32),
        jnp.zeros((HEADS, rows_here), jnp.float32),
    )
    summed, totals = lax.fori_loop(0, key_count // block_rows, one_step, start_state)
    attended_f = (summed / jnp.transpose(totals)[:, :, None]).reshape(rows_here, HEADS * HEAD_DIM)
    return (attended_f, totals)


def attend_backward(
    queries,
    key_all,
    value_all,
    segment_all,
    valid_all,
    segment_mine,
    first_query,
    seq_length,
    grad_unnorm,
    grad_totals,
):
    score_scale = 1.0 / math.sqrt(HEAD_DIM)
    rows_here = queries.shape[0]
    key_count = key_all.shape[0]
    block_rows = min(512, key_count)
    query_heads = queries.reshape(rows_here, HEADS, HEAD_DIM)
    query_pos = first_query + jnp.arange(rows_here, dtype=jnp.int32)
    seq_start = first_query // seq_length * seq_length
    last_query = first_query + rows_here - 1

    def one_step(block_index, state):
        block_start = block_index * block_rows

        def accumulate(inner):
            weights, key_heads = key_block(
                query_heads,
                key_all,
                segment_all,
                valid_all,
                segment_mine,
                query_pos,
                seq_length,
                block_start,
                block_rows,
            )
            value_heads = lax.dynamic_slice_in_dim(value_all, block_start, block_rows, 0).reshape(
                block_rows, HEADS, HEAD_DIM
            )
            grad_weights = jnp.einsum(
                "qhd,khd->hqk", grad_unnorm, value_heads, preferred_element_type=jnp.float32
            )
            grad_scores = (weights * (grad_weights + grad_totals[:, :, None])).astype(jnp.bfloat16)
            grad_query = inner[0] + score_scale * jnp.einsum(
                "hqk,khd->qhd", grad_scores, key_heads, preferred_element_type=jnp.float32
            )
            part_keys = score_scale * jnp.einsum(
                "hqk,qhd->khd", grad_scores, query_heads, preferred_element_type=jnp.float32
            )
            part_values = jnp.einsum(
                "hqk,qhd->khd",
                weights.astype(jnp.bfloat16),
                grad_unnorm,
                preferred_element_type=jnp.float32,
            )
            grad_keys = lax.dynamic_update_slice_in_dim(
                inner[1], part_keys.reshape(block_rows, HEADS * HEAD_DIM), block_start, 0
            )
            grad_values = lax.dynamic_update_slice_in_dim(
                inner[2], part_values.reshape(block_rows, HEADS * HEAD_DIM), block_start, 0
            )
            return (grad_query, grad_keys, grad_values)

        needed = (block_start <= last_query) & (block_start + block_rows - 1 >= seq_start)
        return lax.cond(needed, accumulate, lambda inner: inner, state)

    start_state = (
        jnp.zeros((rows_here, HEADS, HEAD_DIM), jnp.float32),
        jnp.zeros((key_count, HEADS * HEAD_DIM), jnp.float32),
        jnp.zeros((key_count, HEADS * HEAD_DIM), jnp.float32),
    )
    final_state = lax.fori_loop(0, key_count // block_rows, one_step, start_state)
    grad_query = final_state[0].reshape(rows_here, HEADS * HEAD_DIM)
    return (grad_query, final_state[1], final_state[2])


def shards(
    inputs,
    kv_input,
    segment_ids,
    valid_mask,
    w_query,
    w_key,
    w_value,
    w_out,
    w_gate,
    w_up,
    w_down,
    gain_attn,
    gain_ffn,
    cotangent,
):
    rows_here = inputs.shape[0]
    width_model = inputs.shape[1]
    group_rows = rows_here * lax.axis_size("fsdp")
    seq_length = min(SEQ_LEN, group_rows)
    first_query = lax.axis_index("fsdp") * rows_here
    stream = inputs.astype(jnp.float32)
    full_query, full_key, full_value, full_gain_attn = attention_weights(
        w_query, w_key, w_value, gain_attn
    )
    unit_one, factor_one = unit_rows(stream)
    normed1 = (unit_one * full_gain_attn.astype(jnp.float32)).astype(jnp.bfloat16)
    queries = forward_dot(normed1, full_query).astype(jnp.bfloat16)
    key_proj = forward_dot(kv_input, full_key).astype(jnp.bfloat16)
    value_proj = forward_dot(kv_input, full_value).astype(jnp.bfloat16)
    key_all, value_all, segment_all, valid_all = shared_keys(
        key_proj, value_proj, segment_ids, valid_mask
    )
    attended_f, totals = attend_forward(
        queries, key_all, value_all, segment_all, valid_all, segment_ids, first_query, seq_length
    )
    attended = attended_f.astype(jnp.bfloat16)
    full_out = output_weight(w_out)
    middle = stream + forward_dot(attended, full_out)
    unit_two, factor_two = unit_rows(middle)
    full_gate, full_up, full_gain_ffn = feed_weights(w_gate, w_up, gain_ffn)
    normed2 = (unit_two * full_gain_ffn.astype(jnp.float32)).astype(jnp.bfloat16)
    gate_proj = forward_dot(normed2, full_gate)
    up_proj = forward_dot(normed2, full_up)
    activation_f, silu_pull = jax.vjp(
        lambda gate_in, up_in: jax.nn.silu(gate_in) * up_in, gate_proj, up_proj
    )
    activation = activation_f.astype(jnp.bfloat16)
    full_down = down_weight(w_down)
    result = middle + forward_dot(activation, full_down)
    back_down = down_weight(w_down)
    back_gate, back_up, back_gain_ffn = feed_weights(w_gate, w_up, gain_ffn)
    grad_w_down = left_trans(activation, cotangent)
    grad_activation = right_trans(cotangent, back_down)
    grad_gate_f, grad_up_f = silu_pull(grad_activation)
    grad_gate = grad_gate_f.astype(jnp.bfloat16)
    grad_up = grad_up_f.astype(jnp.bfloat16)
    grad_w_gate = left_trans(normed2, grad_gate)
    grad_w_up = left_trans(normed2, grad_up)
    grad_normed2 = right_trans(grad_gate, back_gate) + right_trans(grad_up, back_up)
    grad_mid_norm, grad_gain_ffn = unit_back(
        grad_normed2, unit_two, factor_two, back_gain_ffn.astype(jnp.float32)
    )
    grad_middle = cotangent.astype(jnp.float32) + grad_mid_norm
    share_gate, share_up, share_gain_ffn = (
        lax.psum_scatter(grad_w_gate, ("dp", "fsdp"), scatter_dimension=0, tiled=True),
        lax.psum_scatter(grad_w_up, ("dp", "fsdp"), scatter_dimension=0, tiled=True),
        lax.psum_scatter(grad_gain_ffn, ("dp", "fsdp"), scatter_dimension=0, tiled=True),
    )
    share_down = lax.psum_scatter(grad_w_down, ("dp", "fsdp"), scatter_dimension=0, tiled=True)
    back_out = output_weight(w_out)
    grad_branch = grad_middle.astype(jnp.bfloat16)
    grad_w_out = left_trans(attended, grad_branch)
    share_out = lax.psum_scatter(grad_w_out, ("dp", "fsdp"), scatter_dimension=0, tiled=True)
    grad_attended = right_trans(grad_branch, back_out)
    head_prod = jnp.sum((grad_attended * attended_f).reshape(rows_here, HEADS, HEAD_DIM), axis=-1)
    grad_totals = -jnp.transpose(head_prod) / totals
    grad_unnorm = (
        grad_attended.reshape(rows_here, HEADS, HEAD_DIM) / jnp.transpose(totals)[:, :, None]
    ).astype(jnp.bfloat16)
    back_keys, back_values, back_segments, back_valid = shared_keys(
        key_proj, value_proj, segment_ids, valid_mask
    )
    grad_query_f, grad_keys_all, grad_values_all = attend_backward(
        queries,
        back_keys,
        back_values,
        back_segments,
        back_valid,
        segment_ids,
        first_query,
        seq_length,
        grad_unnorm,
        grad_totals,
    )
    own_keys, own_values = (
        lax.psum_scatter(
            grad_keys_all.astype(jnp.bfloat16), "fsdp", scatter_dimension=0, tiled=True
        ).astype(jnp.float32),
        lax.psum_scatter(
            grad_values_all.astype(jnp.bfloat16), "fsdp", scatter_dimension=0, tiled=True
        ).astype(jnp.float32),
    )
    grad_queries = grad_query_f.astype(jnp.bfloat16)
    grad_keys = own_keys.astype(jnp.bfloat16)
    grad_values = own_values.astype(jnp.bfloat16)
    back_query, back_key, back_value, back_gain_attn = attention_weights(
        w_query, w_key, w_value, gain_attn
    )
    grad_w_query = left_trans(normed1, grad_queries)
    grad_w_key = left_trans(kv_input, grad_keys)
    grad_w_value = left_trans(kv_input, grad_values)
    grad_kv_input = right_trans(grad_keys, back_key) + right_trans(grad_values, back_value)
    grad_normed1 = right_trans(grad_queries, back_query)
    grad_in_norm, grad_gain_attn = unit_back(
        grad_normed1, unit_one, factor_one, back_gain_attn.astype(jnp.float32)
    )
    grad_inputs = grad_middle + grad_in_norm
    share_query, share_key, share_value, share_gain_attn = (
        lax.psum_scatter(grad_w_query, ("dp", "fsdp"), scatter_dimension=0, tiled=True),
        lax.psum_scatter(grad_w_key, ("dp", "fsdp"), scatter_dimension=0, tiled=True),
        lax.psum_scatter(grad_w_value, ("dp", "fsdp"), scatter_dimension=0, tiled=True),
        lax.psum_scatter(grad_gain_attn, ("dp", "fsdp"), scatter_dimension=0, tiled=True),
    )
    valid_float = valid_mask.astype(jnp.float32)
    sums = lax.psum(
        (
            jnp.sum(valid_float * jnp.sum(stream * stream, axis=-1)),
            jnp.sum(valid_float * jnp.sum(middle * middle, axis=-1)),
            jnp.sum(valid_float * jnp.sum(result * result, axis=-1)),
            jnp.sum(valid_float),
        ),
        ("dp", "fsdp"),
    )
    divisor = sums[3] * width_model
    rms_in = jnp.sqrt(sums[0] / divisor)
    rms_mid = jnp.sqrt(sums[1] / divisor)
    rms_out = jnp.sqrt(sums[2] / divisor)
    return (
        result.astype(jnp.bfloat16),
        grad_inputs,
        grad_kv_input,
        share_query,
        share_key,
        share_value,
        share_out,
        share_gate,
        share_up,
        share_down,
        share_gain_attn,
        share_gain_ffn,
        rms_in,
        rms_mid,
        rms_out,
    )


def solution(mesh):
    placed = (
        P(("dp", "fsdp"), None),
        P(("dp", "fsdp"), None),
        P(("dp", "fsdp")),
        P(("dp", "fsdp")),
        P(("dp", "fsdp"), None),
        P(("dp", "fsdp"), None),
        P(("dp", "fsdp"), None),
        P(("dp", "fsdp"), None),
        P(("dp", "fsdp"), None),
        P(("dp", "fsdp"), None),
        P(("dp", "fsdp"), None),
        P(("dp", "fsdp")),
        P(("dp", "fsdp")),
        P(("dp", "fsdp"), None),
    )
    return jax.shard_map(
        shards,
        mesh=mesh,
        in_specs=placed,
        out_specs=(
            P(("dp", "fsdp"), None),
            P(("dp", "fsdp"), None),
            P(("dp", "fsdp"), None),
            P(("dp", "fsdp"), None),
            P(("dp", "fsdp"), None),
            P(("dp", "fsdp"), None),
            P(("dp", "fsdp"), None),
            P(("dp", "fsdp"), None),
            P(("dp", "fsdp"), None),
            P(("dp", "fsdp"), None),
            P(("dp", "fsdp")),
            P(("dp", "fsdp")),
            P(),
            P(),
            P(),
        ),
        check_vma=False,
    )
```

profile of v0, /device:TPU:0, one launch (start us, length us, event | category | flops | bytes accessed | tf_op | source)
XLA Modules:
  0.0 5777.2 jit_solution(5794620267871336300)
XLA Ops:
  9.5 81.7 %all-gather.13.cloned.1.call-done = bf16[2048,2048]{1,0:T(8,128)(2,1)} async-done(((bf16[64,2048]{1,0:T(8,128)(2,1)}), bf16[2048,2048]{1,0:T(8,128)(2,1)}) %all-gather.13.cloned.1.call-update) | async-done | bytes 8388624 | tf_op jit(solution)/shard_map/all_gather | solution.py:48
  97.9 72.2 %all-gather.17.cloned.1.call-done = bf16[2048,2048]{1,0:T(8,128)(2,1)} async-done(((bf16[64,2048]{1,0:T(8,128)(2,1)}), bf16[2048,2048]{1,0:T(8,128)(2,1)}) %all-gather.17.cloned.1.call-update) | async-done | bytes 8388624 | tf_op jit(solution)/shard_map/all_gather | solution.py:47
  180.3 39.8 all-reduce.7
  220.1 20.1 all-gather
  266.6 108.8 %all-gather.15.cloned.1.call-done = bf16[2048,2048]{1,0:T(8,128)(2,1)} async-done(((bf16[256,2048]{1,0:T(8,128)(2,1)}), bf16[2048,2048]{1,0:T(8,128)(2,1)}) %all-gather.15.cloned.1.call-update) | async-done | bytes 8388624 | tf_op jit(solution)/shard_map/all_gather | solution.py:72
  387.9 113.2 %all-gather.19.cloned.1.call-done = bf16[2048,2048]{1,0:T(8,128)(2,1)} async-done(((bf16[256,2048]{1,0:T(8,128)(2,1)}), bf16[2048,2048]{1,0:T(8,128)(2,1)}) %all-gather.19.cloned.1.call-update) | async-done | bytes 8388624 | tf_op jit(solution)/shard_map/all_gather | solution.py:71
  524.9 54.8 all-gather.23.cloned.1.call-done
  588.3 137.5 %all-gather.29.cloned.1.call-done = bf16[32,172,2048]{2,1,0:T(8,128)(2,1)} async-done(((bf16[1,172,2048]{2,1,0:T(8,128)(2,1)}), bf16[32,172,2048]{2,1,0:T(8,128)(2,1)}) %all-gather.29.cloned.1.call-update) | async-done | bytes 22544400 | tf_op jit(solution)/shard_map/all_gather | solution.py:66
  725.8 22.2 reshape.392
  748.0 120.9 %all-gather.27.cloned.1.call-done = bf16[2048,5504]{1,0:T(8,128)(2,1)} async-done(((bf16[64,5504]{1,0:T(8,128)(2,1)}), bf16[2048,5504]{1,0:T(8,128)(2,1)}) %all-gather.27.cloned.1.call-update) | async-done | bytes 22544400 | tf_op jit(solution)/shard_map/all_gather | solution.py:60
  881.4 130.6 %all-gather.25.cloned.1.call-done = bf16[2048,5504]{1,0:T(8,128)(2,1)} async-done(((bf16[64,5504]{1,0:T(8,128)(2,1)}), bf16[2048,5504]{1,0:T(8,128)(2,1)}) %all-gather.25.cloned.1.call-update) | async-done | bytes 22544400 | tf_op jit(solution)/shard_map/all_gather | solution.py:59
  1024.8 24.7 multiply_convert_fusion
  1146.2 168.2 %reduce-scatter.17.cloned.1.call-done = bf16[256,2048]{0,1:T(8,128)(2,1)} async-done(((bf16[2048,2048]{0,1:T(8,128)(2,1)}), bf16[256,2048]{0,1:T(8,128)(2,1)}) %reduce-scatter.17.cloned.1.call-update) | async-done | bytes 1048592 | tf_op jit(solution)/shard_map/reduce_scatter | solution.py:335
  1323.7 18.2 copy.96
  1342.0 124.9 %reduce-scatter.15.cloned.1.call-done = bf16[256,2048]{0,1:T(8,128)(2,1)} async-done(((bf16[2048,2048]{0,1:T(8,128)(2,1)}), bf16[256,2048]{0,1:T(8,128)(2,1)}) %reduce-scatter.15.cloned.1.call-update) | async-done | bytes 1048592 | tf_op jit(solution)/shard_map/reduce_scatter | solution.py:332
  1476.5 17.7 copy.94
  1495.4 19.5 fusion.61
  1515.3 19.6 fusion.60
  1536.1 19.4 fusion.62
  1555.5 1864.4 %fusion.4 = f32[176,2048]{1,0:T(8,128)S(1)} fusion(f32[5504,2048]{1,0:T(8,128)} %fusion.62), kind=kCustom, calls=%all-reduce-scatter | all-reduce-scatter fusion | flops 11534337 | bytes 46530560
  3442.0 94.3 %all-reduce.6 = (f32[2048]{0:T(1024)S(1)}, f32[2048]{0:T(1024)S(1)}, f32[]{:T(128)}, f32[]{:T(128)}, f32[]{:T(128)}, /*index=5*/f32[]{:T(128)}) all-reduce(f32[2048]{0:T(1024)S(1)} %get-tuple-element.1179, f32[2048]{0:T(1024)S(1)} %copy-done.32, f32[]{:T(128)} %get-tuple-element.1184, ...), channel_id=11, replica_groups=mesh['dp'=4,'fsdp'=8] {'dp','fsdp'}, use_global_device_ids=true, to_apply=%region_24.25.clone | all-reduce | flops 4100 | bytes 32800
  3564.8 306.4 %reduce-scatter.27.cloned.1.call-done = f32[64,2048]{1,0:T(8,128)} async-done(((f32[2048,2048]{1,0:T(8,128)}), f32[64,2048]{1,0:T(8,128)}) %reduce-scatter.27.cloned.1.call-update) | async-done | bytes 524304
  3871.2 947.6 %reduce-scatter.25.cloned.1.call-done = f32[64,5504]{1,0:T(8,128)} async-done(((f32[2048,5504]{1,0:T(8,128)}), f32[64,5504]{1,0:T(8,128)}) %reduce-scatter.25.cloned.1.call-update) | async-done | bytes 1409040 | tf_op jit(solution)/shard_map/reduce_scatter | solution.py:302
  4818.8 948.3 %reduce-scatter.23.cloned.1.call-done = f32[64,5504]{1,0:T(8,128)} async-done(((f32[2048,5504]{1,0:T(8,128)}), f32[64,5504]{1,0:T(8,128)}) %reduce-scatter.23.cloned.1.call-update) | async-done | bytes 1409040 | tf_op jit(solution)/shard_map/reduce_scatter | solution.py:301
  (222 shorter events, 324.5 us)
Async XLA Ops:
  7.2 84.0 %copy-start = (bf16[256,2048]{1,0:T(8,128)(2,1)S(1)}, bf16[256,2048]{1,0:T(8,128)(2,1)}, u32[]{:S(2)}) copy-start(bf16[256,2048]{1,0:T(8,128)(2,1)} %param.23) | copy-start | bytes 3145732
  7.2 84.0 %all-gather.13.cloned.1.call-start = ((), (), s32[]{:S(2)}) async-start(), calls=%async_computation.8 | async-start | bytes 8650752 | tf_op jit(solution)/shard_map/all_gather | solution.py:48
  7.9 162.2 %all-gather.17.cloned.1.call-start = ((), (), s32[]{:S(2)}) async-start(), calls=%async_computation.10 | async-start | bytes 8650752 | tf_op jit(solution)/shard_map/all_gather | solution.py:47
  8.7 248.1 %all-gather.21.cloned.1.call-start = ((), (), s32[]{:S(2)}) async-start(), calls=%async_computation.12 | async-start | bytes 8650752 | tf_op jit(solution)/shard_map/all_gather | solution.py:46
  9.4 366.1 %all-gather.15.cloned.1.call-start = ((), (), s32[]{:S(2)}) async-start(), calls=%async_computation.9 | async-start | bytes 9437184 | tf_op jit(solution)/shard_map/all_gather | solution.py:72
  97.9 403.3 %all-gather.19.cloned.1.call-start = ((), (), s32[]{:S(2)}) async-start(), calls=%async_computation.11 | async-start | bytes 9437184 | tf_op jit(solution)/shard_map/all_gather | solution.py:71
  176.8 63.4 %copy-start.33 = (s32[256]{0:T(256)S(1)}, s32[256]{0:T(256)}, u32[]{:S(2)}) copy-start(s32[256]{0:T(256)} %param.25) | copy-start | bytes 3076
  176.8 79.6 %copy-start.11 = (bf16[256,2048]{1,0:T(8,128)(2,1)S(1)}, bf16[256,2048]{1,0:T(8,128)(2,1)}, u32[]{:S(2)}) copy-start(bf16[256,2048]{1,0:T(8,128)(2,1)} %param.22) | copy-start | bytes 3145732
  176.9 402.8 %all-gather.23.cloned.1.call-start = ((), (), s32[]{:S(2)}) async-start(), calls=%async_computation.13 | async-start | bytes 8650752 | tf_op jit(solution)/shard_map/all_gather | solution.py:54
  177.5 548.3 %all-gather.29.cloned.1.call-start = ((), (), s32[]{:S(2)}) async-start(), calls=%async_computation.22 | async-start | bytes 23789568 | tf_op jit(solution)/shard_map/all_gather | solution.py:66
  178.2 690.7 %all-gather.27.cloned.1.call-start = ((), (), s32[]{:S(2)}) async-start(), calls=%async_computation.15 | async-start | bytes 23248896 | tf_op jit(solution)/shard_map/all_gather | solution.py:60
  179.0 833.1 %all-gather.25.cloned.1.call-start = ((), (), s32[]{:S(2)}) async-start(), calls=%async_computation.14 | async-start | bytes 23248896 | tf_op jit(solution)/shard_map/all_gather | solution.py:59
  179.7 1134.7 %reduce-scatter.17.cloned.1.call-start = ((), (), s32[]{:S(2)}) async-start(), calls=%async_computation.17 | async-start | bytes 9437184 | tf_op jit(solution)/shard_map/reduce_scatter | solution.py:335
  220.1 43.3 copy-start.25
  524.9 561.7 %copy-start.5 = (f32[256,2048]{1,0:T(8,128)}, f32[256,2048]{1,0:T(8,128)S(1)}, u32[]{:S(2)}) copy-start(f32[256,2048]{1,0:T(8,128)S(1)} %copy.92) | copy-start | bytes 6291460
  1123.6 343.3 %reduce-scatter.15.cloned.1.call-start = ((), (), s32[]{:S(2)}) async-start(), calls=%async_computation.16 | async-start | bytes 9437184 | tf_op jit(solution)/shard_map/reduce_scatter | solution.py:332
  1124.4 2440.5 %reduce-scatter.21.cloned.1.call-start = ((), (), s32[]{:S(2)}) async-start(), calls=%async_computation.19 | async-start | bytes 17301504 | tf_op jit(solution)/shard_map/reduce_scatter | solution.py:309
  1135.0 2429.8 %reduce-scatter.19.cloned.1.call-start = ((), (), s32[]{:S(2)}) async-start(), calls=%async_computation.18 | async-start | bytes 17301504 | tf_op jit(solution)/shard_map/reduce_scatter | solution.py:355
  1145.9 2418.9 %reduce-scatter.29.cloned.1.call-start = ((), (), s32[]{:S(2)}) async-start(), calls=%async_computation.24 | async-start | bytes 17301504
  1341.9 2529.3 %reduce-scatter.27.cloned.1.call-start = ((), (), s32[]{:S(2)}) async-start(), calls=%async_computation.23 | async-start | bytes 17301504
  1494.2 3324.6 %reduce-scatter.25.cloned.1.call-start = ((), (), s32[]{:S(2)}) async-start(), calls=%async_computation.21 | async-start | bytes 46497792 | tf_op jit(solution)/shard_map/reduce_scatter | solution.py:302
  1515.0 4252.1 %reduce-scatter.23.cloned.1.call-start = ((), (), s32[]{:S(2)}) async-start(), calls=%async_computation.20 | async-start | bytes 46497792 | tf_op jit(solution)/shard_map/reduce_scatter | solution.py:301
  3421.1 122.9 %collective-permute-start = (f32[124,2048]{1,0:T(8,128)}, f32[124,2048]{1,0:T(8,128)}, u32[]{:S(2)}, u32[]{:S(2)}) collective-permute-start(f32[124,2048]{1,0:T(8,128)} %slice), channel_id=1, source_target_pairs={{0,1},{1,2},{2,3},{3,4},{4,5},{5,6},{6,7},{7,8},{8,9},{9,10},{10,1... | collective-permute-start | bytes 3047432
  3437.2 102.9 %copy-start.8 = (f32[256,2048]{1,0:T(8,128)S(1)}, f32[256,2048]{1,0:T(8,128)}, u32[]{:S(2)}) copy-start(f32[256,2048]{1,0:T(8,128)} %copy-done.7) | copy-start | bytes 6291460
  (35 other events, 220.0 us)
Sparse Core Ops, SparseCore 0:
  11.0 80.0 all-gather.12
  94.1 75.9 all-gather.16
  173.1 76.1 all-gather.20
  251.9 123.5 all-gather.14
  378.0 123.1 all-gather.18
  504.0 75.5 all-gather.22
  582.6 143.1 all-gather.28
  728.6 140.2 all-gather.26
  871.8 140.2 all-gather.24
  1123.7 190.5 reduce-scatter.16
  1318.5 148.4 reduce-scatter.14
  1469.7 640.5 reduce-scatter.20
  2113.2 724.6 reduce-scatter.18
  2840.6 668.0 reduce-scatter.28
  3511.4 359.7 reduce-scatter.26
  3874.0 944.7 reduce-scatter.24
  4821.5 945.5 reduce-scatter.22
where the time goes:
time: 5790 us; the launch traced here: 5780 us
  waiting for transfers between devices  3320 us (57%)
  blocking collectives  2030 us (35%)
  matrix products  248 us (4%)
  local copies, waits for them, and re-layouts  131 us (2%)
    unnamed x3, blocking collectives  2000 us
    reduce_scatter x1, waiting for transfers between devices, shards(): lax.psum_scatter(grad_w_gate, ('dp', 'fsdp'), scatter_dimension=0, tiled=...  948 us
    reduce_scatter x1, waiting for transfers between devices, shards(): lax.psum_scatter(grad_w_up, ('dp', 'fsdp'), scatter_dimension=0, tiled=True)  948 us
    unnamed x20, waiting for transfers between devices  312 us
    reduce_scatter x1, waiting for transfers between devices, shards(): lax.psum_scatter(grad_values_all.astype(jnp.bfloat16), 'fsdp', scatter_di...  168 us
    all_gather x1, waiting for transfers between devices, down_weight(): return lax.all_gather(w_down, ('dp', 'fsdp'), axis=0, tiled=True)  138 us
    all_gather x1, waiting for transfers between devices, feed_weights(): lax.all_gather(w_gate, ('dp', 'fsdp'), axis=0, tiled=True)  131 us
    reduce_scatter x1, waiting for transfers between devices, shards(): lax.psum_scatter(grad_keys_all.astype(jnp.bfloat16), 'fsdp', scatter_dime...  125 us
  transfers between devices with their start and end apart: 18, of which 13 were waited for; matrix products, arithmetic and copies ran while one was open for 37% of the time, Pallas kernels for 0%

commit v1 on v0

v1 whole, which is shorter than its diff:
```python
import functools
import math

import jax
import jax.numpy as jnp
from jax import lax
from jax.experimental import pallas as pl
from jax.experimental.pallas import tpu as pltpu
from jax.sharding import Mesh
from jax.sharding import PartitionSpec as P

HEAD_DIM = 128
SEQ_LEN = 4096
EPSILON = 1e-06
ALL = ("x", "core", "z", "y")
GROUP = ("x", "core", "y")
F32 = jnp.float32
BF16 = jnp.bfloat16


def dot_nn(a, b):
    return lax.dot_general(a, b, (((1,), (0,)), ((), ())), preferred_element_type=F32)


def dot_nt(a, b):
    return lax.dot_general(a, b, (((1,), (1,)), ((), ())), preferred_element_type=F32)


def dot_tn(a, b):
    return lax.dot_general(a, b, (((0,), (0,)), ((), ())), preferred_element_type=F32)


def swap(a, axis, step=1):
    return lax.ppermute(a, axis, [(i, i ^ step) for i in range(lax.axis_size(axis))])


def shift(a, axis, step):
    n = lax.axis_size(axis)
    return lax.ppermute(a, axis, [(i, i + step) for i in range(n) if 0 <= i + step < n])


def pick(a, index, axis):
    return lax.dynamic_index_in_dim(a, index, axis, keepdims=False)


def after(value, *others):
    return lax.optimization_barrier((value,) + others)[0]


def gather_level(w):
    depth = lax.axis_size("z")
    return [w] + [swap(w, "z", j) for j in range(1, depth)]


def gather_rest(got):
    rows, cols = got[0].shape
    depth = len(got)
    z, y = lax.axis_index("z"), lax.axis_index("y")
    ordered = []
    for p in range(depth):
        v = got[0]
        for j in range(1, depth):
            v = jnp.where(z == (p ^ j), got[j], v)
        ordered.append(v)
    own = jnp.stack(ordered)
    other = swap(own, "y")
    block = jnp.stack([jnp.where(y == 0, own, other), jnp.where(y == 0, other, own)], axis=1)
    block = block.reshape(depth * 2 * rows, cols)
    near = jnp.stack([block, swap(block, "x")])
    return near, swap(near, "core")


def reduce_rows(acts, grads, dp):
    tokens, width = acts.shape
    cols = grads.shape[1]
    depth = lax.axis_size("z")
    z, y = lax.axis_index("z"), lax.axis_index("y")
    part = width // 4
    rows = part // (depth * 2)
    block = lambda d: lax.dynamic_slice_in_dim(acts, (dp ^ d) * part, part, 1)
    away = jnp.concatenate([block(1), block(3)], axis=1)
    got = swap(dot_tn(away, grads).astype(BF16), "core")
    far = (dot_tn(block(2), grads) + got[part:].astype(F32)).astype(BF16)
    far = swap(far, "x")
    near = dot_tn(block(0), grads) + got[:part].astype(F32)
    near = (near + far.astype(F32)).astype(BF16).reshape(depth, 2, rows, cols)
    far = swap(pick(near, 1 - y, 1), "y")
    near = (pick(near, y, 1).astype(F32) + far.astype(F32)).astype(BF16)
    total = pick(near, z, 0).astype(F32)
    for j in range(1, depth):
        total = total + swap(pick(near, z ^ j, 0), "z", j).astype(F32)
    return total


def project_kernel(place, x_ref, near_ref, far_ref, out_ref):
    part = near_ref.shape[1]
    total = None
    for d in range(4):
        cols = pl.ds(pl.multiple_of((place[0] ^ d) * part, part), part)
        weight = (far_ref if d & 1 else near_ref)[d >> 1]
        term = dot_nn(x_ref[:, cols], weight)
        total = term if total is None else total + term
    out_ref[...] = total.astype(out_ref.dtype)


def project(x, weight, place, kind):
    near, far = weight
    tokens, width = x.shape
    _, part, cols = near.shape
    tile = 512
    return pl.pallas_call(
        project_kernel,
        grid_spec=pltpu.PrefetchScalarGridSpec(
            num_scalar_prefetch=1,
            grid=(cols // tile,),
            in_specs=[
                pl.BlockSpec((tokens, width), lambda i, p: (0, 0)),
                pl.BlockSpec((2, part, tile), lambda i, p: (0, 0, i)),
                pl.BlockSpec((2, part, tile), lambda i, p: (0, 0, i)),
            ],
            out_specs=pl.BlockSpec((tokens, tile), lambda i, p: (0, i)),
        ),
        out_shape=jax.ShapeDtypeStruct((tokens, cols), kind),
        compiler_params=pltpu.CompilerParams(vmem_limit_bytes=50 << 20),
        cost_estimate=pl.CostEstimate(
            flops=2 * tokens * width * cols,
            transcendentals=0,
            bytes_accessed=2 * (tokens * width + width * cols + tokens * cols),
        ),
        name="project",
    )(place, x, near, far)


def project_back_kernel(place, *refs, count):
    grads, weights, out_ref = refs[:count], refs[count : 3 * count], refs[3 * count]

    def step(side):
        total = None
        for i in range(count):
            term = dot_nt(grads[i][...], weights[2 * i + side][0])
            total = term if total is None else total + term
        out_ref[...] = total.astype(out_ref.dtype)

    @pl.when(pl.program_id(0) < 2)
    def _():
        step(0)

    @pl.when(pl.program_id(0) >= 2)
    def _():
        step(1)


def project_back(grads, weights, place, kind):
    tokens, cols = grads[0].shape
    _, part, _ = weights[0][0].shape
    count = len(grads)
    return pl.pallas_call(
        functools.partial(project_back_kernel, count=count),
        grid_spec=pltpu.PrefetchScalarGridSpec(
            num_scalar_prefetch=1,
            grid=(4,),
            in_specs=[pl.BlockSpec((tokens, cols), lambda i, p: (0, 0))] * count
            + [
                pl.BlockSpec((1, part, cols), lambda i, p: (jnp.minimum(i, 1), 0, 0)),
                pl.BlockSpec((1, part, cols), lambda i, p: (jnp.maximum(i - 2, 0), 0, 0)),
            ]
            * count,
            out_specs=pl.BlockSpec((tokens, part), lambda i, p: (0, p[0] ^ ((i % 2) * 2 + i // 2))),
        ),
        out_shape=jax.ShapeDtypeStruct((tokens, 4 * part), kind),
        compiler_params=pltpu.CompilerParams(vmem_limit_bytes=58 << 20),
        cost_estimate=pl.CostEstimate(
            flops=8 * tokens * part * cols * count,
            transcendentals=0,
            bytes_accessed=2 * (tokens * cols + 4 * part * cols) * count + 8 * tokens * part,
        ),
        name="project_back",
    )(place, *grads, *[w for pair in weights for w in pair])


def feed_kernel(x_ref, cot_ref, pair_ref, down_ref, out_ref, grad_ref, act_ref, hid_ref):
    depth, units, part = pair_ref.shape
    units = units // 2
    cot = cot_ref[...]
    gate, up = None, None
    for level in range(depth):
        cols = x_ref[:, level * part : (level + 1) * part]
        first = dot_nt(pair_ref[level, :units, :], cols)
        second = dot_nt(pair_ref[level, units:, :], cols)
        gate = first if gate is None else gate + first
        up = second if up is None else up + second
    grad_act = dot_nt(down_ref[...], cot)
    sig = 1.0 / (1.0 + jnp.exp(-gate))
    silu = gate * sig
    act = (silu * up).astype(BF16)
    act_ref[...] = act
    grad_gate = (grad_act * up * (sig * (1.0 + gate * (1.0 - sig)))).astype(BF16)
    grad_up = (grad_act * silu).astype(BF16)
    hid_ref[:units, :] = grad_gate
    hid_ref[units:, :] = grad_up
    out_ref[...] = dot_tn(act, down_ref[...]).astype(BF16)
    for level in range(depth):
        both = dot_tn(grad_gate, pair_ref[level, :units, :])
        both = both + dot_tn(grad_up, pair_ref[level, units:, :])
        grad_ref[:, level * part : (level + 1) * part] = both.astype(BF16)


def feed(x, cot, pair, down):
    tokens, width = x.shape
    depth, units2, part = pair.shape
    units = units2 // 2
    tile = 256
    row = lambda n: pl.BlockSpec((tile, n), lambda i: (i, 0))
    col = lambda n: pl.BlockSpec((n, tile), lambda i: (0, i))
    return pl.pallas_call(
        feed_kernel,
        grid=(tokens // tile,),
        in_specs=[
            row(width),
            row(width),
            pl.BlockSpec(pair.shape, lambda i: (0, 0, 0)),
            pl.BlockSpec(down.shape, lambda i: (0, 0)),
        ],
        out_specs=[row(width), row(width), col(units), col(units2)],
        out_shape=[
            jax.ShapeDtypeStruct((tokens, width), BF16),
            jax.ShapeDtypeStruct((tokens, width), BF16),
            jax.ShapeDtypeStruct((units, tokens), BF16),
            jax.ShapeDtypeStruct((units2, tokens), BF16),
        ],
        compiler_params=pltpu.CompilerParams(vmem_limit_bytes=50 << 20),
        cost_estimate=pl.CostEstimate(
            flops=12 * tokens * width * units,
            transcendentals=tokens * units,
            bytes_accessed=2 * (4 * tokens * width + 3 * units * width + 3 * units * tokens),
        ),
        name="feed",
    )(x, cot, pair, down)


def feed_weights_kernel(x_ref, cot_ref, act_ref, hid_ref, pair_ref, down_ref):
    pair_ref[0] = dot_nn(hid_ref[...], x_ref[...]).astype(BF16)
    down = dot_nn(act_ref[...], cot_ref[...]).astype(BF16)
    hidden = down_ref.shape[1]
    for level in range(down_ref.shape[0]):
        down_ref[level] = down[level * hidden : (level + 1) * hidden]


def feed_weights(x, cot, act, hid, depth):
    tokens, width = x.shape
    units, units2 = act.shape[0], hid.shape[0]
    part = width // depth
    return pl.pallas_call(
        feed_weights_kernel,
        grid=(depth,),
        in_specs=[
            pl.BlockSpec((tokens, part), lambda i: (0, i)),
            pl.BlockSpec((tokens, part), lambda i: (0, i)),
            pl.BlockSpec(act.shape, lambda i: (0, 0)),
            pl.BlockSpec(hid.shape, lambda i: (0, 0)),
        ],
        out_specs=[
            pl.BlockSpec((1, units2, part), lambda i: (i, 0, 0)),
            pl.BlockSpec((depth, units // depth, part), lambda i: (0, 0, i)),
        ],
        out_shape=[
            jax.ShapeDtypeStruct((depth, units2, part), BF16),
            jax.ShapeDtypeStruct((depth, units // depth, width), BF16),
        ],
        compiler_params=pltpu.CompilerParams(vmem_limit_bytes=50 << 20),
        cost_estimate=pl.CostEstimate(
            flops=6 * tokens * width * units,
            transcendentals=0,
            bytes_accessed=2 * (2 * tokens * width + 3 * units * (tokens + width)),
        ),
        name="feed_weights",
    )(x, cot, act, hid)


def gather_group(a):
    half = a.shape[1] // 2
    first, second = a[:, :half], a[:, half:]
    first2 = jnp.stack([first, swap(first, "x")])
    second2 = jnp.stack([second, swap(second, "y")])
    first4 = jnp.stack([first2, swap(first2, "y")], axis=1)
    second4 = jnp.stack([second2, swap(second2, "x")])
    four = jnp.concatenate([first4, second4], axis=-1)
    return jnp.concatenate([four, swap(four, "core")]).reshape(-1, a.shape[1])


def reduce_group(partial, rows):
    width = partial.shape[1]
    half = width // 2
    parts = partial.reshape(2, 2, 2, rows, width)
    mine = parts[0].astype(F32) + swap(parts[1], "core").astype(F32)
    first, second = mine[..., :half], mine[..., half:]
    first = first[:, 0] + swap(first[:, 1].astype(BF16), "y").astype(F32)
    first = first[0] + swap(first[1].astype(BF16), "x").astype(F32)
    second = second[0] + swap(second[1].astype(BF16), "x").astype(F32)
    second = second[0] + swap(second[1].astype(BF16), "y").astype(F32)
    return jnp.concatenate([first, second], axis=-1)


LOG2E = 1.4426950408889634


def write_bias(query_ref, key_ref, bias_ref):
    query_code = query_ref[:, 0:1]
    query_pos = query_ref[:, 1:2]
    key_code = key_ref[0:1, :]
    key_pos = key_ref[1:2, :]
    key_valid = key_ref[2:3, :]
    allowed = (
        (query_code == key_code)
        & (key_pos <= query_pos)
        & ((key_valid == 1) | (key_pos == query_pos))
    )
    bias_ref[...] = jnp.where(allowed, 0.0, -1e30)


def forward_kernel(query_ref, key_ref, q_ref, k_ref, v_ref, out_ref, low_ref, bias_ref, *, scale):
    @pl.when(pl.program_id(0) == 0)
    def _():
        write_bias(query_ref, key_ref, bias_ref)

    scores = dot_nt(q_ref[...], k_ref[...])
    weights = jnp.exp2(scores * (scale * LOG2E) + bias_ref[...])
    totals = jnp.sum(weights, axis=-1, keepdims=True)
    unnorm = dot_nn(weights.astype(BF16), v_ref[...])
    attended = unnorm / totals
    out_ref[...] = attended
    low_ref[...] = attended.astype(BF16)


def backward_kernel(
    query_ref, key_ref, q_ref, k_ref, v_ref, att_ref, grad_ref, dq_ref, dk_ref, dv_ref, bias_ref, *, scale
):
    @pl.when(pl.program_id(0) == 0)
    def _():
        write_bias(query_ref, key_ref, bias_ref)

    q, k, v = q_ref[...], k_ref[...], v_ref[...]
    grad = grad_ref[...]
    scores = dot_nt(q, k)
    weights = jnp.exp2(scores * (scale * LOG2E) + bias_ref[...])
    totals = jnp.sum(weights, axis=-1, keepdims=True)
    grad_totals = -jnp.sum(grad * att_ref[...], axis=-1, keepdims=True) / totals
    grad_unnorm = (grad / totals).astype(BF16)
    grad_weights = dot_nt(grad_unnorm, v)
    grad_scores = (weights * (grad_weights + grad_totals)).astype(BF16)
    dq_ref[...] = (dot_nn(grad_scores, k) * scale).astype(BF16)
    dk_ref[...] = (dot_tn(grad_scores, q) * scale).astype(BF16)
    dv_ref[...] = dot_tn(weights.astype(BF16), grad_unnorm).astype(BF16)


def attention_specs(rows, keys):
    whole = lambda shape: pl.BlockSpec(shape, lambda h: (0, 0))
    head = lambda n: pl.BlockSpec((n, HEAD_DIM), lambda h: (0, h))
    return whole, head


def attend_forward(query_info, key_info, queries, keys, values):
    rows, width = queries.shape
    count = keys.shape[0]
    whole, head = attention_specs(rows, count)
    return pl.pallas_call(
        functools.partial(forward_kernel, scale=1.0 / math.sqrt(HEAD_DIM)),
        grid=(width // HEAD_DIM,),
        in_specs=[whole(query_info.shape), whole(key_info.shape), head(rows), head(count), head(count)],
        out_specs=[head(rows), head(rows)],
        out_shape=[
            jax.ShapeDtypeStruct((rows, width), F32),
            jax.ShapeDtypeStruct((rows, width), BF16),
        ],
        scratch_shapes=[pltpu.VMEM((rows, count), F32)],
        compiler_params=pltpu.CompilerParams(vmem_limit_bytes=40 << 20),
        cost_estimate=pl.CostEstimate(
            flops=4 * rows * count * width,
            transcendentals=rows * count * width // HEAD_DIM,
            bytes_accessed=2 * (2 * count + 4 * rows) * width,
        ),
        name="attend_forward",
    )(query_info, key_info, queries, keys, values)


def attend_backward(query_info, key_info, queries, keys, values, attended, grads):
    rows, width = queries.shape
    count = keys.shape[0]
    whole, head = attention_specs(rows, count)
    return pl.pallas_call(
        functools.partial(backward_kernel, scale=1.0 / math.sqrt(HEAD_DIM)),
        grid=(width // HEAD_DIM,),
        in_specs=[
            whole(query_info.shape),
            whole(key_info.shape),
            head(rows),
            head(count),
            head(count),
            head(rows),
            head(rows),
        ],
        out_specs=[head(rows), head(count), head(count)],
        out_shape=[
            jax.ShapeDtypeStruct((rows, width), BF16),
            jax.ShapeDtypeStruct((count, width), BF16),
            jax.ShapeDtypeStruct((count, width), BF16),
        ],
        scratch_shapes=[pltpu.VMEM((rows, count), F32)],
        compiler_params=pltpu.CompilerParams(vmem_limit_bytes=48 << 20),
        cost_estimate=pl.CostEstimate(
            flops=10 * rows * count * width,
            transcendentals=rows * count * width // HEAD_DIM,
            bytes_accessed=2 * (4 * count + 6 * rows) * width,
        ),
        name="attend_backward",
    )(query_info, key_info, queries, keys, values, attended, grads)


def shards(
    inputs,
    kv_input,
    segment_ids,
    valid_mask,
    w_query,
    w_key,
    w_value,
    w_out,
    w_gate,
    w_up,
    w_down,
    gain_attn,
    gain_ffn,
    cotangent,
):
    rows, width = inputs.shape
    x, core, z, y = (lax.axis_index(name) for name in ALL)
    depth = lax.axis_size("z")
    devices = 4 * depth * 2
    dp, fsdp = x * 2 + core, z * 2 + y
    group_rows = rows * depth * 2
    seq_length = min(SEQ_LEN, group_rows)
    wide = w_query.shape[0]
    hidden = w_down.shape[0]

    small = jnp.concatenate(
        [gain_attn.astype(F32), gain_ffn.astype(F32), segment_ids.astype(F32), valid_mask.astype(F32)]
    )
    small = lax.all_to_all(
        jnp.broadcast_to(small[None], (devices, small.shape[0])), ALL, 0, 0, tiled=True
    )
    full_gain_attn = small[:, :wide].reshape(-1)
    full_gain_ffn = small[:, wide : 2 * wide].reshape(-1)
    ids_all = lax.dynamic_slice_in_dim(small, dp * depth * 2, depth * 2, 0)[:, 2 * wide :]
    ids_all = ids_all.astype(jnp.int32)

    (kv_first, w_key_, w_down_) = lax.optimization_barrier((kv_input, w_key, w_down, small))[:3]
    place = jnp.reshape(dp, (1,)).astype(jnp.int32)

    reach = min(-(-(seq_length // 2 - 1) // (2 * rows)), depth - 1)
    levels = [kv_first]
    for _ in range(reach):
        levels.append(shift(levels[-1], "z", 1))
    others = [swap(level, "y") for level in levels]
    kv_halo = jnp.concatenate(levels + others)
    block_ids = []
    for other in range(2):
        for level in range(reach + 1):
            block_ids.append(2 * (z - level) + (y ^ other))
    key_pos, key_seg, key_valid = [], [], []
    for block in block_ids:
        here = pick(ids_all, jnp.maximum(block, 0), 0)
        key_seg.append(here[:rows])
        key_valid.append(here[rows:])
        key_pos.append(block * rows + jnp.arange(rows, dtype=jnp.int32))
    key_pos, key_seg, key_valid = (jnp.concatenate(v) for v in (key_pos, key_seg, key_valid))
    query_pos = fsdp * rows + jnp.arange(rows, dtype=jnp.int32)
    code = lambda seg, pos: seg * 4096 + pos // seq_length
    zeros = jnp.zeros_like(key_pos)
    key_info = jnp.stack([code(key_seg, key_pos), key_pos, key_valid] + [zeros] * 5)
    zeros = jnp.zeros_like(query_pos)
    query_info = jnp.stack([code(segment_ids, query_pos), query_pos] + [zeros] * 6, axis=1)

    level_key = gather_level(w_key_)
    level_value = gather_level(after(w_value, *level_key))
    level_query = gather_level(after(w_query, *level_value))
    level_out = gather_level(after(w_out, *level_query))
    full_key = gather_rest(level_key)
    full_value = gather_rest(level_value)
    full_query = gather_rest(level_query)
    full_out = gather_rest(level_out)

    def split_columns(w):
        return w.reshape(wide, 4, depth, 2, hidden).transpose(1, 3, 0, 2, 4)

    pair = jnp.stack([split_columns(w_gate), split_columns(w_up)], axis=2)
    pair = pair.reshape(8, 2 * wide, depth * hidden)
    pair = lax.all_to_all(pair, GROUP, 0, 0, tiled=True)
    pair = pair.reshape(8, 2, wide, depth * hidden).transpose(1, 3, 0, 2)
    pair = pair.reshape(2 * depth * hidden, 8 * wide)
    part_down = lax.all_gather(w_down_, "z", axis=0, tiled=False).reshape(depth * hidden, width)
    pair = lax.all_gather(pair, "z", axis=0, tiled=False)

    def by_level(a):
        return a.reshape(rows, 4, depth, 2 * wide).swapaxes(1, 2).reshape(rows, width)

    def by_dp(a):
        return a.reshape(rows, depth, 4, 2 * wide).swapaxes(1, 2).reshape(rows, width)

    cot_all = gather_group(after(cotangent, *level_out))

    stream = inputs.astype(F32)
    squares_in = jnp.sum(stream * stream, axis=-1, keepdims=True)
    factor_one = lax.rsqrt(squares_in / width + EPSILON)
    unit_one = stream * factor_one
    normed1 = (unit_one * full_gain_attn).astype(BF16)
    keys = project(kv_halo, full_key, place, BF16)
    values = project(kv_halo, full_value, place, BF16)
    queries = project(normed1, full_query, place, BF16)
    attended_f, attended = attend_forward(query_info, key_info, queries, keys, values)
    middle = stream + project(attended, full_out, place, F32)
    squares_mid = jnp.sum(middle * middle, axis=-1, keepdims=True)
    factor_two = lax.rsqrt(squares_mid / width + EPSILON)
    unit_two = middle * factor_two
    normed2 = by_level((unit_two * full_gain_ffn).astype(BF16))
    normed2 = gather_group(normed2)
    out_parts, grad_parts, act, hid = feed(normed2, cot_all, pair, part_down)
    grad_normed2 = by_dp(reduce_group(grad_parts, rows))

    grad_pair, grad_down = feed_weights(normed2, cot_all, act, hid, depth)
    share_down = lax.psum_scatter(grad_down, "z", scatter_dimension=0, tiled=True)
    share_down = share_down.reshape(hidden, width).astype(F32)
    grad_pair = lax.psum_scatter(grad_pair, "z", scatter_dimension=0, tiled=True)
    grad_pair = grad_pair.reshape(2 * depth * hidden, 8 * wide).T
    grad_pair = grad_pair.reshape(8, wide, 2 * depth * hidden)
    grad_pair = lax.all_to_all(grad_pair, GROUP, 0, 0, tiled=True)
    grad_pair = grad_pair.reshape(4, 2, wide, 2, depth, hidden).transpose(3, 2, 0, 4, 1, 5)
    grad_pair = grad_pair.reshape(2, wide, devices * hidden).astype(F32)
    share_gate, share_up = grad_pair[0], grad_pair[1]

    part_gain_ffn = jnp.sum(grad_normed2 * unit_two, axis=0)
    inner = grad_normed2 * full_gain_ffn
    grad_middle = cotangent.astype(F32) + factor_two * (
        inner - unit_two * jnp.mean(inner * unit_two, axis=-1, keepdims=True)
    )
    grad_branch = grad_middle.astype(BF16)
    result = middle + reduce_group(after(out_parts, grad_branch), rows)
    share_out = reduce_rows(attended, grad_branch, dp)
    grad_attended = project_back([grad_branch], [full_out], place, F32)
    grad_queries, grad_keys, grad_values = attend_backward(
        query_info, key_info, queries, keys, values, attended_f, grad_attended
    )
    grad_halo = project_back([grad_keys, grad_values], [full_key, full_value], place, BF16)
    grad_halo = grad_halo.reshape(2, reach + 1, rows, width)
    grad_levels = grad_halo[0].astype(F32) + swap(grad_halo[1], "y").astype(F32)
    back = grad_levels[reach]
    for level in reversed(range(reach)):
        back = grad_levels[level] + shift(back.astype(BF16), "z", -1).astype(F32)
    grad_kv_input = back
    share_key = reduce_rows(kv_halo, grad_keys, dp)
    share_value = reduce_rows(kv_halo, grad_values, dp)
    share_query = reduce_rows(normed1, grad_queries, dp)
    grad_normed1 = project_back([grad_queries], [full_query], place, F32)
    part_gain_attn = jnp.sum(grad_normed1 * unit_one, axis=0)
    inner = grad_normed1 * full_gain_attn
    grad_inputs = grad_middle + factor_one * (
        inner - unit_one * jnp.mean(inner * unit_one, axis=-1, keepdims=True)
    )

    valid = valid_mask.astype(F32)
    squares_out = jnp.sum(result * result, axis=-1)
    sums = jnp.stack(
        [
            jnp.sum(valid * squares_in[:, 0]),
            jnp.sum(valid * squares_mid[:, 0]),
            jnp.sum(valid * squares_out),
            jnp.sum(valid),
        ]
    )
    tiny = jnp.concatenate(
        [
            part_gain_attn.reshape(devices, wide),
            part_gain_ffn.reshape(devices, wide),
            jnp.broadcast_to(sums[None], (devices, 4)),
        ],
        axis=1,
    )
    tiny = jnp.sum(lax.all_to_all(tiny, ALL, 0, 0, tiled=True), axis=0)
    divisor = tiny[2 * wide + 3] * width
    rms_in = jnp.sqrt(tiny[2 * wide] / divisor)
    rms_mid = jnp.sqrt(tiny[2 * wide + 1] / divisor)
    rms_out = jnp.sqrt(tiny[2 * wide + 2] / divisor)
    return (
        result.astype(BF16),
        grad_inputs,
        grad_kv_input,
        share_query,
        share_key,
        share_value,
        share_out,
        share_gate,
        share_up,
        share_down,
        tiny[:wide],
        tiny[wide : 2 * wide],
        rms_in,
        rms_mid,
        rms_out,
    )


def solution(mesh):
    inner = Mesh(
        mesh.devices.reshape(2, mesh.shape["dp"] // 2, mesh.shape["fsdp"] // 2, 2), ALL
    )
    rows, flat = P(ALL, None), P(ALL)
    return jax.shard_map(
        shards,
        mesh=inner,
        in_specs=(rows, rows, flat, flat) + (rows,) * 7 + (flat, flat, rows),
        out_specs=(rows,) * 10 + (flat, flat, P(), P(), P()),
        check_vma=False,
    )
```

time: 5790 us -> 1300 us (0.22)
  waiting for transfers between devices: 3320 us -> 548 us
  blocking collectives: 2030 us -> 0 us
  Pallas kernels: 0 us -> 213 us
  matrix products: 248 us -> 68.3 us
  starting transfers between devices: 4.15 us -> 173 us
  other arithmetic: 17.4 us -> 115 us
    reduce_scatter x6 -> x2, waiting for transfers between devices: 2190 us -> 2.49 us  [the longest x1 2.48 us: shards(): lax.psum_scatter(grad_down, 'z', scatter_dimension=0, tiled=True)]
    unnamed x3 -> x0, blocking collectives: 2000 us -> none
    all_gather x9 -> x2, waiting for transfers between devices: 820 us -> 0.02 us  [the longest x1 0.02 us: shards(): lax.all_gather(w_down_, 'z', axis=0, tiled=False)]
    ppermute x0 -> x76, waiting for transfers between devices: none -> 530 us  [the longest x72 511 us: swap(): lax.ppermute(a, axis, [(i, i ^ step) for i in range(lax.axis_size(axis))])]
    unnamed x20 -> x4, waiting for transfers between devices: 312 us -> 0.07 us
    pallas_call x0 -> x11, Pallas kernels: none -> 213 us  [the longest x3 51.8 us: project_back(): pl.pallas_call(functools.partial(project_back_kernel, count=count), grid_...]
    dot_general x28 -> x12, matrix products: 248 us -> 68.3 us  [dot_tn(): lax.dot_general(a, b, (((0,), (0,)), ((), ())), preferred_element_type=F32)]
    ppermute x0 -> x76, starting transfers between devices: none -> 150 us  [the longest x72 133 us: swap(): lax.ppermute(a, axis, [(i, i ^ step) for i in range(lax.axis_size(axis))])]
  transfers between devices with their start and end apart: 18 -> 84, of which waited for: 13 -> 34; matrix products, arithmetic and copies ran while one was open for 37% -> 24% of each run, Pallas kernels for 0% -> 13%
where the time goes in v1:
time: 1300 us; the launch traced here: 1290 us
  waiting for transfers between devices  548 us (42%)
  Pallas kernels  213 us (16%)
  starting transfers between devices  173 us (13%)
  local copies, waits for them, and re-layouts  148 us (11%)
  other arithmetic  115 us (9%)
  matrix products  68.3 us (5%)
  between operations  21.6 us (2%)
    ppermute x72, waiting for transfers between devices, swap(): lax.ppermute(a, axis, [(i, i ^ step) for i in range(lax.axis_size(axis))])  511 us
    ppermute x72, starting transfers between devices, swap(): lax.ppermute(a, axis, [(i, i ^ step) for i in range(lax.axis_size(axis))])  133 us
    dot_general x12, matrix products, dot_tn(): lax.dot_general(a, b, (((0,), (0,)), ((), ())), preferred_element_type=F32)  68.3 us
    pallas_call x3, Pallas kernels, project_back(): pl.pallas_call(functools.partial(project_back_kernel, count=count), grid_...  51.8 us
    pallas_call x4, Pallas kernels, project(): pl.pallas_call(project_kernel, grid_spec=pltpu.PrefetchScalarGridSpec(num...  49.4 us
    pallas_call x1, Pallas kernels, feed(): pl.pallas_call(feed_kernel, grid=(tokens // tile,), in_specs=[row(width),...  47.2 us
  transfers between devices with their start and end apart: 84, of which 34 were waited for; matrix products, arithmetic and copies ran while one was open for 24% of the time, Pallas kernels for 13%

profile of v1, /device:TPU:0, one launch (start us, length us, event | category | flops | bytes accessed | tf_op | source)
XLA Modules:
  0.0 1286.0 jit_solution(16886816339217121106)
XLA Ops:
  54.3 14.5 %collective-permute-done.1 = bf16[64,2048]{1,0:T(8,128)(2,1)S(1)} collective-permute-done((bf16[64,2048]{1,0:T(8,128)(2,1)S(1)}, bf16[64,2048]{1,0:T(8,128)(2,1)S(1)}, u32[]{:S(2)}, u32[]{:S(2)}) %collective-permute-start.1) | collective-permute-done | bytes 262176 | tf_op jit(solution)/shard_map/ppermute | solution.py:34
  68.8 20.7 %collective-permute-start.3 = (bf16[64,2048]{1,0:T(8,128)(2,1)S(1)}, bf16[64,2048]{1,0:T(8,128)(2,1)S(1)}, u32[]{:S(2)}, u32[]{:S(2)}) collective-permute-start(bf16[64,2048]{1,0:T(8,128)(2,1)S(1)} %copy-done.59), channel_id=1, source_target_pairs={{0,2},{2,0},{4,6},{6,4},{1,3},{3,1},{5,7},{7,5},{8,10},{10,8},{12,... | collective-permute-start | bytes 786440 | tf_op jit(solution)/shard_map/ppermute | solution.py:34
  92.8 16.8 %collective-permute-done.3 = bf16[64,2048]{1,0:T(8,128)(2,1)S(1)} collective-permute-done((bf16[64,2048]{1,0:T(8,128)(2,1)S(1)}, bf16[64,2048]{1,0:T(8,128)(2,1)S(1)}, u32[]{:S(2)}, u32[]{:S(2)}) %collective-permute-start.3) | collective-permute-done | bytes 262176 | tf_op jit(solution)/shard_map/ppermute | solution.py:34
  109.6 13.0 %collective-permute-done.4 = bf16[64,2048]{1,0:T(8,128)(2,1)S(1)} collective-permute-done((bf16[64,2048]{1,0:T(8,128)(2,1)S(1)}, bf16[64,2048]{1,0:T(8,128)(2,1)S(1)}, u32[]{:S(2)}, u32[]{:S(2)}) %collective-permute-start.4) | collective-permute-done | bytes 262176 | tf_op jit(solution)/shard_map/ppermute | solution.py:34
  194.0 19.1 %collective-permute-done.20 = bf16[4,64,2048]{2,1,0:T(8,128)(2,1)S(1)} collective-permute-done((bf16[4,64,2048]{2,1,0:T(8,128)(2,1)S(1)}, bf16[4,64,2048]{2,1,0:T(8,128)(2,1)S(1)}, u32[]{:S(2)}, u32[]{:S(2)}) %collective-permute-start.20) | collective-permute-done | bytes 1048608 | tf_op jit(solution)/shard_map/ppermute | solution.py:34
  214.8 20.8 %collective-permute-done.26 = bf16[4,64,2048]{2,1,0:T(8,128)(2,1)S(1)} collective-permute-done((bf16[4,64,2048]{2,1,0:T(8,128)(2,1)S(1)}, bf16[4,64,2048]{2,1,0:T(8,128)(2,1)S(1)}, u32[]{:S(2)}, u32[]{:S(2)}) %collective-permute-start.26) | collective-permute-done | bytes 1048608 | tf_op jit(solution)/shard_map/ppermute | solution.py:34
  244.1 40.9 %collective-permute-done.18 = bf16[512,2048]{1,0:T(8,128)(2,1)S(1)} collective-permute-done((bf16[512,2048]{1,0:T(8,128)(2,1)S(1)}, bf16[512,2048]{1,0:T(8,128)(2,1)S(1)}, u32[]{:S(2)}, u32[]{:S(2)}) %collective-permute-start.18) | collective-permute-done | bytes 2097184 | tf_op jit(solution)/shard_map/ppermute | solution.py:34
  292.2 49.0 %collective-permute-done.34 = bf16[256,1024]{1,0:T(8,128)(2,1)S(1)} collective-permute-done((bf16[256,1024]{1,0:T(8,128)(2,1)S(1)}, bf16[256,1024]{1,0:T(8,128)(2,1)S(1)}, u32[]{:S(2)}, u32[]{:S(2)}) %collective-permute-start.34) | collective-permute-done | bytes 524320 | tf_op jit(solution)/shard_map/ppermute | solution.py:34
  413.8 18.5 %project.5.k_ref = bf16[1536,2048]{1,0:T(8,128)(2,1)} custom-call(s32[1]{0:T(128)} %bitcast.place, bf16[1536,2048]{1,0:T(8,128)(2,1)} %constant_dynamic-update-slice_fusion.14.x_ref, bf16[2,512,2048]{2,1,0:T(8,128)(2,1)} %pad_maximum_fusion.3.near_ref.refs_2_, bf16[2,512,2048]{2,1,0:T(8,128)(2,1)} %collective-permute-done.19.far_ref.refs_3_), custom_call_target="tpu_custom_call" | custom-call | flops 12884901888 | bytes 20971520 | tf_op jit(solution)/shard_map/project/pallas_call | solution.py:111
  432.3 18.7 %project.6.v_ref = bf16[1536,2048]{1,0:T(8,128)(2,1)} custom-call(s32[1]{0:T(128)} %bitcast.place, bf16[1536,2048]{1,0:T(8,128)(2,1)} %constant_dynamic-update-slice_fusion.14.x_ref, bf16[2,512,2048]{2,1,0:T(8,128)(2,1)} %pad_maximum_fusion.4.near_ref.refs_4_, bf16[2,512,2048]{2,1,0:T(8,128)(2,1)} %collective-permute-done.22.far_ref.refs_5_), custom_call_target="tpu_custom_call" | custom-call | flops 12884901888 | bytes 20971520 | tf_op jit(solution)/shard_map/project/pallas_call | solution.py:111
  451.0 15.4 %attend_forward.1 = (f32[256,2048]{1,0:T(8,128)S(1)}, bf16[256,2048]{1,0:T(8,128)(2,1)S(1)}) custom-call(s32[256,8]{1,0:T(8,128)S(1)} %copy.84.query_ref, s32[8,1536]{1,0:T(8,128)S(1)} %stack.249.key_ref, bf16[256,2048]{1,0:T(8,128)(2,1)S(1)} %project.4.q_ref, bf16[1536,2048]{1,0:T(8,128)(2,1)S(1)} %copy-done.2, bf16[1536,2048]{1,0:T(8,128)(2,1)} %project.6.v_ref), custom_call_target="tpu_custom_call" | custom-call | flops 3221225472 | bytes 16777216 | tf_op jit(solution)/shard_map/attend_forward/pallas_call | solution.py:366
  503.5 16.1 %collective-permute-done.30 = bf16[2,256,1024]{2,1,0:T(8,128)(2,1)S(1)} collective-permute-done((bf16[2,256,1024]{2,1,0:T(8,128)(2,1)S(1)}, bf16[2,256,1024]{2,1,0:T(8,128)(2,1)S(1)}, u32[]{:S(2)}, u32[]{:S(2)}) %collective-permute-start.30) | collective-permute-done | bytes 1048608 | tf_op jit(solution)/shard_map/ppermute | solution.py:34
  539.6 47.2 %feed.1 = (bf16[2048,2048]{1,0:T(8,128)(2,1)}, bf16[2048,2048]{1,0:T(8,128)(2,1)}, bf16[688,2048]{1,0:T(8,128)(2,1)S(1)}, bf16[1376,2048]{1,0:T(8,128)(2,1)}) custom-call(bf16[2048,2048]{1,0:T(8,128)(2,1)} %bitcast.302, bf16[2048,2048]{1,0:T(8,128)(2,1)} %bitcast.300, bf16[4,1376,512]{2,1,0:T(8,128)(2,1)} %all-gather.5.cloned.1.call-done.pair_ref, ...), custom_call_target="tpu_custom_call" | custom-call | flops 34628173824 | bytes 50462720 | tf_op jit(solution)/shard_map/feed/pallas_call | solution.py:215
  602.5 23.1 %feed_weights.1 = (bf16[4,1376,512]{2,1,0:T(8,128)(2,1)}, bf16[4,172,2048]{2,1,0:T(8,128)(2,1)}) custom-call(bf16[2048,2048]{1,0:T(8,128)(2,1)} %bitcast.303, bf16[2048,2048]{1,0:T(8,128)(2,1)} %bitcast.301, bf16[688,2048]{1,0:T(8,128)(2,1)S(1)} %copy-done.6, bf16[1376,2048]{1,0:T(8,128)(2,1)} %get-tuple-element.50.hid_ref), custom_call_target="tpu_custom_call" | custom-call | flops 17314086912 | bytes 33685504 | tf_op jit(solution)/shard_map/feed_weights/pallas_call | solution.py:253
  650.8 18.0 %collective-permute-done.40 = bf16[2,256,1024]{1,2,0:T(8,128)(2,1)} collective-permute-done((bf16[2,256,1024]{1,2,0:T(8,128)(2,1)}, bf16[2,256,1024]{1,2,0:T(8,128)(2,1)}, u32[]{:S(2)}, u32[]{:S(2)}) %collective-permute-start.40) | collective-permute-done | bytes 1048608 | tf_op jit(solution)/shard_map/ppermute | solution.py:34
  719.6 25.7 %attend_backward.1 = (bf16[256,2048]{1,0:T(8,128)(2,1)S(1)}, bf16[1536,2048]{1,0:T(8,128)(2,1)}, bf16[1536,2048]{1,0:T(8,128)(2,1)}) custom-call(s32[256,8]{1,0:T(8,128)S(1)} %copy.84.query_ref, s32[8,1536]{1,0:T(8,128)S(1)} %stack.249.key_ref, bf16[256,2048]{1,0:T(8,128)(2,1)S(1)} %project.4.q_ref, bf16[1536,2048]{1,0:T(8,128)(2,1)} %project.5.k_ref, ...), custom_call_target="tpu_custom_call" | custom-call | flops 8053063680 | bytes 31457280 | tf_op jit(solution)/shard_map/attend_backward/pallas_call | solution.py:390
  746.2 36.2 %project_back.5 = bf16[1536,2048]{1,0:T(8,128)(2,1)} custom-call(s32[1]{0:T(128)} %bitcast.place, bf16[1536,2048]{1,0:T(8,128)(2,1)} %get-tuple-element.47.refs_0_, bf16[1536,2048]{1,0:T(8,128)(2,1)} %get-tuple-element.48.refs_1_, bf16[2,512,2048]{2,1,0:T(8,128)(2,1)} %pad_maximum_fusion.3.near_ref.refs_2_, ...), custom_call_target="tpu_custom_call" | custom-call | flops 25769803776 | bytes 35651584 | tf_op jit(solution)/shard_map/project_back/pallas_call | solution.py:157
  834.1 25.8 %collective-permute-done.49 = bf16[3,256,2048]{2,1,0:T(8,128)(2,1)} collective-permute-done((bf16[3,256,2048]{2,1,0:T(8,128)(2,1)}, bf16[3,256,2048]{2,1,0:T(8,128)(2,1)}, u32[]{:S(2)}, u32[]{:S(2)}) %collective-permute-start.49) | collective-permute-done | bytes 3145760 | tf_op jit(solution)/shard_map/ppermute | solution.py:34
  911.0 136.3 %collective-permute-done.46 = bf16[256,1024]{1,0:T(8,128)(2,1)S(1)} collective-permute-done((bf16[256,1024]{1,0:T(8,128)(2,1)S(1)}, bf16[256,1024]{1,0:T(8,128)(2,1)S(1)}, u32[]{:S(2)}, u32[]{:S(2)}) %collective-permute-start.46) | collective-permute-done | bytes 524320 | tf_op jit(solution)/shard_map/ppermute | solution.py:34
  1081.0 14.7 %all-to-all-done.3 = f32[32,1,132]{2,1,0:T(1,128)S(1)} async-done(((f32[32,1,132]{2,1,0:T(1,128)}), f32[32,1,132]{2,1,0:T(1,128)S(1)}, u32[]{:S(2)}, u32[]{:S(2)}) %all-to-all-start.3) | async-done | bytes 16928 | tf_op jit(solution)/shard_map/all_to_all | solution.py:587
  1169.8 16.8 %collective-permute-done.60 = bf16[4,64,2048]{2,1,0:T(8,128)(2,1)} collective-permute-done((bf16[4,64,2048]{2,1,0:T(8,128)(2,1)S(1)}, bf16[4,64,2048]{2,1,0:T(8,128)(2,1)}, u32[]{:S(2)}, u32[]{:S(2)}) %collective-permute-start.60) | collective-permute-done | bytes 1048608 | tf_op jit(solution)/shard_map/ppermute | solution.py:34
  1190.3 18.3 %collective-permute-done.54 = bf16[4,64,2048]{2,1,0:T(8,128)(2,1)} collective-permute-done((bf16[4,64,2048]{2,1,0:T(8,128)(2,1)}, bf16[4,64,2048]{2,1,0:T(8,128)(2,1)}, u32[]{:S(2)}, u32[]{:S(2)}) %collective-permute-start.54) | collective-permute-done | bytes 1048608 | tf_op jit(solution)/shard_map/ppermute | solution.py:34
  1231.2 15.2 %collective-permute-start.56 = (bf16[64,2048]{1,0:T(8,128)(2,1)S(1)}, bf16[64,2048]{1,0:T(8,128)(2,1)S(1)}, u32[]{:S(2)}, u32[]{:S(2)}) collective-permute-start(bf16[64,2048]{1,0:T(8,128)(2,1)S(1)} %get-tuple-element.101), channel_id=1, source_target_pairs={{0,4},{2,6},{4,0},{6,2},{1,5},{3,7},{5,1},{7,3},{8,12},{10,14},{12... | collective-permute-start | bytes 786440 | tf_op jit(solution)/shard_map/ppermute | solution.py:34
  1250.7 13.0 %collective-permute-done.62 = bf16[64,2048]{1,0:T(8,128)(2,1)S(1)} collective-permute-done((bf16[64,2048]{1,0:T(8,128)(2,1)S(1)}, bf16[64,2048]{1,0:T(8,128)(2,1)S(1)}, u32[]{:S(2)}, u32[]{:S(2)}) %collective-permute-start.62) | collective-permute-done | bytes 262176 | tf_op jit(solution)/shard_map/ppermute | solution.py:34
  (518 shorter events, 610.6 us)
Async XLA Ops:
  36.2 324.3 %all-to-all-start.1 = ((bf16[8,128,688]{1,2,0:T(8,128)(2,1)}), bf16[8,128,688]{1,2,0:T(8,128)(2,1)}, u32[]{:S(2)}, u32[]{:S(2)}) async-start(bf16[8,128,688]{1,2,0:T(8,128)(2,1)} %copy.92), calls=%async_computation.1 | async-start | bytes 2818048 | tf_op jit(solution)/shard_map/all_to_all | solution.py:497
  40.5 481.8 %all-gather.7.cloned.1.call-start = ((), (), s32[]{:S(2)}) async-start(), calls=%async_computation.9 | async-start | bytes 3604480 | tf_op jit(solution)/shard_map/all_gather | solution.py:500
  45.1 494.5 %all-gather.5.cloned.1.call-start = ((), (), s32[]{:S(2)}) async-start(), calls=%async_computation.6 | async-start | bytes 7045120 | tf_op jit(solution)/shard_map/all_gather | solution.py:501
  171.0 116.4 %collective-permute-start.12 = (bf16[256,2048]{1,0:T(8,128)(2,1)S(1)}, bf16[256,2048]{1,0:T(8,128)(2,1)}, u32[]{:S(2)}, u32[]{:S(2)}) collective-permute-start(bf16[256,2048]{1,0:T(8,128)(2,1)S(1)} %copy-done.50), channel_id=1, source_target_pairs={{0,2},{2,4},{4,6},{1,3},{3,5},{5,7},{8,10},{10,12},{12,14},{9,11},... | collective-permute-start | bytes 3145736 | tf_op jit(solution)/shard_map/ppermute | solution.py:39
  193.5 91.5 %collective-permute-start.18 = (bf16[512,2048]{1,0:T(8,128)(2,1)S(1)}, bf16[512,2048]{1,0:T(8,128)(2,1)S(1)}, u32[]{:S(2)}, u32[]{:S(2)}) collective-permute-start(bf16[512,2048]{1,0:T(8,128)(2,1)S(1)} %bitcast.307), channel_id=1, source_target_pairs={{0,16},{16,0},{1,17},{17,1},{2,18},{18,2},{3,19},{19,3},{4,20},{20... | collective-permute-start | bytes 6291464 | tf_op jit(solution)/shard_map/ppermute | solution.py:34
  236.4 107.9 %collective-permute-start.21 = (bf16[512,2048]{1,0:T(8,128)(2,1)S(1)}, bf16[512,2048]{1,0:T(8,128)(2,1)}, u32[]{:S(2)}, u32[]{:S(2)}) collective-permute-start(bf16[512,2048]{1,0:T(8,128)(2,1)S(1)} %bitcast.309), channel_id=1, source_target_pairs={{0,16},{16,0},{1,17},{17,1},{2,18},{18,2},{3,19},{19,3},{4,20},{20... | collective-permute-start | bytes 6291464 | tf_op jit(solution)/shard_map/ppermute | solution.py:34
  240.1 101.1 %collective-permute-start.34 = (bf16[256,1024]{1,0:T(8,128)(2,1)S(1)}, bf16[256,1024]{1,0:T(8,128)(2,1)S(1)}, u32[]{:S(2)}, u32[]{:S(2)}) collective-permute-start(bf16[256,1024]{1,0:T(8,128)(2,1)S(1)} %get-tuple-element.109), channel_id=1, source_target_pairs={{0,16},{16,0},{1,17},{17,1},{2,18},{18,2},{3,19},{19,3},{4,20},{20... | collective-permute-start | bytes 1572872 | tf_op jit(solution)/shard_map/ppermute | solution.py:34
  285.0 121.4 %collective-permute-start.11 = (bf16[2,512,2048]{2,1,0:T(8,128)(2,1)}, bf16[2,512,2048]{2,1,0:T(8,128)(2,1)}, u32[]{:S(2)}, u32[]{:S(2)}) collective-permute-start(bf16[2,512,2048]{2,1,0:T(8,128)(2,1)} %pad_maximum_fusion.2.near_ref.refs_1_), channel_id=1, source_target_pairs={{0,8},{8,0},{1,9},{9,1},{2,10},{10,2},{3,11},{11,3},{4,12},{12,4},... | collective-permute-start | bytes 12582920 | tf_op jit(solution)/shard_map/ppermute | solution.py:34
  287.4 126.4 %collective-permute-start.19 = (bf16[2,512,2048]{2,1,0:T(8,128)(2,1)}, bf16[2,512,2048]{2,1,0:T(8,128)(2,1)}, u32[]{:S(2)}, u32[]{:S(2)}) collective-permute-start(bf16[2,512,2048]{2,1,0:T(8,128)(2,1)} %pad_maximum_fusion.3.near_ref.refs_2_), channel_id=1, source_target_pairs={{0,8},{8,0},{1,9},{9,1},{2,10},{10,2},{3,11},{11,3},{4,12},{12,4},... | collective-permute-start | bytes 12582920 | tf_op jit(solution)/shard_map/ppermute | solution.py:34
  290.5 89.8 %collective-permute-start.27 = (bf16[512,2048]{1,0:T(8,128)(2,1)}, bf16[512,2048]{1,0:T(8,128)(2,1)}, u32[]{:S(2)}, u32[]{:S(2)}) collective-permute-start(bf16[512,2048]{1,0:T(8,128)(2,1)} %bitcast.48), channel_id=1, source_target_pairs={{0,16},{16,0},{1,17},{17,1},{2,18},{18,2},{3,19},{19,3},{4,20},{20... | collective-permute-start | bytes 6291464 | tf_op jit(solution)/shard_map/ppermute | solution.py:34
  353.8 78.5 %collective-permute-start.22 = (bf16[2,512,2048]{2,1,0:T(8,128)(2,1)}, bf16[2,512,2048]{2,1,0:T(8,128)(2,1)}, u32[]{:S(2)}, u32[]{:S(2)}) collective-permute-start(bf16[2,512,2048]{2,1,0:T(8,128)(2,1)} %pad_maximum_fusion.4.near_ref.refs_4_), channel_id=1, source_target_pairs={{0,8},{8,0},{1,9},{9,1},{2,10},{10,2},{3,11},{11,3},{4,12},{12,4},... | collective-permute-start | bytes 12582920 | tf_op jit(solution)/shard_map/ppermute | solution.py:34
  369.8 309.6 %reduce-scatter.5.cloned.1.call-start = ((), (), s32[]{:S(2)}) async-start(), calls=%async_computation.8 | async-start | bytes 3604480 | tf_op jit(solution)/shard_map/reduce_scatter | solution.py:530
  385.6 80.8 %collective-permute-start.28 = (bf16[2,512,2048]{2,1,0:T(8,128)(2,1)}, bf16[2,512,2048]{2,1,0:T(8,128)(2,1)}, u32[]{:S(2)}, u32[]{:S(2)}) collective-permute-start(bf16[2,512,2048]{2,1,0:T(8,128)(2,1)} %pad_maximum_fusion.5.near_ref.refs_1_), channel_id=1, source_target_pairs={{0,8},{8,0},{1,9},{9,1},{2,10},{10,2},{3,11},{11,3},{4,12},{12,4},... | collective-permute-start | bytes 12582920 | tf_op jit(solution)/shard_map/ppermute | solution.py:34
  403.6 96.4 %collective-permute-start.35 = (bf16[2,256,1024]{2,1,0:T(8,128)(2,1)}, bf16[2,256,1024]{2,1,0:T(8,128)(2,1)}, u32[]{:S(2)}, u32[]{:S(2)}) collective-permute-start(bf16[2,256,1024]{2,1,0:T(8,128)(2,1)} %get-tuple-element.105), channel_id=1, source_target_pairs={{0,1},{1,0},{2,3},{3,2},{4,5},{5,4},{6,7},{7,6},{8,9},{9,8},{10,11... | collective-permute-start | bytes 3145736 | tf_op jit(solution)/shard_map/ppermute | solution.py:34
  406.4 93.6 %collective-permute-start.37 = (bf16[2,256,1024]{2,1,0:T(8,128)(2,1)}, bf16[2,256,1024]{2,1,0:T(8,128)(2,1)}, u32[]{:S(2)}, u32[]{:S(2)}) collective-permute-start(bf16[2,256,1024]{2,1,0:T(8,128)(2,1)} %get-tuple-element.111), channel_id=1, source_target_pairs={{0,16},{16,0},{1,17},{17,1},{2,18},{18,2},{3,19},{19,3},{4,20},{20... | collective-permute-start | bytes 3145736 | tf_op jit(solution)/shard_map/ppermute | solution.py:34
  625.6 452.8 %reduce-scatter.3.cloned.1.call-start = ((), (), s32[]{:S(2)}) async-start(), calls=%async_computation.7 | async-start | bytes 7045120 | tf_op jit(solution)/shard_map/reduce_scatter | solution.py:532
  711.9 152.5 %collective-permute-start.44 = (bf16[2,2,256,2048]{3,2,0,1:T(8,128)(2,1)}, bf16[2,2,256,2048]{3,2,0,1:T(8,128)(2,1)}, u32[]{:S(2)}, u32[]{:S(2)}) collective-permute-start(bf16[2,2,256,2048]{3,2,0,1:T(8,128)(2,1)} %copy.100), channel_id=1, source_target_pairs={{0,8},{8,0},{1,9},{9,1},{2,10},{10,2},{3,11},{11,3},{4,12},{12,4},... | collective-permute-start | bytes 12582920 | tf_op jit(solution)/shard_map/ppermute | solution.py:34
  892.1 212.0 %collective-permute-start.71 = (bf16[512,2048]{1,0:T(8,128)(2,1)}, bf16[512,2048]{1,0:T(8,128)(2,1)}, u32[]{:S(2)}, u32[]{:S(2)}) collective-permute-start(bf16[512,2048]{1,0:T(8,128)(2,1)} %add_convert_fusion.1), channel_id=1, source_target_pairs={{0,16},{16,0},{1,17},{17,1},{2,18},{18,2},{3,19},{19,3},{4,20},{20... | collective-permute-start | bytes 6291464 | tf_op jit(solution)/shard_map/ppermute | solution.py:34
  895.4 216.5 %collective-permute-start.65 = (bf16[512,2048]{1,0:T(8,128)(2,1)}, bf16[512,2048]{1,0:T(8,128)(2,1)}, u32[]{:S(2)}, u32[]{:S(2)}) collective-permute-start(bf16[512,2048]{1,0:T(8,128)(2,1)} %add_convert_fusion.3), channel_id=1, source_target_pairs={{0,16},{16,0},{1,17},{17,1},{2,18},{18,2},{3,19},{19,3},{4,20},{20... | collective-permute-start | bytes 6291464 | tf_op jit(solution)/shard_map/ppermute | solution.py:34
  903.1 217.1 %collective-permute-start.59 = (bf16[512,2048]{1,0:T(8,128)(2,1)}, bf16[512,2048]{1,0:T(8,128)(2,1)}, u32[]{:S(2)}, u32[]{:S(2)}) collective-permute-start(bf16[512,2048]{1,0:T(8,128)(2,1)} %add_convert_fusion.5), channel_id=1, source_target_pairs={{0,16},{16,0},{1,17},{17,1},{2,18},{18,2},{3,19},{19,3},{4,20},{20... | collective-permute-start | bytes 6291464 | tf_op jit(solution)/shard_map/ppermute | solution.py:34
  905.0 142.3 %collective-permute-start.46 = (bf16[256,1024]{1,0:T(8,128)(2,1)S(1)}, bf16[256,1024]{1,0:T(8,128)(2,1)S(1)}, u32[]{:S(2)}, u32[]{:S(2)}) collective-permute-start(bf16[256,1024]{1,0:T(8,128)(2,1)S(1)} %fusion.34), channel_id=1, source_target_pairs={{0,16},{16,0},{1,17},{17,1},{2,18},{18,2},{3,19},{19,3},{4,20},{20... | collective-permute-start | bytes 1572872 | tf_op jit(solution)/shard_map/ppermute | solution.py:34
  906.4 141.9 %collective-permute-start.48 = (bf16[256,1024]{1,0:T(8,128)(2,1)S(1)}, bf16[256,1024]{1,0:T(8,128)(2,1)S(1)}, u32[]{:S(2)}, u32[]{:S(2)}) collective-permute-start(bf16[256,1024]{1,0:T(8,128)(2,1)S(1)} %fusion.35), channel_id=1, source_target_pairs={{0,1},{1,0},{2,3},{3,2},{4,5},{5,4},{6,7},{7,6},{8,9},{9,8},{10,11... | collective-permute-start | bytes 1572872 | tf_op jit(solution)/shard_map/ppermute | solution.py:34
  1047.3 80.3 %collective-permute-start.53 = (bf16[512,2048]{1,0:T(8,128)(2,1)}, bf16[512,2048]{1,0:T(8,128)(2,1)}, u32[]{:S(2)}, u32[]{:S(2)}) collective-permute-start(bf16[512,2048]{1,0:T(8,128)(2,1)} %add_convert_fusion.7), channel_id=1, source_target_pairs={{0,16},{16,0},{1,17},{17,1},{2,18},{18,2},{3,19},{19,3},{4,20},{20... | collective-permute-start | bytes 6291464 | tf_op jit(solution)/shard_map/ppermute | solution.py:34
  1132.0 76.6 %collective-permute-start.54 = (bf16[4,64,2048]{2,1,0:T(8,128)(2,1)}, bf16[4,64,2048]{2,1,0:T(8,128)(2,1)}, u32[]{:S(2)}, u32[]{:S(2)}) collective-permute-start(bf16[4,64,2048]{2,1,0:T(8,128)(2,1)} %dynamic-slice_bitcast_fusion.3), channel_id=1, source_target_pairs={{0,1},{1,0},{2,3},{3,2},{4,5},{5,4},{6,7},{7,6},{8,9},{9,8},{10,11... | collective-permute-start | bytes 3145736 | tf_op jit(solution)/shard_map/ppermute | solution.py:34
  (138 other events, 3721.6 us)
Sparse Core Ops, SparseCore 0:
  45.2 106.3 all-gather.6
  369.9 106.0 all-gather.4
  625.7 53.6 reduce-scatter.4
  681.5 99.9 reduce-scatter.2

commit v2 on v1

v2 whole, which is shorter than its diff:
```python
import functools
import math

import jax
import jax.numpy as jnp
from jax import lax
from jax.experimental import pallas as pl
from jax.experimental.pallas import tpu as pltpu
from jax.sharding import Mesh
from jax.sharding import PartitionSpec as P

HEAD_DIM = 128
SEQ_LEN = 4096
EPSILON = 1e-06
ALL = ("x", "core", "z", "y")
GROUP = ("x", "core", "y")
F32 = jnp.float32
BF16 = jnp.bfloat16


def dot_nn(a, b):
    return lax.dot_general(a, b, (((1,), (0,)), ((), ())), preferred_element_type=F32)


def dot_nt(a, b):
    return lax.dot_general(a, b, (((1,), (1,)), ((), ())), preferred_element_type=F32)


def dot_tn(a, b):
    return lax.dot_general(a, b, (((0,), (0,)), ((), ())), preferred_element_type=F32)


def swap(a, axis, step=1):
    return lax.ppermute(a, axis, [(i, i ^ step) for i in range(lax.axis_size(axis))])


def shift(a, axis, step):
    n = lax.axis_size(axis)
    return lax.ppermute(a, axis, [(i, i + step) for i in range(n) if 0 <= i + step < n])


def pick(a, index, axis):
    return lax.dynamic_index_in_dim(a, index, axis, keepdims=False)


def after(value, *others):
    return lax.optimization_barrier((value,) + others)[0]


def together(*values):
    return lax.optimization_barrier(values)


def copy_kernel(x_ref, out_ref):
    out_ref[...] = x_ref[...]


def settle(x):
    rows, cols = x.shape
    tile = 512 if cols % 512 == 0 else cols
    spec = pl.BlockSpec((rows, tile), lambda i: (0, i))
    return pl.pallas_call(
        copy_kernel,
        grid=(cols // tile,),
        in_specs=[spec],
        out_specs=spec,
        out_shape=jax.ShapeDtypeStruct(x.shape, x.dtype),
        name="settle",
    )(x)


def take_block(a, d, dp):
    part = a.shape[1] // 4
    return lax.dynamic_slice_in_dim(a, (dp ^ d) * part, part, 1)


def columns(acts, first, second, dp):
    return jnp.concatenate([take_block(acts, first, dp), take_block(acts, second, dp)], axis=1).T


def weight_grad_kernel(*refs, parts):
    outs = refs[len(refs) - parts :]
    total = dot_nn(refs[0][...], refs[1][...])
    if len(refs) - parts == 3:
        total = total + refs[2][...].astype(F32)
    rows = outs[0].shape[0]
    for i, out in enumerate(outs):
        out[...] = total[i * rows : (i + 1) * rows].astype(BF16)


def weight_grad(acts, grads, got=None, parts=1):
    rows, tokens = acts.shape
    cols = grads.shape[1]
    tile = 512
    col = lambda n: pl.BlockSpec((n, tile), lambda i: (0, i))
    args = (acts, grads) if got is None else (acts, grads, got)
    out = pl.pallas_call(
        functools.partial(weight_grad_kernel, parts=parts),
        grid=(cols // tile,),
        in_specs=[pl.BlockSpec(acts.shape, lambda i: (0, 0)), col(tokens), col(rows)][: len(args)],
        out_specs=[col(rows // parts)] * parts,
        out_shape=[jax.ShapeDtypeStruct((rows // parts, cols), BF16)] * parts,
        compiler_params=pltpu.CompilerParams(vmem_limit_bytes=40 << 20),
        cost_estimate=pl.CostEstimate(
            flops=2 * rows * tokens * cols,
            transcendentals=0,
            bytes_accessed=2 * (rows * tokens + tokens * cols + 2 * rows * cols),
        ),
        name="weight_grad",
    )(*args)
    return out if parts > 1 else out[0]


def by_owner(near):
    depth = lax.axis_size("z")
    return near.reshape(depth, 2, -1, near.shape[1])


def add(a, b):
    return (a.astype(F32) + b.astype(F32)).astype(BF16)


def split_y(a):
    y = lax.axis_index("y")
    return pick(a, 1 - y, a.ndim - 3), pick(a, y, a.ndim - 3)


def collect(a):
    out = lax.psum_scatter(a, "z", scatter_dimension=0, tiled=True)
    return out.reshape(out.shape[1:]).astype(F32)


def project_kernel(*refs):
    weight_ref, out_ref = refs[-2:]
    at = 0
    for x_ref in refs[:-2]:
        rows = x_ref.shape[0]
        out_ref[at : at + rows, :] = dot_nn(x_ref[...], weight_ref[...]).astype(out_ref.dtype)
        at += rows


def project(pieces, weights, first, count, kind):
    rows, width = pieces[0].shape
    tokens, cols = rows * len(pieces), count * width
    tile = 512
    return pl.pallas_call(
        project_kernel,
        grid=(cols // tile,),
        in_specs=[pl.BlockSpec((rows, width), lambda i: (0, 0))] * len(pieces)
        + [pl.BlockSpec((width, tile), lambda i: (0, first * (width // tile) + i))],
        out_specs=pl.BlockSpec((tokens, tile), lambda i: (0, i)),
        out_shape=jax.ShapeDtypeStruct((tokens, cols), kind),
        compiler_params=pltpu.CompilerParams(vmem_limit_bytes=50 << 20),
        cost_estimate=pl.CostEstimate(
            flops=2 * tokens * width * cols,
            transcendentals=0,
            bytes_accessed=2 * (tokens * width + width * cols + tokens * cols),
        ),
        name="project",
    )(*pieces, weights)


def project_back_kernel(*refs, count):
    total = None
    for i in range(count):
        term = dot_nt(refs[i][...], refs[count + i][...])
        total = term if total is None else total + term
    refs[-1][...] = total.astype(refs[-1].dtype)


def project_back(grads, weights, numbers, kind):
    tokens, width = grads[0].shape
    tile = 512
    count = len(grads)
    weight = lambda number: pl.BlockSpec((tile, width), lambda i: (i, number))
    return pl.pallas_call(
        functools.partial(project_back_kernel, count=count),
        grid=(width // tile,),
        in_specs=[pl.BlockSpec((tokens, width), lambda i: (0, 0))] * count
        + [weight(number) for number in numbers],
        out_specs=pl.BlockSpec((tokens, tile), lambda i: (0, i)),
        out_shape=jax.ShapeDtypeStruct((tokens, width), kind),
        compiler_params=pltpu.CompilerParams(vmem_limit_bytes=58 << 20),
        cost_estimate=pl.CostEstimate(
            flops=2 * tokens * width * width * count,
            transcendentals=0,
            bytes_accessed=2 * (tokens + width) * width * count + 4 * tokens * width,
        ),
        name="project_back",
    )(*grads, *[weights] * count)


def level_spans(width, depth, natural):
    part = width // depth
    if not natural:
        return [[(level * part, part)] for level in range(depth)]
    piece = part // 4
    return [[((p * depth + level) * piece, piece) for p in range(4)] for level in range(depth)]


def feed_kernel(x_ref, cot_ref, pair_ref, down_ref, *refs, spans, summed):
    units = down_ref.shape[0]
    gate, up = None, None
    for level, pieces in enumerate(spans):
        cols = [x_ref[:, start : start + size] for start, size in pieces]
        cols = cols[0] if len(cols) == 1 else jnp.concatenate(cols, axis=1)
        first = dot_nt(pair_ref[level, :units, :], cols)
        second = dot_nt(pair_ref[level, units : 2 * units, :], cols)
        gate = first if gate is None else gate + first
        up = second if up is None else up + second
    grad_act = dot_nt(down_ref[...], cot_ref[...])
    sig = 1.0 / (1.0 + jnp.exp(-gate))
    silu = gate * sig
    act = (silu * up).astype(BF16)
    grad_gate = (grad_act * up * (sig * (1.0 + gate * (1.0 - sig)))).astype(BF16)
    grad_up = (grad_act * silu).astype(BF16)
    act_ref, hid_ref = refs[-2:] if not summed else refs[2:4]
    act_ref[...] = act
    hid_ref[:units, :] = grad_gate
    hid_ref[units:, :] = grad_up
    if summed:
        grad_got, grad_ref = refs[0], refs[8]
    else:
        grad_ref = refs[1]
    out_ref = refs[1 if summed else 0]
    out_ref[...] = dot_tn(act, down_ref[...]).astype(BF16)
    for level, pieces in enumerate(spans):
        both = dot_tn(grad_gate, pair_ref[level, :units, :])
        both = both + dot_tn(grad_up, pair_ref[level, units : 2 * units, :])
        at = 0
        for start, size in pieces:
            term = both[:, at : at + size]
            if summed:
                term = term + grad_got[:, start : start + size].astype(F32)
            grad_ref[:, start : start + size] = term.astype(grad_ref.dtype)
            at += size
    if summed:
        step = pl.program_id(0)
        half = grad_ref.shape[1] // 2
        for number, (mine, cols) in enumerate(
            (
                (step % 2 == 0, slice(0, half)),
                (step % 2 == 1, slice(0, half)),
                (step < 2, slice(half, 2 * half)),
                (step >= 2, slice(half, 2 * half)),
            )
        ):

            @pl.when(mine)
            def _(piece=refs[4 + number], cols=cols):
                piece[0] = grad_ref[:, cols].astype(BF16)


def feed(x, cot, pair, down, natural, got=None):
    tokens, width = x.shape
    depth, units = pair.shape[0], down.shape[0]
    units2 = 2 * units
    tile = tokens // 4
    half = width // 2
    summed = got is not None
    row = lambda n: pl.BlockSpec((tile, n), lambda i: (i, 0))
    col = lambda n: pl.BlockSpec((n, tile), lambda i: (0, i))
    piece = lambda at: pl.BlockSpec((1, tile, half), lambda i: (at(i), 0, 0))
    pieces = [
        piece(lambda i: i // 2),
        piece(lambda i: i // 2),
        piece(lambda i: jnp.minimum(i, 1)),
        piece(lambda i: jnp.maximum(i - 2, 0)),
    ]
    big = [jax.ShapeDtypeStruct((tokens, width), BF16)] * 2
    sums = [jax.ShapeDtypeStruct((2, tile, half), BF16)] * 4
    acts = [
        jax.ShapeDtypeStruct((units, tokens), BF16),
        jax.ShapeDtypeStruct((units2, tokens), BF16),
    ]
    acts_specs = [col(units), col(units2)]
    return pl.pallas_call(
        functools.partial(
            feed_kernel, spans=level_spans(width, depth, natural), summed=summed
        ),
        grid=(4,),
        in_specs=[
            row(width),
            row(width),
            pl.BlockSpec(pair.shape, lambda i: (0, 0, 0)),
            pl.BlockSpec(down.shape, lambda i: (0, 0)),
        ]
        + ([row(width)] if summed else []),
        out_specs=[row(width)] + (acts_specs + pieces if summed else [row(width)] + acts_specs),
        out_shape=big[:1] + acts + sums if summed else big + acts,
        scratch_shapes=[pltpu.VMEM((tile, width), F32)] if summed else [],
        compiler_params=pltpu.CompilerParams(vmem_limit_bytes=56 << 20),
        cost_estimate=pl.CostEstimate(
            flops=12 * tokens * width * units,
            transcendentals=tokens * units,
            bytes_accessed=2 * (4 * tokens * width + 3 * units * width + 3 * units * tokens),
        ),
        name="feed_sum" if summed else "feed",
    )(x, cot, pair, down, *((got,) if summed else ()))


def feed_weights_kernel(*refs, count):
    pair_ref, down_ref = refs[4 * count :]
    pair, down = None, None
    for i in range(count):
        x_ref, cot_ref, act_ref, hid_ref = refs[4 * i : 4 * i + 4]
        first = dot_nn(hid_ref[...], x_ref[...])
        second = dot_nn(act_ref[...], cot_ref[...])
        pair = first if pair is None else pair + first
        down = second if down is None else down + second
    pair, down = pair.astype(BF16), down.astype(BF16)
    for level in range(pair_ref.shape[0]):
        size = pair_ref.shape[2]
        pair_ref[level] = pair[:, level * size : (level + 1) * size]
    for level in range(down_ref.shape[0]):
        size = down_ref.shape[1]
        down_ref[level] = down[level * size : (level + 1) * size]


def feed_weights(sets, depth, natural):
    x, _, act, hid = sets[0]
    tokens, width = x.shape
    units, units2 = act.shape[0], hid.shape[0]
    steps = 4 if natural else depth
    part = width // steps
    if natural:
        pair_spec = pl.BlockSpec((depth, units2, part // depth), lambda i: (0, 0, i))
    else:
        pair_spec = pl.BlockSpec((1, units2, part), lambda i: (i, 0, 0))
    return pl.pallas_call(
        functools.partial(feed_weights_kernel, count=len(sets)),
        grid=(steps,),
        in_specs=[
            pl.BlockSpec((tokens, part), lambda i: (0, i)),
            pl.BlockSpec((tokens, part), lambda i: (0, i)),
            pl.BlockSpec(act.shape, lambda i: (0, 0)),
            pl.BlockSpec(hid.shape, lambda i: (0, 0)),
        ]
        * len(sets),
        out_specs=[
            pair_spec,
            pl.BlockSpec((depth, units // depth, part), lambda i: (0, 0, i)),
        ],
        out_shape=[
            pltpu.HBM((depth, units2, width // depth), BF16),
            pltpu.HBM((depth, units // depth, width), BF16),
        ],
        compiler_params=pltpu.CompilerParams(vmem_limit_bytes=50 << 20),
        cost_estimate=pl.CostEstimate(
            flops=6 * tokens * width * units * len(sets),
            transcendentals=0,
            bytes_accessed=2 * (2 * tokens * width + 3 * units * tokens) * len(sets)
            + 6 * units * width,
        ),
        name="feed_weights",
    )(*[v for group in sets for v in group])


def reduce_last(first, first_y, second, second_x):
    first, second = add(first, first_y), add(second, second_x)
    return first[0], first[1], second[0], second[1]


def reduce_done(first, first_x, second, second_y):
    first = first.astype(F32) + first_x.astype(F32)
    second = second.astype(F32) + second_y.astype(F32)
    return jnp.concatenate([first, second], axis=-1)


LOG2E = 1.4426950408889634


def write_bias(query_ref, key_ref, bias_ref):
    query_code = query_ref[:, 0:1]
    query_pos = query_ref[:, 1:2]
    key_code = key_ref[0:1, :]
    key_pos = key_ref[1:2, :]
    key_valid = key_ref[2:3, :]
    allowed = (
        (query_code == key_code)
        & (key_pos <= query_pos)
        & ((key_valid == 1) | (key_pos == query_pos))
    )
    bias_ref[...] = jnp.where(allowed, 0.0, -1e30)


def forward_kernel(query_ref, key_ref, q_ref, k_ref, v_ref, out_ref, low_ref, bias_ref, *, scale):
    @pl.when(pl.program_id(0) == 0)
    def _():
        write_bias(query_ref, key_ref, bias_ref)

    scores = dot_nt(q_ref[...], k_ref[...])
    weights = jnp.exp2(scores * (scale * LOG2E) + bias_ref[...])
    totals = jnp.sum(weights, axis=-1, keepdims=True)
    unnorm = dot_nn(weights.astype(BF16), v_ref[...])
    attended = unnorm / totals
    out_ref[...] = attended
    low_ref[...] = attended.astype(BF16)


def backward_kernel(
    query_ref, key_ref, q_ref, k_ref, v_ref, att_ref, grad_ref, dq_ref, dk_ref, dv_ref, bias_ref, *, scale
):
    @pl.when(pl.program_id(0) == 0)
    def _():
        write_bias(query_ref, key_ref, bias_ref)

    q, k, v = q_ref[...], k_ref[...], v_ref[...]
    grad = grad_ref[...]
    scores = dot_nt(q, k)
    weights = jnp.exp2(scores * (scale * LOG2E) + bias_ref[...])
    totals = jnp.sum(weights, axis=-1, keepdims=True)
    grad_totals = -jnp.sum(grad * att_ref[...], axis=-1, keepdims=True) / totals
    grad_unnorm = (grad / totals).astype(BF16)
    grad_weights = dot_nt(grad_unnorm, v)
    grad_scores = (weights * (grad_weights + grad_totals)).astype(BF16)
    dq_ref[...] = (dot_nn(grad_scores, k) * scale).astype(BF16)
    dk_ref[...] = (dot_tn(grad_scores, q) * scale).astype(BF16)
    dv_ref[...] = dot_tn(weights.astype(BF16), grad_unnorm).astype(BF16)


def attention_specs(rows, keys):
    whole = lambda shape: pl.BlockSpec(shape, lambda h: (0, 0))
    head = lambda n, first=0: pl.BlockSpec((n, HEAD_DIM), lambda h: (0, first + h))
    return whole, head


def attend_forward(query_info, key_info, queries, pairs):
    rows, width = queries.shape
    count = pairs.shape[0]
    whole, head = attention_specs(rows, count)
    return pl.pallas_call(
        functools.partial(forward_kernel, scale=1.0 / math.sqrt(HEAD_DIM)),
        grid=(width // HEAD_DIM,),
        in_specs=[
            whole(query_info.shape),
            whole(key_info.shape),
            head(rows),
            head(count),
            head(count, width // HEAD_DIM),
        ],
        out_specs=[head(rows), head(rows)],
        out_shape=[
            jax.ShapeDtypeStruct((rows, width), F32),
            jax.ShapeDtypeStruct((rows, width), BF16),
        ],
        scratch_shapes=[pltpu.VMEM((rows, count), F32)],
        compiler_params=pltpu.CompilerParams(vmem_limit_bytes=40 << 20),
        cost_estimate=pl.CostEstimate(
            flops=4 * rows * count * width,
            transcendentals=rows * count * width // HEAD_DIM,
            bytes_accessed=2 * (2 * count + 4 * rows) * width,
        ),
        name="attend_forward",
    )(query_info, key_info, queries, pairs, pairs)


def attend_backward(query_info, key_info, queries, pairs, attended, grads):
    rows, width = queries.shape
    count = pairs.shape[0]
    whole, head = attention_specs(rows, count)
    return pl.pallas_call(
        functools.partial(backward_kernel, scale=1.0 / math.sqrt(HEAD_DIM)),
        grid=(width // HEAD_DIM,),
        in_specs=[
            whole(query_info.shape),
            whole(key_info.shape),
            head(rows),
            head(count),
            head(count, width // HEAD_DIM),
            head(rows),
            head(rows),
        ],
        out_specs=[head(rows), head(count), head(count)],
        out_shape=[
            jax.ShapeDtypeStruct((rows, width), BF16),
            jax.ShapeDtypeStruct((count, width), BF16),
            jax.ShapeDtypeStruct((count, width), BF16),
        ],
        scratch_shapes=[pltpu.VMEM((rows, count), F32)],
        compiler_params=pltpu.CompilerParams(vmem_limit_bytes=48 << 20),
        cost_estimate=pl.CostEstimate(
            flops=10 * rows * count * width,
            transcendentals=rows * count * width // HEAD_DIM,
            bytes_accessed=2 * (4 * count + 6 * rows) * width,
        ),
        name="attend_backward",
    )(query_info, key_info, queries, pairs, pairs, attended, grads)


def shards(
    inputs,
    kv_input,
    segment_ids,
    valid_mask,
    w_query,
    w_key,
    w_value,
    w_out,
    w_gate,
    w_up,
    w_down,
    gain_attn,
    gain_ffn,
    cotangent,
):
    rows, width = inputs.shape
    x, core, z, y = (lax.axis_index(name) for name in ALL)
    depth = lax.axis_size("z")
    devices = 4 * depth * 2
    dp, fsdp = x * 2 + core, z * 2 + y
    group_rows = rows * depth * 2
    seq_length = min(SEQ_LEN, group_rows)
    wide = w_query.shape[0]
    hidden = w_down.shape[0]

    small = jnp.concatenate(
        [gain_attn.astype(F32), gain_ffn.astype(F32), segment_ids.astype(F32), valid_mask.astype(F32)]
    )
    small = lax.all_to_all(
        jnp.broadcast_to(small[None], (devices, small.shape[0])), ALL, 0, 0, tiled=True
    )
    reach = min(-(-(seq_length // 2 - 1) // (2 * rows)), depth - 1)
    natural = 2 * wide % 128 == 0


    weights = jnp.concatenate([w_key, w_value, w_query, w_out], axis=1)
    weights = lax.all_gather(weights, ALL, axis=0, tiled=True)
    levels = [kv_input, shift(kv_input, "z", 1)]
    others = [swap(kv_input, "y")]

    def split_columns(w):
        return w.reshape(wide, 4, depth, 2, hidden).transpose(1, 3, 0, 2, 4)

    pair = jnp.stack([split_columns(w_gate), split_columns(w_up)], axis=2)
    pair = pair.reshape(8, 2 * wide, depth * hidden)
    levels[1], others[0], pair = together(levels[1], others[0], pair)

    others.append(swap(levels[1], "y"))
    for _ in range(reach - 1):
        levels.append(shift(levels[-1], "z", 1))
    for level in levels[2:-1]:
        others.append(swap(level, "y"))
    pair = lax.all_to_all(pair, GROUP, 0, 0, tiled=True)
    pair, *held = together(pair, *others, *levels[1:])
    others, levels = held[: len(others)], [kv_input] + held[len(others) :]

    if len(others) < len(levels):
        others.append(swap(levels[-1], "y"))
    pair = pair.reshape(8, 2, wide, depth * hidden).transpose(1, 3, 0, 2)
    pair = settle(pair.reshape(2 * depth * hidden, 8 * wide))
    pair, small, weights, cot_first, down, *halo = together(
        pair, small, weights, cotangent, w_down, *levels, *others
    )

    pair = lax.all_gather(pair, "z", axis=0, tiled=False)
    cot_y = swap(cot_first, "y")
    pairs = project(halo, weights, 0, 2, BF16)
    cot_y, pairs = together(cot_y, pairs)
    cot_pair = jnp.concatenate([cot_first, cot_y])
    cot_x = swap(cot_pair, "x")
    full_gain_attn = small[:, :wide].reshape(-1)
    full_gain_ffn = small[:, wide : 2 * wide].reshape(-1)
    ids_all = lax.dynamic_slice_in_dim(small, dp * depth * 2, depth * 2, 0)[:, 2 * wide :]
    ids_all = ids_all.astype(jnp.int32)
    block_ids = []
    for other in range(2):
        for level in range(reach + 1):
            block_ids.append(2 * (z - level) + (y ^ other))
    key_pos, key_seg, key_valid = [], [], []
    for block in block_ids:
        here = pick(ids_all, jnp.maximum(block, 0), 0)
        key_seg.append(here[:rows])
        key_valid.append(here[rows:])
        key_pos.append(block * rows + jnp.arange(rows, dtype=jnp.int32))
    key_pos, key_seg, key_valid = (jnp.concatenate(v) for v in (key_pos, key_seg, key_valid))
    query_pos = fsdp * rows + jnp.arange(rows, dtype=jnp.int32)
    code = lambda seg, pos: seg * 4096 + pos // seq_length
    zeros = jnp.zeros_like(key_pos)
    key_info = jnp.stack([code(key_seg, key_pos), key_pos, key_valid] + [zeros] * 5)
    zeros = jnp.zeros_like(query_pos)
    query_info = jnp.stack([code(segment_ids, query_pos), query_pos] + [zeros] * 6, axis=1)
    stream = inputs.astype(F32)
    squares_in = jnp.sum(stream * stream, axis=-1, keepdims=True)
    factor_one = lax.rsqrt(squares_in / width + EPSILON)
    unit_one = stream * factor_one
    normed1 = (unit_one * full_gain_attn).astype(BF16)
    queries = project([normed1], weights, 2, 1, BF16)
    attended_f, attended = attend_forward(query_info, key_info, queries, pairs)
    middle = stream + project([attended], weights, 3, 1, F32)
    squares_mid = jnp.sum(middle * middle, axis=-1, keepdims=True)
    factor_two = lax.rsqrt(squares_mid / width + EPSILON)
    unit_two = middle * factor_two
    normed2 = (unit_two * full_gain_ffn).astype(BF16)
    if not natural:
        normed2 = normed2.reshape(rows, 4, depth, 2 * wide).swapaxes(1, 2).reshape(rows, width)
    half = width // 2
    first, second, cot_x, pair, down = together(
        normed2[:, :half], normed2[:, half:], cot_x, pair, down
    )
    part_down = lax.all_gather(down, "z", axis=0, tiled=False)
    cot_near = jnp.concatenate([cot_pair, cot_x])
    cot_far = swap(cot_near, "core")

    halo = jnp.concatenate(halo)
    first_x, second_y = swap(first, "x"), swap(second, "y")
    halo_far, halo_near = columns(halo, 1, 3, dp), columns(halo, 0, 2, dp)
    first_x, second_y, halo_far, halo_near, cot_near, cot_far = together(
        first_x, second_y, halo_far, halo_near, cot_near, cot_far
    )
    first, second = jnp.stack([first, first_x]), jnp.stack([second, second_y])
    first_y, second_x = swap(first, "y"), swap(second, "x")
    part_down = part_down.reshape(depth * hidden, width)
    attended_far, attended_near = columns(attended, 1, 3, dp), columns(attended, 0, 2, dp)
    normed1_far, normed1_near = columns(normed1, 1, 3, dp), columns(normed1, 0, 2, dp)
    (
        first_y, second_x, part_down, attended_far, attended_near, normed1_far, normed1_near,
    ) = together(
        first_y, second_x, part_down, attended_far, attended_near, normed1_far, normed1_near,
    )
    first = jnp.stack([first, first_y], axis=1)
    second = jnp.stack([second, second_x])
    x_near = jnp.concatenate([first, second], axis=-1).reshape(4 * rows, width)
    x_far = swap(x_near, "core")
    feeds = pair

    out_far, grad_far, act_far, hid_far = feed(x_far, cot_far, feeds, part_down, natural)
    got = swap(grad_far, "core")
    out_near, act_near, hid_near, first, first_away, second, second_away = feed(
        x_near, cot_near, feeds, part_down, natural, got
    )
    out_got = swap(out_far, "core")
    first_y, second_x = swap(first_away, "y"), swap(second_away, "x")
    grad_pair, grad_down = feed_weights(
        [(x_near, cot_near, act_near, hid_near), (x_far, cot_far, act_far, hid_far)], depth, natural
    )
    first, first_away, second, second_away = reduce_last(first, first_y, second, second_x)
    first, first_away, second, second_away, grad_pair, grad_down, out_near, out_got = together(
        first, first_away, second, second_away, grad_pair, grad_down, out_near, out_got
    )
    grad_pair = lax.psum_scatter(grad_pair, "z", scatter_dimension=0, tiled=True)
    share_down = collect(grad_down)
    first_x, second_y = swap(first_away, "x"), swap(second_away, "y")
    grad_normed2 = reduce_done(first, first_x, second, second_y)
    if not natural:
        grad_normed2 = grad_normed2.reshape(rows, depth, 4, 2 * wide).swapaxes(1, 2)
        grad_normed2 = grad_normed2.reshape(rows, width)

    part_gain_ffn = jnp.sum(grad_normed2 * unit_two, axis=0)
    inner = grad_normed2 * full_gain_ffn
    grad_middle = cotangent.astype(F32) + factor_two * (
        inner - unit_two * jnp.mean(inner * unit_two, axis=-1, keepdims=True)
    )
    grad_branch = grad_middle.astype(BF16)
    far_out = weight_grad(attended_far, grad_branch)
    far_out, grad_branch, grad_middle = together(far_out, grad_branch, grad_middle)
    got_out = swap(far_out, "core")
    grad_attended = project_back([grad_branch], weights, [3], F32)
    out_home, out_away = weight_grad(attended_near, grad_branch, got_out, 2)
    out_home, out_away, grad_attended = together(out_home, out_away, grad_attended)

    out_x = swap(out_away, "x")
    grad_queries, grad_keys, grad_values = attend_backward(
        query_info, key_info, queries, pairs, attended_f, grad_attended
    )
    far_key = weight_grad(halo_far, grad_keys)
    out_x, far_key, grad_keys, grad_values, grad_queries = together(
        out_x, far_key, grad_keys, grad_values, grad_queries
    )

    got_key = swap(far_key, "core")
    far_value = weight_grad(halo_far, grad_values)
    got_key, far_value, grad_keys, grad_values, grad_queries = together(
        got_key, far_value, grad_keys, grad_values, grad_queries
    )

    got_value = swap(far_value, "core")
    key_home, key_away = weight_grad(halo_near, grad_keys, got_key, 2)
    got_value, key_home, key_away, grad_keys, grad_values, grad_queries, grad_pair = together(
        got_value, key_home, key_away, grad_keys, grad_values, grad_queries, grad_pair
    )

    key_x = swap(key_away, "x")
    out_away, out_home = split_y(by_owner(add(out_home, out_x)))
    out_y = swap(out_away, "y")
    value_near = weight_grad(halo_near, grad_values, got_value)
    far_query = weight_grad(normed1_far, grad_queries)
    grad_halo = project_back([grad_keys, grad_values], weights, [0, 1], BF16)
    query_home, query_away = weight_grad(normed1_near, grad_queries, swap(far_query, "core"), 2)
    grad_pair = settle(grad_pair.reshape(2 * depth * hidden, 8 * wide)).T
    key_x, out_y, value_near, query_home, query_away, grad_halo, grad_queries, grad_pair = together(
        key_x, out_y, value_near, query_home, query_away, grad_halo, grad_queries, grad_pair
    )

    value_away, value_home = split_y(value_near.reshape(2, depth, 2, wide, width))
    query_x, value_y = swap(query_away, "x"), swap(value_away, "y")
    grad_halo = grad_halo.reshape(2, reach + 1, rows, width)
    back = grad_halo[:, reach]
    for level in reversed(range(1, reach)):
        back = shift(back, "z", -1)
        back = add(grad_halo[:, level], back) if level > 1 else back
    share_out = collect(add(out_home, out_y))
    grad_normed1 = project_back([grad_queries], weights, [2], F32)
    grad_pair = settle(grad_pair).reshape(8, wide, 2 * depth * hidden)
    grad_pair = lax.all_to_all(grad_pair, GROUP, 0, 0, tiled=True)
    query_x, value_y, back, grad_normed1, grad_pair = together(
        query_x, value_y, back, grad_normed1, grad_pair
    )

    key_away, key_home = split_y(by_owner(add(key_home, key_x)))
    query_away, query_home = split_y(by_owner(add(query_home, query_x)))
    value_home = add(value_home, value_y)
    key_y, query_y, value_x = swap(key_away, "y"), swap(query_away, "y"), swap(value_home[1], "x")
    if reach > 1:
        back = add(grad_halo[:, 1], back)
    back = shift(back, "z", -1)
    part_gain_attn = jnp.sum(grad_normed1 * unit_one, axis=0)
    inner = grad_normed1 * full_gain_attn
    grad_inputs = grad_middle + factor_one * (
        inner - unit_one * jnp.mean(inner * unit_one, axis=-1, keepdims=True)
    )
    grad_pair = grad_pair.reshape(4, 2, wide, 2, depth, hidden).transpose(3, 2, 0, 4, 1, 5)
    grad_pair = grad_pair.reshape(2, wide, devices * hidden).astype(F32)
    sums = add(out_near, out_got).reshape(2, 2, rows, width)
    sums = sums[:, 0, :, :half], sums[:, 1, :, :half], sums[0, :, :, half:], sums[1, :, :, half:]
    key_y, query_y, value_x, back, grad_inputs, share_gate, share_up, *sums = together(
        key_y, query_y, value_x, back, grad_inputs, grad_pair[0], grad_pair[1], *sums
    )

    shares = jnp.concatenate(
        [add(key_home, key_y), add(value_home[0], value_x), add(query_home, query_y)], axis=1
    )
    shares = lax.psum_scatter(shares, "z", scatter_dimension=0, tiled=True)[0].astype(F32)
    sum_y, sum_x = swap(sums[1], "y"), swap(sums[3], "x")
    back = add(grad_halo[:, 0], back)
    sum_y, sum_x, back = together(sum_y, sum_x, back)
    sums = reduce_last(sums[0], sum_y, sums[2], sum_x)
    back_y = swap(back[1], "y")
    sum_x, sum_y = together(swap(sums[1], "x"), swap(sums[3], "y"))
    grad_kv_input = back[0].astype(F32) + back_y.astype(F32)
    result = middle + reduce_done(sums[0], sum_x, sums[2], sum_y)
    valid = valid_mask.astype(F32)
    squares_out = jnp.sum(result * result, axis=-1)
    sums = jnp.stack(
        [
            jnp.sum(valid * squares_in[:, 0]),
            jnp.sum(valid * squares_mid[:, 0]),
            jnp.sum(valid * squares_out),
            jnp.sum(valid),
        ]
    )
    tiny = jnp.concatenate(
        [
            part_gain_attn.reshape(devices, wide),
            part_gain_ffn.reshape(devices, wide),
            jnp.broadcast_to(sums[None], (devices, 4)),
        ],
        axis=1,
    )
    tiny = lax.all_to_all(tiny, ALL, 0, 0, tiled=True)
    share_key, share_value, share_query = (
        shares[i * wide : (i + 1) * wide] for i in range(3)
    )

    tiny = jnp.sum(tiny, axis=0)
    divisor = tiny[2 * wide + 3] * width
    rms_in = jnp.sqrt(tiny[2 * wide] / divisor)
    rms_mid = jnp.sqrt(tiny[2 * wide + 1] / divisor)
    rms_out = jnp.sqrt(tiny[2 * wide + 2] / divisor)
    return (
        result.astype(BF16),
        grad_inputs,
        grad_kv_input,
        share_query,
        share_key,
        share_value,
        share_out,
        share_gate,
        share_up,
        share_down,
        tiny[:wide],
        tiny[wide : 2 * wide],
        rms_in,
        rms_mid,
        rms_out,
    )


def solution(mesh):
    inner = Mesh(
        mesh.devices.reshape(2, mesh.shape["dp"] // 2, mesh.shape["fsdp"] // 2, 2), ALL
    )
    rows, flat = P(ALL, None), P(ALL)
    return jax.shard_map(
        shards,
        mesh=inner,
        in_specs=(rows, rows, flat, flat) + (rows,) * 7 + (flat, flat, rows),
        out_specs=(rows,) * 10 + (flat, flat, P(), P(), P()),
        check_vma=False,
    )
```

time: 1300 us -> 946 us (0.73)
  waiting for transfers between devices: 548 us -> 345 us
  starting transfers between devices: 173 us -> 81.9 us
  matrix products: 68.3 us -> 0 us
  Pallas kernels: 213 us -> 274 us
  other arithmetic: 115 us -> 74.1 us
    ppermute x72 -> x34, waiting for transfers between devices: 511 us -> 107 us  [swap(): lax.ppermute(a, axis, [(i, i ^ step) for i in range(lax.axis_size(axis))])]
    all_gather x1 -> x2, waiting for transfers between devices: 0.02 us -> 130 us  [the longest x1 107 us: shards(): weights = lax.all_gather(weights, ALL, axis=0, tiled=True)]
    ppermute x72 -> x34, starting transfers between devices: 133 us -> 30.2 us  [swap(): lax.ppermute(a, axis, [(i, i ^ step) for i in range(lax.axis_size(axis))])]
    dot_general x12 -> x0, matrix products: 68.3 us -> none  [dot_tn(): lax.dot_general(a, b, (((0,), (0,)), ((), ())), preferred_element_type=F32)]
    pallas_call x9 -> x20, Pallas kernels: 171 us -> 232 us  [the longest x2 54.2 us: feed(): pl.pallas_call(functools.partial(feed_kernel, spans=level_spans(width, de...]
    all_to_all x1, waiting for transfers between devices: 0.01 us -> 36.8 us  [shards(): grad_pair = lax.all_to_all(grad_pair, GROUP, 0, 0, tiled=True)]
    slice x6 -> x3, local copies, waits for them, and re-layouts: 31.1 us -> 5.44 us  [the longest x1 2.95 us: shards(): grad_pair[1]]
    unnamed x179 -> x178, local copies, waits for them, and re-layouts: 21 us -> 43.2 us
  transfers between devices with their start and end apart: 84 -> 49, of which waited for: 34 -> 25; matrix products, arithmetic and copies ran while one was open for 24% -> 18% of each run, Pallas kernels for 13% -> 26%
where the time goes in v2:
time: 946 us; the launch traced here: 934 us
  waiting for transfers between devices  345 us (36%)
  Pallas kernels  274 us (29%)
  local copies, waits for them, and re-layouts  137 us (14%)
  starting transfers between devices  81.9 us (9%)
  other arithmetic  74.1 us (8%)
  between operations  21.8 us (2%)
    all_gather x1, waiting for transfers between devices, shards(): weights = lax.all_gather(weights, ALL, axis=0, tiled=True)  107 us
    ppermute x34, waiting for transfers between devices, swap(): lax.ppermute(a, axis, [(i, i ^ step) for i in range(lax.axis_size(axis))])  107 us
    pallas_call x2, Pallas kernels, feed(): pl.pallas_call(functools.partial(feed_kernel, spans=level_spans(width, de...  54.2 us
    pallas_call x8, Pallas kernels, weight_grad(): pl.pallas_call(functools.partial(weight_grad_kernel, parts=parts), grid=(...  53.8 us
    pallas_call x3, Pallas kernels, project_back(): pl.pallas_call(functools.partial(project_back_kernel, count=count), grid=...  49.5 us
    unnamed x178, local copies, waits for them, and re-layouts  43.2 us
    pallas_call x3, Pallas kernels, project(): pl.pallas_call(project_kernel, grid=(cols // tile,), in_specs=[pl.BlockSp...  43.1 us
    all_to_all x1, waiting for transfers between devices, shards(): grad_pair = lax.all_to_all(grad_pair, GROUP, 0, 0, tiled=True)  36.8 us
  transfers between devices with their start and end apart: 49, of which 25 were waited for; matrix products, arithmetic and copies ran while one was open for 18% of the time, Pallas kernels for 26%

profile of v2, /device:TPU:0, one launch (start us, length us, event | category | flops | bytes accessed | tf_op | source)
XLA Modules:
  0.0 934.1 jit_solution(16321457665322655916)
XLA Ops:
  31.7 21.9 %collective-permute-done = bf16[256,2048]{0,1:T(8,128)(2,1)} collective-permute-done((bf16[256,2048]{0,1:T(8,128)(2,1)}, bf16[256,2048]{0,1:T(8,128)(2,1)}, u32[]{:S(2)}, u32[]{:S(2)}) %collective-permute-start) | collective-permute-done | bytes 1048608 | tf_op jit(solution)/shard_map/ppermute | solution.py:39
  61.9 12.0 %collective-permute-start.3 = (bf16[256,2048]{0,1:T(8,128)(2,1)}, bf16[256,2048]{0,1:T(8,128)(2,1)}, u32[]{:S(2)}, u32[]{:S(2)}) collective-permute-start(bf16[256,2048]{0,1:T(8,128)(2,1)} %collective-permute-done), channel_id=1, source_target_pairs={{0,2},{2,4},{4,6},{1,3},{3,5},{5,7},{8,10},{10,12},{12,14},{9,11},... | collective-permute-start | bytes 3145736 | tf_op jit(solution)/shard_map/ppermute | solution.py:39
  74.1 13.7 %all-to-all-done = bf16[8,128,688]{1,2,0:T(8,128)(2,1)S(1)} async-done(((bf16[8,128,688]{1,2,0:T(8,128)(2,1)}), bf16[8,128,688]{1,2,0:T(8,128)(2,1)S(1)}, u32[]{:S(2)}, u32[]{:S(2)}) %all-to-all-start) | async-done | bytes 1409056 | tf_op jit(solution)/shard_map/all_to_all | solution.py:544
  88.6 19.1 %all-to-all-start.1 = ((f32[32,1,640]{2,1,0:T(1,128)}), f32[32,1,640]{2,1,0:T(1,128)S(1)}, u32[]{:S(2)}, u32[]{:S(2)}) async-start(f32[32,1,640]{2,1,0:T(1,128)} %broadcast_in_dim.4), calls=%async_computation.1 | async-start | bytes 163840 | tf_op jit(solution)/shard_map/all_to_all | solution.py:520
  107.8 8.8 collective-permute-done.2
  133.2 10.0 %collective-permute-done.4 = bf16[256,2048]{0,1:T(8,128)(2,1)} collective-permute-done((bf16[256,2048]{0,1:T(8,128)(2,1)}, bf16[256,2048]{0,1:T(8,128)(2,1)}, u32[]{:S(2)}, u32[]{:S(2)}) %collective-permute-start.4) | collective-permute-done | bytes 1048608 | tf_op jit(solution)/shard_map/ppermute | solution.py:34
  143.2 107.4 %all-gather.7.cloned.1.call-done.refs_1_.refs_6_.refs_2_.refs_3_ = bf16[2048,8192]{1,0:T(8,128)(2,1)} async-done(((bf16[64,8192]{1,0:T(8,128)(2,1)}), bf16[2048,8192]{1,0:T(8,128)(2,1)}) %all-gather.7.cloned.1.call-update) | async-done | bytes 33554448 | tf_op jit(solution)/shard_map/all_gather | solution.py:528
  262.0 31.7 %project.4.k_ref.v_ref = bf16[1536,4096]{1,0:T(8,128)(2,1)} custom-call(bf16[256,2048]{1,0:T(8,128)(2,1)S(1)} %copy-done.5, bf16[256,2048]{1,0:T(8,128)(2,1)S(1)} %copy.92.refs_1_, bf16[256,2048]{1,0:T(8,128)(2,1)S(1)} %copy.93.refs_2_, bf16[256,2048]{1,0:T(8,128)(2,1)} %copy.94.refs_3_, bf16[256,2048]{1,0:T(8,128)(2,1)} %copy.95.refs_4_, ...), custom_call_target="tpu_custom_call" | custom-call | flops 25769803776 | bytes 35651584 | tf_op jit(solution)/shard_map/project/pallas_call | solution.py:146
  306.1 15.9 %attend_forward.1 = (f32[256,2048]{1,0:T(8,128)S(1)}, bf16[256,2048]{1,0:T(8,128)(2,1)S(1)}) custom-call(s32[256,8]{1,0:T(8,128)S(1)} %copy.97.query_ref, s32[8,1536]{1,0:T(8,128)S(1)} %stack.96.key_ref, bf16[256,2048]{1,0:T(8,128)(2,1)S(1)} %project.3.q_ref, bf16[1536,4096]{1,0:T(8,128)(2,1)} %project.4.k_ref.v_ref, bf16[1536,4096]{1,0:T(8,128)(2,1)} %project.4.k_ref.v_ref), custom_call_target="tpu_custom_call" | custom-call | flops 3221225472 | bytes 16777216 | tf_op jit(solution)/shard_map/attend_forward/pallas_call | solution.py:432
  333.8 18.1 %collective-permute-done.6 = bf16[512,2048]{1,0:T(8,128)(2,1)} collective-permute-done((bf16[512,2048]{1,0:T(8,128)(2,1)S(1)}, bf16[512,2048]{1,0:T(8,128)(2,1)}, u32[]{:S(2)}, u32[]{:S(2)}) %collective-permute-start.6) | collective-permute-done | bytes 2097184 | tf_op jit(solution)/shard_map/ppermute | solution.py:34
  396.8 22.9 %all-gather.11.cloned.1.call-done = bf16[4,172,2048]{2,1,0:T(8,128)(2,1)} async-done(((bf16[1,172,2048]{2,1,0:T(8,128)(2,1)}), bf16[4,172,2048]{2,1,0:T(8,128)(2,1)}) %all-gather.11.cloned.1.call-update) | async-done | bytes 2818064 | tf_op jit(solution)/shard_map/all_gather | solution.py:601
  436.1 25.8 %feed.1 = (bf16[1024,2048]{1,0:T(8,128)(2,1)}, bf16[1024,2048]{1,0:T(8,128)(2,1)}, bf16[688,1024]{1,0:T(8,128)(2,1)}, bf16[1376,1024]{1,0:T(8,128)(2,1)}) custom-call(bf16[1024,2048]{1,0:T(8,128)(2,1)} %copy-done.74, bf16[1024,2048]{1,0:T(8,128)(2,1)} %collective-permute-done.9.cot_ref.refs_5_, bf16[4,1376,512]{2,1,0:T(8,128)(2,1)} %bitcast.218, ...), custom_call_target="tpu_custom_call" | custom-call | flops 17314086912 | bytes 29458432 | tf_op jit(solution)/shard_map/feed/pallas_call | solution.py:277
  469.5 28.4 %feed_sum.1 = (bf16[1024,2048]{1,0:T(8,128)(2,1)}, bf16[688,1024]{1,0:T(8,128)(2,1)}, bf16[1376,1024]{1,0:T(8,128)(2,1)}, bf16[2,256,1024]{2,1,0:T(8,128)(2,1)},...) custom-call(bf16[1024,2048]{1,0:T(8,128)(2,1)} %bitcast.195, ...), custom_call_target="tpu_custom_call" | custom-call | flops 17314086912 | bytes 29458432 | tf_op jit(solution)/shard_map/feed_sum/pallas_call | solution.py:277
  502.1 23.7 %feed_weights.1 = (bf16[4,1376,512]{2,1,0:T(8,128)(2,1)}, bf16[4,172,2048]{2,1,0:T(8,128)(2,1)}) custom-call(bf16[1024,2048]{1,0:T(8,128)(2,1)} %bitcast.196, bf16[1024,2048]{1,0:T(8,128)(2,1)} %constant_dynamic-update-slice_fusion.20.cot_ref.refs_1_, bf16[688,1024]{1,0:T(8,128)(2,1)S(1)} %copy-done.22, bf16[1376,1024]{1,0:T(8,128)(2,1)} %get-tuple-element.180.refs_3_, ...), custom_call_target="tpu_custom_call" | custom-call | flops 17314086912 | bytes 33685504 | tf_op jit(solution)/shard_map/feed_weights/pallas_call | solution.py:330
  529.5 12.5 %collective-permute-done.17 = bf16[256,1024]{1,0:T(8,128)(2,1)S(1)} collective-permute-done((bf16[256,1024]{1,0:T(8,128)(2,1)}, bf16[256,1024]{1,0:T(8,128)(2,1)S(1)}, u32[]{:S(2)}, u32[]{:S(2)}) %collective-permute-start.17) | collective-permute-done | bytes 524320 | tf_op jit(solution)/shard_map/ppermute | solution.py:34
  564.4 25.9 %attend_backward.1 = (bf16[256,2048]{1,0:T(8,128)(2,1)S(1)}, bf16[1536,2048]{1,0:T(8,128)(2,1)}, bf16[1536,2048]{1,0:T(8,128)(2,1)}) custom-call(s32[256,8]{1,0:T(8,128)S(1)} %copy.97.query_ref, s32[8,1536]{1,0:T(8,128)S(1)} %stack.96.key_ref, bf16[256,2048]{1,0:T(8,128)(2,1)S(1)} %project.3.q_ref, bf16[1536,4096]{1,0:T(8,128)(2,1)} %project.4.k_ref.v_ref, ...), custom_call_target="tpu_custom_call" | custom-call | flops 8053063680 | bytes 31457280 | tf_op jit(solution)/shard_map/attend_backward/pallas_call | solution.py:462
  593.7 8.7 weight_grad.10
  614.4 8.7 weight_grad.11
  629.6 9.7 %weight_grad.12 = (bf16[512,2048]{1,0:T(8,128)(2,1)S(1)}, bf16[512,2048]{1,0:T(8,128)(2,1)}) custom-call(bf16[1024,1536]{1,0:T(8,128)(2,1)S(1)} %copy-done.6, bf16[1536,2048]{1,0:T(8,128)(2,1)} %get-tuple-element.226.refs_1_.refs_0_, bf16[1024,2048]{1,0:T(8,128)(2,1)S(1)} %copy-done.20), custom_call_target="tpu_custom_call" | custom-call | flops 6442450944 | bytes 17825792 | tf_op jit(solution)/shard_map/weight_grad/pallas_call | solution.py:97
  662.6 34.7 %project_back.4 = bf16[1536,2048]{1,0:T(8,128)(2,1)} custom-call(bf16[1536,2048]{1,0:T(8,128)(2,1)} %get-tuple-element.226.refs_1_.refs_0_, bf16[1536,2048]{1,0:T(8,128)(2,1)} %get-tuple-element.219.refs_1_, bf16[2048,8192]{1,0:T(8,128)(2,1)} %all-gather.7.cloned.1.call-done.refs_1_.refs_6_.refs_2_.refs_3_, ...), custom_call_target="tpu_custom_call" | custom-call | flops 25769803776 | bytes 41943040 | tf_op jit(solution)/shard_map/project_back/pallas_call | solution.py:176
  704.2 9.2 weight_grad.13
  753.4 36.8 %all-to-all-done.2 = bf16[8,64,1376]{2,1,0:T(8,128)(2,1)S(1)} async-done(((bf16[8,64,1376]{2,1,0:T(8,128)(2,1)}), bf16[8,64,1376]{2,1,0:T(8,128)(2,1)S(1)}, u32[]{:S(2)}, u32[]{:S(2)}) %all-to-all-start.2) | async-done | bytes 1409056 | tf_op jit(solution)/shard_map/all_to_all | solution.py:705
  835.8 9.8 %collective-permute-done.32 = bf16[2,256,2048]{2,1,0:T(8,128)(2,1)} collective-permute-done((bf16[2,256,2048]{2,1,0:T(8,128)(2,1)}, bf16[2,256,2048]{2,1,0:T(8,128)(2,1)}, u32[]{:S(2)}, u32[]{:S(2)}) %collective-permute-start.32) | collective-permute-done | bytes 2097184 | tf_op jit(solution)/shard_map/ppermute | solution.py:39
  857.7 18.4 %collective-permute-done.33 = bf16[2,256,1024]{2,1,0:T(8,128)(2,1)S(1)} collective-permute-done((bf16[2,256,1024]{2,1,0:T(8,128)(2,1)}, bf16[2,256,1024]{2,1,0:T(8,128)(2,1)S(1)}, u32[]{:S(2)}, u32[]{:S(2)}) %collective-permute-start.33) | collective-permute-done | bytes 1048608 | tf_op jit(solution)/shard_map/ppermute | solution.py:34
  (422 shorter events, 378.3 us)
Async XLA Ops:
  7.2 243.4 %all-gather.7.cloned.1.call-start = ((), (), s32[]{:S(2)}) async-start(), calls=%async_computation.8 | async-start | bytes 34603008 | tf_op jit(solution)/shard_map/all_gather | solution.py:528
  10.9 42.7 %collective-permute-start = (bf16[256,2048]{0,1:T(8,128)(2,1)}, bf16[256,2048]{0,1:T(8,128)(2,1)}, u32[]{:S(2)}, u32[]{:S(2)}) collective-permute-start(bf16[256,2048]{0,1:T(8,128)(2,1)} %copy.84), channel_id=1, source_target_pairs={{0,2},{2,4},{4,6},{1,3},{3,5},{5,7},{8,10},{10,12},{12,14},{9,11},... | collective-permute-start | bytes 3145736 | tf_op jit(solution)/shard_map/ppermute | solution.py:39
  16.8 36.8 %collective-permute-start.1 = (bf16[256,2048]{0,1:T(8,128)(2,1)}, bf16[256,2048]{0,1:T(8,128)(2,1)}, u32[]{:S(2)}, u32[]{:S(2)}) collective-permute-start(bf16[256,2048]{0,1:T(8,128)(2,1)} %copy.84), channel_id=1, source_target_pairs={{0,1},{1,0},{2,3},{3,2},{4,5},{5,4},{6,7},{7,6},{8,9},{9,8},{10,11... | collective-permute-start | bytes 3145736 | tf_op jit(solution)/shard_map/ppermute | solution.py:34
  59.9 56.7 %collective-permute-start.2 = (bf16[256,2048]{0,1:T(8,128)(2,1)}, bf16[256,2048]{0,1:T(8,128)(2,1)}, u32[]{:S(2)}, u32[]{:S(2)}) collective-permute-start(bf16[256,2048]{0,1:T(8,128)(2,1)} %collective-permute-done), channel_id=1, source_target_pairs={{0,1},{1,0},{2,3},{3,2},{4,5},{5,4},{6,7},{7,6},{8,9},{9,8},{10,11... | collective-permute-start | bytes 3145736 | tf_op jit(solution)/shard_map/ppermute | solution.py:34
  61.9 57.3 %collective-permute-start.3 = (bf16[256,2048]{0,1:T(8,128)(2,1)}, bf16[256,2048]{0,1:T(8,128)(2,1)}, u32[]{:S(2)}, u32[]{:S(2)}) collective-permute-start(bf16[256,2048]{0,1:T(8,128)(2,1)} %collective-permute-done), channel_id=1, source_target_pairs={{0,2},{2,4},{4,6},{1,3},{3,5},{5,7},{8,10},{10,12},{12,14},{9,11},... | collective-permute-start | bytes 3145736 | tf_op jit(solution)/shard_map/ppermute | solution.py:39
  107.7 250.9 %all-gather.9.cloned.1.call-start = ((), (), s32[]{:S(2)}) async-start(), calls=%async_computation.13 | async-start | bytes 7045120 | tf_op jit(solution)/shard_map/all_gather | solution.py:556
  250.6 169.0 %all-gather.11.cloned.1.call-start = ((), (), s32[]{:S(2)}) async-start(), calls=%async_computation.14 | async-start | bytes 3604480 | tf_op jit(solution)/shard_map/all_gather | solution.py:601
  261.2 40.5 %collective-permute-start.5 = (bf16[256,2048]{1,0:T(8,128)(2,1)}, bf16[256,2048]{1,0:T(8,128)(2,1)}, u32[]{:S(2)}, u32[]{:S(2)}) collective-permute-start(bf16[256,2048]{1,0:T(8,128)(2,1)} %param.27), channel_id=1, source_target_pairs={{0,1},{1,0},{2,3},{3,2},{4,5},{5,4},{6,7},{7,6},{8,9},{9,8},{10,11... | collective-permute-start | bytes 3145736 | tf_op jit(solution)/shard_map/ppermute | solution.py:34
  303.2 48.8 %collective-permute-start.6 = (bf16[512,2048]{1,0:T(8,128)(2,1)S(1)}, bf16[512,2048]{1,0:T(8,128)(2,1)}, u32[]{:S(2)}, u32[]{:S(2)}) collective-permute-start(bf16[512,2048]{1,0:T(8,128)(2,1)S(1)} %pad_maximum_fusion.2), channel_id=1, source_target_pairs={{0,16},{16,0},{1,17},{17,1},{2,18},{18,2},{3,19},{19,3},{4,20},{20... | collective-permute-start | bytes 6291464 | tf_op jit(solution)/shard_map/ppermute | solution.py:34
  361.9 285.6 %reduce-scatter.5.cloned.1.call-start = ((), (), s32[]{:S(2)}) async-start(), calls=%async_computation.9 | async-start | bytes 7045120 | tf_op jit(solution)/shard_map/reduce_scatter | solution.py:641
  462.1 66.3 %collective-permute-start.16 = (bf16[1024,2048]{1,0:T(8,128)(2,1)}, bf16[1024,2048]{1,0:T(8,128)(2,1)}, u32[]{:S(2)}, u32[]{:S(2)}) collective-permute-start(bf16[1024,2048]{1,0:T(8,128)(2,1)} %get-tuple-element.186), channel_id=1, source_target_pairs={{0,8},{8,0},{1,9},{9,1},{2,10},{10,2},{3,11},{11,3},{4,12},{12,4},... | collective-permute-start | bytes 12582920 | tf_op jit(solution)/shard_map/ppermute | solution.py:34
  549.2 334.4 %reduce-scatter.11.cloned.1.call-start = ((), (), s32[]{:S(2)}) async-start(), calls=%async_computation.12 | async-start | bytes 3604480 | tf_op jit(solution)/shard_map/reduce_scatter | solution.py:129
  562.9 48.0 %collective-permute-start.20 = (bf16[512,2048]{1,0:T(8,128)(2,1)S(1)}, bf16[512,2048]{1,0:T(8,128)(2,1)S(1)}, u32[]{:S(2)}, u32[]{:S(2)}) collective-permute-start(bf16[512,2048]{1,0:T(8,128)(2,1)S(1)} %get-tuple-element.195), channel_id=1, source_target_pairs={{0,16},{16,0},{1,17},{17,1},{2,18},{18,2},{3,19},{19,3},{4,20},{20... | collective-permute-start | bytes 6291464 | tf_op jit(solution)/shard_map/ppermute | solution.py:34
  650.9 62.5 %collective-permute-start.25 = (bf16[1024,2048]{1,0:T(8,128)(2,1)}, bf16[1024,2048]{1,0:T(8,128)(2,1)}, u32[]{:S(2)}, u32[]{:S(2)}) collective-permute-start(bf16[1024,2048]{1,0:T(8,128)(2,1)} %weight_grad.14), channel_id=1, source_target_pairs={{0,8},{8,0},{1,9},{9,1},{2,10},{10,2},{3,11},{11,3},{4,12},{12,4},... | collective-permute-start | bytes 12582920 | tf_op jit(solution)/shard_map/ppermute | solution.py:34
  659.6 60.2 %collective-permute-start.24 = (bf16[4,64,2048]{2,1,0:T(8,128)(2,1)S(1)}, bf16[4,64,2048]{2,1,0:T(8,128)(2,1)}, u32[]{:S(2)}, u32[]{:S(2)}) collective-permute-start(bf16[4,64,2048]{2,1,0:T(8,128)(2,1)S(1)} %dynamic-slice_bitcast_fusion.3), channel_id=1, source_target_pairs={{0,1},{1,0},{2,3},{3,2},{4,5},{5,4},{6,7},{7,6},{8,9},{9,8},{10,11... | collective-permute-start | bytes 3145736 | tf_op jit(solution)/shard_map/ppermute | solution.py:34
  661.1 58.7 %collective-permute-start.23 = (bf16[512,2048]{1,0:T(8,128)(2,1)}, bf16[512,2048]{1,0:T(8,128)(2,1)}, u32[]{:S(2)}, u32[]{:S(2)}) collective-permute-start(bf16[512,2048]{1,0:T(8,128)(2,1)} %get-tuple-element.216), channel_id=1, source_target_pairs={{0,16},{16,0},{1,17},{17,1},{2,18},{18,2},{3,19},{19,3},{4,20},{20... | collective-permute-start | bytes 6291464 | tf_op jit(solution)/shard_map/ppermute | solution.py:34
  721.8 68.4 %collective-permute-start.28 = (bf16[2,4,64,2048]{3,2,1,0:T(8,128)(2,1)}, bf16[2,4,64,2048]{3,2,1,0:T(8,128)(2,1)}, u32[]{:S(2)}, u32[]{:S(2)}) collective-permute-start(bf16[2,4,64,2048]{3,2,1,0:T(8,128)(2,1)} %dynamic-slice_bitcast_fusion), channel_id=1, source_target_pairs={{0,1},{1,0},{2,3},{3,2},{4,5},{5,4},{6,7},{7,6},{8,9},{9,8},{10,11... | collective-permute-start | bytes 6291464 | tf_op jit(solution)/shard_map/ppermute | solution.py:34
  725.8 66.4 %collective-permute-start.29 = (bf16[2,256,2048]{2,1,0:T(8,128)(2,1)}, bf16[2,256,2048]{2,1,0:T(8,128)(2,1)}, u32[]{:S(2)}, u32[]{:S(2)}) collective-permute-start(bf16[2,256,2048]{2,1,0:T(8,128)(2,1)} %slice_bitcast_fusion.2), channel_id=1, source_target_pairs={{2,0},{4,2},{6,4},{3,1},{5,3},{7,5},{10,8},{12,10},{14,12},{11,9},... | collective-permute-start | bytes 6291464 | tf_op jit(solution)/shard_map/ppermute | solution.py:39
  727.1 65.2 %collective-permute-start.27 = (bf16[512,2048]{1,0:T(8,128)(2,1)}, bf16[512,2048]{1,0:T(8,128)(2,1)}, u32[]{:S(2)}, u32[]{:S(2)}) collective-permute-start(bf16[512,2048]{1,0:T(8,128)(2,1)} %get-tuple-element.230), channel_id=1, source_target_pairs={{0,16},{16,0},{1,17},{17,1},{2,18},{18,2},{3,19},{19,3},{4,20},{20... | collective-permute-start | bytes 6291464 | tf_op jit(solution)/shard_map/ppermute | solution.py:34
  733.3 56.9 %all-to-all-start.2 = ((bf16[8,64,1376]{2,1,0:T(8,128)(2,1)}), bf16[8,64,1376]{2,1,0:T(8,128)(2,1)S(1)}, u32[]{:S(2)}, u32[]{:S(2)}) async-start(bf16[8,64,1376]{2,1,0:T(8,128)(2,1)} %bitcast.193), calls=%async_computation.3 | async-start | bytes 2883584 | tf_op jit(solution)/shard_map/all_to_all | solution.py:705
  737.1 169.8 %reduce-scatter.9.cloned.1.call-start = ((), (), s32[]{:S(2)}) async-start(), calls=%async_computation.11 | async-start | bytes 1310720 | tf_op jit(solution)/shard_map/reduce_scatter | solution.py:129
  741.9 94.0 %collective-permute-start.26 = (bf16[4,64,2048]{2,1,0:T(8,128)(2,1)}, bf16[4,64,2048]{2,1,0:T(8,128)(2,1)}, u32[]{:S(2)}, u32[]{:S(2)}) collective-permute-start(bf16[4,64,2048]{2,1,0:T(8,128)(2,1)} %dynamic-slice_bitcast_fusion.2), channel_id=1, source_target_pairs={{0,1},{1,0},{2,3},{3,2},{4,5},{5,4},{6,7},{7,6},{8,9},{9,8},{10,11... | collective-permute-start | bytes 3145736 | tf_op jit(solution)/shard_map/ppermute | solution.py:34
  746.5 174.7 %reduce-scatter.7.cloned.1.call-start = ((), (), s32[]{:S(2)}) async-start(), calls=%async_computation.10 | async-start | bytes 3932160 | tf_op jit(solution)/shard_map/reduce_scatter | solution.py:733
  796.7 48.9 %collective-permute-start.32 = (bf16[2,256,2048]{2,1,0:T(8,128)(2,1)}, bf16[2,256,2048]{2,1,0:T(8,128)(2,1)}, u32[]{:S(2)}, u32[]{:S(2)}) collective-permute-start(bf16[2,256,2048]{2,1,0:T(8,128)(2,1)} %fusion.1), channel_id=1, source_target_pairs={{2,0},{4,2},{6,4},{3,1},{5,3},{7,5},{10,8},{12,10},{14,12},{11,9},... | collective-permute-start | bytes 6291464 | tf_op jit(solution)/shard_map/ppermute | solution.py:39
  (102 other events, 1348.0 us)
Sparse Core Ops, SparseCore 0:
  11.6 238.9 all-gather.6
  252.8 105.8 all-gather.8
  362.0 57.5 all-gather.10
  549.3 98.0 reduce-scatter.4
  649.6 56.6 reduce-scatter.10
  746.6 46.1 reduce-scatter.8
  852.8 59.9 reduce-scatter.6

commit v3 on v2

--- a/solution.py
+++ b/solution.py
@@ -67,6 +67,26 @@
         out_shape=jax.ShapeDtypeStruct(x.shape, x.dtype),
         name="settle",
     )(x)
+
+
+def join_kernel(*refs):
+    rows = refs[0].shape[0]
+    for i, ref in enumerate(refs[:-1]):
+        refs[-1][i * rows : (i + 1) * rows, :] = ref[...]
+
+
+def join(pieces):
+    rows, cols = pieces[0].shape
+    tile = 512
+    col = lambda n: pl.BlockSpec((n, tile), lambda i: (0, i))
+    return pl.pallas_call(
+        join_kernel,
+        grid=(cols // tile,),
+        in_specs=[col(rows)] * len(pieces),
+        out_specs=col(rows * len(pieces)),
+        out_shape=pltpu.HBM((rows * len(pieces), cols), pieces[0].dtype),
+        name="join",
+    )(*pieces)
 
 
 def take_block(a, d, dp):
@@ -168,15 +188,16 @@
     refs[-1][...] = total.astype(refs[-1].dtype)
 
 
-def project_back(grads, weights, numbers, kind):
-    tokens, width = grads[0].shape
+def project_back(grads, weights, numbers, kind, block=0, tokens=None):
+    width = grads[0].shape[1]
+    tokens = tokens or grads[0].shape[0]
     tile = 512
     count = len(grads)
     weight = lambda number: pl.BlockSpec((tile, width), lambda i: (i, number))
     return pl.pallas_call(
         functools.partial(project_back_kernel, count=count),
         grid=(width // tile,),
-        in_specs=[pl.BlockSpec((tokens, width), lambda i: (0, 0))] * count
+        in_specs=[pl.BlockSpec((tokens, width), lambda i: (block, 0))] * count
         + [weight(number) for number in numbers],
         out_specs=pl.BlockSpec((tokens, tile), lambda i: (0, i)),
         out_shape=jax.ShapeDtypeStruct((tokens, width), kind),
@@ -528,13 +549,14 @@
     weights = lax.all_gather(weights, ALL, axis=0, tiled=True)
     levels = [kv_input, shift(kv_input, "z", 1)]
     others = [swap(kv_input, "y")]
+    cot_y = swap(cotangent, "y")
 
     def split_columns(w):
         return w.reshape(wide, 4, depth, 2, hidden).transpose(1, 3, 0, 2, 4)
 
     pair = jnp.stack([split_columns(w_gate), split_columns(w_up)], axis=2)
     pair = pair.reshape(8, 2 * wide, depth * hidden)
-    levels[1], others[0], pair = together(levels[1], others[0], pair)
+    levels[1], others[0], pair, cot_y = together(levels[1], others[0], pair, cot_y)
 
     others.append(swap(levels[1], "y"))
     for _ in range(reach - 1):
@@ -542,30 +564,24 @@
     for level in levels[2:-1]:
         others.append(swap(level, "y"))
     pair = lax.all_to_all(pair, GROUP, 0, 0, tiled=True)
-    pair, *held = together(pair, *others, *levels[1:])
+    cot_pair = jnp.concatenate([cotangent, cot_y])
+    pair, cot_pair, *held = together(pair, cot_pair, *others, *levels[1:])
     others, levels = held[: len(others)], [kv_input] + held[len(others) :]
 
     if len(others) < len(levels):
         others.append(swap(levels[-1], "y"))
     pair = pair.reshape(8, 2, wide, depth * hidden).transpose(1, 3, 0, 2)
     pair = settle(pair.reshape(2 * depth * hidden, 8 * wide))
-    pair, small, weights, cot_first, down, *halo = together(
-        pair, small, weights, cotangent, w_down, *levels, *others
-    )
-
-    pair = lax.all_gather(pair, "z", axis=0, tiled=False)
-    cot_y = swap(cot_first, "y")
-    pairs = project(halo, weights, 0, 2, BF16)
-    cot_y, pairs = together(cot_y, pairs)
-    cot_pair = jnp.concatenate([cot_first, cot_y])
-    cot_x = swap(cot_pair, "x")
+    *held, pair, small = together(*levels, *others, pair, small)
+    halo = join([held[i + j] for i in range(reach + 1) for j in (0, reach + 1)])
+    halo_far, halo_near = columns(halo, 1, 3, dp), columns(halo, 0, 2, dp)
     full_gain_attn = small[:, :wide].reshape(-1)
     full_gain_ffn = small[:, wide : 2 * wide].reshape(-1)
     ids_all = lax.dynamic_slice_in_dim(small, dp * depth * 2, depth * 2, 0)[:, 2 * wide :]
     ids_all = ids_all.astype(jnp.int32)
     block_ids = []
-    for other in range(2):
-        for level in range(reach + 1):
+    for level in range(reach + 1):
+        for other in range(2):
             block_ids.append(2 * (z - level) + (y ^ other))
     key_pos, key_seg, key_valid = [], [], []
     for block in block_ids:
@@ -585,6 +601,19 @@
     factor_one = lax.rsqrt(squares_in / width + EPSILON)
     unit_one = stream * factor_one
     normed1 = (unit_one * full_gain_attn).astype(BF16)
+    normed1_far, normed1_near = columns(normed1, 1, 3, dp), columns(normed1, 0, 2, dp)
+    (
+        pair, weights, cot_pair, down, halo, halo_far, halo_near, full_gain_ffn, normed1, normed1_far,
+        normed1_near, query_info, key_info,
+    ) = together(
+        pair, weights, cot_pair, w_down, halo, halo_far, halo_near, full_gain_ffn, normed1,
+        normed1_far, normed1_near, query_info, key_info,
+    )
+
+    pair = lax.all_gather(pair, "z", axis=0, tiled=False)
+    cot_x = swap(cot_pair, "x")
+    pairs = project([halo], weights, 0, 2, BF16)
+    cot_x, pairs = together(cot_x, pairs)
     queries = project([normed1], weights, 2, 1, BF16)
     attended_f, attended = attend_forward(query_info, key_info, queries, pairs)
     middle = stream + project([attended], weights, 3, 1, F32)
@@ -595,34 +624,27 @@
     if not natural:
         normed2 = normed2.reshape(rows, 4, depth, 2 * wide).swapaxes(1, 2).reshape(rows, width)
     half = width // 2
-    first, second, cot_x, pair, down = together(
-        normed2[:, :half], normed2[:, half:], cot_x, pair, down
-    )
-    part_down = lax.all_gather(down, "z", axis=0, tiled=False)
+    first, second, cot_x = together(normed2[:, :half], normed2[:, half:], cot_x)
     cot_near = jnp.concatenate([cot_pair, cot_x])
     cot_far = swap(cot_near, "core")
 
-    halo = jnp.concatenate(halo)
     first_x, second_y = swap(first, "x"), swap(second, "y")
-    halo_far, halo_near = columns(halo, 1, 3, dp), columns(halo, 0, 2, dp)
-    first_x, second_y, halo_far, halo_near, cot_near, cot_far = together(
-        first_x, second_y, halo_far, halo_near, cot_near, cot_far
-    )
+    first_x, second_y, cot_near, cot_far, pair, down = together(
+        first_x, second_y, cot_near, cot_far, pair, down
+    )
+    part_down = lax.all_gather(down, "z", axis=0, tiled=False)
     first, second = jnp.stack([first, first_x]), jnp.stack([second, second_y])
     first_y, second_x = swap(first, "y"), swap(second, "x")
-    part_down = part_down.reshape(depth * hidden, width)
     attended_far, attended_near = columns(attended, 1, 3, dp), columns(attended, 0, 2, dp)
-    normed1_far, normed1_near = columns(normed1, 1, 3, dp), columns(normed1, 0, 2, dp)
-    (
-        first_y, second_x, part_down, attended_far, attended_near, normed1_far, normed1_near,
-    ) = together(
-        first_y, second_x, part_down, attended_far, attended_near, normed1_far, normed1_near,
+    first_y, second_x, attended_far, attended_near = together(
+        first_y, second_x, attended_far, attended_near
     )
     first = jnp.stack([first, first_y], axis=1)
     second = jnp.stack([second, second_x])
     x_near = jnp.concatenate([first, second], axis=-1).reshape(4 * rows, width)
     x_far = swap(x_near, "core")
     feeds = pair
+    part_down = part_down.reshape(depth * hidden, width)
 
     out_far, grad_far, act_far, hid_far = feed(x_far, cot_far, feeds, part_down, natural)
     got = swap(grad_far, "core")
@@ -639,7 +661,7 @@
         first, first_away, second, second_away, grad_pair, grad_down, out_near, out_got
     )
     grad_pair = lax.psum_scatter(grad_pair, "z", scatter_dimension=0, tiled=True)
-    share_down = collect(grad_down)
+    grad_down = lax.psum_scatter(grad_down, "z", scatter_dimension=0, tiled=True)
     first_x, second_y = swap(first_away, "x"), swap(second_away, "y")
     grad_normed2 = reduce_done(first, first_x, second, second_y)
     if not natural:
@@ -670,74 +692,78 @@
 
     got_key = swap(far_key, "core")
     far_value = weight_grad(halo_far, grad_values)
-    got_key, far_value, grad_keys, grad_values, grad_queries = together(
-        got_key, far_value, grad_keys, grad_values, grad_queries
+    got_key, far_value, grad_keys, grad_values, grad_queries, grad_pair = together(
+        got_key, far_value, grad_keys, grad_values, grad_queries, grad_pair
     )
 
     got_value = swap(far_value, "core")
     key_home, key_away = weight_grad(halo_near, grad_keys, got_key, 2)
-    got_value, key_home, key_away, grad_keys, grad_values, grad_queries, grad_pair = together(
-        got_value, key_home, key_away, grad_keys, grad_values, grad_queries, grad_pair
+    far_query = weight_grad(normed1_far, grad_queries)
+    got_value, key_home, key_away, far_query, grad_keys, grad_values, grad_queries = together(
+        got_value, key_home, key_away, far_query, grad_keys, grad_values, grad_queries
+    )
+
+    got_query = swap(far_query, "core")
+    value_near = weight_grad(halo_near, grad_values, got_value)
+    out_away, out_home = split_y(by_owner(add(out_home, out_x)))
+    got_query, value_near, key_away, out_away, out_home, grad_keys, grad_values = together(
+        got_query, value_near, key_away, out_away, out_home, grad_keys, grad_values
     )
 
     key_x = swap(key_away, "x")
-    out_away, out_home = split_y(by_owner(add(out_home, out_x)))
-    out_y = swap(out_away, "y")
-    value_near = weight_grad(halo_near, grad_values, got_value)
-    far_query = weight_grad(normed1_far, grad_queries)
-    grad_halo = project_back([grad_keys, grad_values], weights, [0, 1], BF16)
-    query_home, query_away = weight_grad(normed1_near, grad_queries, swap(far_query, "core"), 2)
-    grad_pair = settle(grad_pair.reshape(2 * depth * hidden, 8 * wide)).T
-    key_x, out_y, value_near, query_home, query_away, grad_halo, grad_queries, grad_pair = together(
-        key_x, out_y, value_near, query_home, query_away, grad_halo, grad_queries, grad_pair
-    )
-
     value_away, value_home = split_y(value_near.reshape(2, depth, 2, wide, width))
-    query_x, value_y = swap(query_away, "x"), swap(value_away, "y")
-    grad_halo = grad_halo.reshape(2, reach + 1, rows, width)
-    back = grad_halo[:, reach]
+    value_y = swap(value_away, "y")
+    grad_pair = settle(settle(grad_pair.reshape(2 * depth * hidden, 8 * wide)).T)
+    grad_pair = grad_pair.reshape(8, wide, 2 * depth * hidden)
+    grad_pair = lax.all_to_all(grad_pair, GROUP, 0, 0, tiled=True)
+    halves = [grad_keys, grad_values]
+    back = project_back(halves, weights, [0, 1], BF16, reach, 2 * rows)
+    back = shift(back, "z", -1)
+    grad_halo = project_back(halves, weights, [0, 1], BF16, 0, reach * 2 * rows)
+    query_home, query_away = weight_grad(normed1_near, grad_queries, got_query, 2)
+    key_x, value_y, query_home, query_away, grad_halo, back, grad_queries, *held = together(
+        key_x, value_y, query_home, query_away, grad_halo, back, grad_queries, grad_pair, out_near, out_got,
+        grad_down,
+    )
+    grad_pair, out_near, out_got, grad_down = held
+    share_down = grad_down.reshape(hidden, width).astype(F32)
+
+    key_away, key_home = split_y(by_owner(add(key_home, key_x)))
+    query_x, key_y, out_y = swap(query_away, "x"), swap(key_away, "y"), swap(out_away, "y")
     for level in reversed(range(1, reach)):
-        back = shift(back, "z", -1)
-        back = add(grad_halo[:, level], back) if level > 1 else back
-    share_out = collect(add(out_home, out_y))
+        at = level * 2 * rows
+        back = shift(add(grad_halo[at : at + 2 * rows], back), "z", -1)
     grad_normed1 = project_back([grad_queries], weights, [2], F32)
-    grad_pair = settle(grad_pair).reshape(8, wide, 2 * depth * hidden)
-    grad_pair = lax.all_to_all(grad_pair, GROUP, 0, 0, tiled=True)
-    query_x, value_y, back, grad_normed1, grad_pair = together(
-        query_x, value_y, back, grad_normed1, grad_pair
-    )
-
-    key_away, key_home = split_y(by_owner(add(key_home, key_x)))
+    value_home = add(value_home, value_y)
+    sums = add(out_near, out_got).reshape(2, 2, rows, width)
+    sums = sums[:, 0, :, :half], sums[:, 1, :, :half], sums[0, :, :, half:], sums[1, :, :, half:]
+    query_x, key_y, out_y, back, grad_normed1, grad_pair, value_home, *sums = together(
+        query_x, key_y, out_y, back, grad_normed1, grad_pair, value_home, *sums
+    )
+
+    shares_first = jnp.concatenate([add(key_home, key_y), add(out_home, out_y)], axis=1)
+    shares_first = lax.psum_scatter(shares_first, "z", scatter_dimension=0, tiled=True)
     query_away, query_home = split_y(by_owner(add(query_home, query_x)))
-    value_home = add(value_home, value_y)
-    key_y, query_y, value_x = swap(key_away, "y"), swap(query_away, "y"), swap(value_home[1], "x")
-    if reach > 1:
-        back = add(grad_halo[:, 1], back)
-    back = shift(back, "z", -1)
+    query_y, value_x = swap(query_away, "y"), swap(value_home[1], "x")
+    sum_y, sum_x = swap(sums[1], "y"), swap(sums[3], "x")
+    back = add(grad_halo[: 2 * rows], back)
+    grad_pair = grad_pair.reshape(4, 2, wide, 2, depth, hidden).transpose(3, 2, 0, 4, 1, 5)
+    grad_pair = grad_pair.reshape(2, wide, devices * hidden).astype(F32)
     part_gain_attn = jnp.sum(grad_normed1 * unit_one, axis=0)
     inner = grad_normed1 * full_gain_attn
     grad_inputs = grad_middle + factor_one * (
         inner - unit_one * jnp.mean(inner * unit_one, axis=-1, keepdims=True)
     )
-    grad_pair = grad_pair.reshape(4, 2, wide, 2, depth, hidden).transpose(3, 2, 0, 4, 1, 5)
-    grad_pair = grad_pair.reshape(2, wide, devices * hidden).astype(F32)
-    sums = add(out_near, out_got).reshape(2, 2, rows, width)
-    sums = sums[:, 0, :, :half], sums[:, 1, :, :half], sums[0, :, :, half:], sums[1, :, :, half:]
-    key_y, query_y, value_x, back, grad_inputs, share_gate, share_up, *sums = together(
-        key_y, query_y, value_x, back, grad_inputs, grad_pair[0], grad_pair[1], *sums
-    )
-
-    shares = jnp.concatenate(
-        [add(key_home, key_y), add(value_home[0], value_x), add(query_home, query_y)], axis=1
-    )
-    shares = lax.psum_scatter(shares, "z", scatter_dimension=0, tiled=True)[0].astype(F32)
-    sum_y, sum_x = swap(sums[1], "y"), swap(sums[3], "x")
-    back = add(grad_halo[:, 0], back)
-    sum_y, sum_x, back = together(sum_y, sum_x, back)
+    query_y, value_x, back, sum_y, sum_x, share_gate, share_up, grad_inputs = together(
+        query_y, value_x, back, sum_y, sum_x, grad_pair[0], grad_pair[1], grad_inputs
+    )
+
+    shares = jnp.concatenate([add(value_home[0], value_x), add(query_home, query_y)], axis=1)
+    shares = lax.psum_scatter(shares, "z", scatter_dimension=0, tiled=True)
     sums = reduce_last(sums[0], sum_y, sums[2], sum_x)
-    back_y = swap(back[1], "y")
-    sum_x, sum_y = together(swap(sums[1], "x"), swap(sums[3], "y"))
-    grad_kv_input = back[0].astype(F32) + back_y.astype(F32)
+    sum_x, sum_y, back_y = swap(sums[1], "x"), swap(sums[3], "y"), swap(back[rows:], "y")
+    sum_x, sum_y = together(sum_x, sum_y)
+    grad_kv_input = back[:rows].astype(F32) + back_y.astype(F32)
     result = middle + reduce_done(sums[0], sum_x, sums[2], sum_y)
     valid = valid_mask.astype(F32)
     squares_out = jnp.sum(result * result, axis=-1)
@@ -758,9 +784,8 @@
         axis=1,
     )
     tiny = lax.all_to_all(tiny, ALL, 0, 0, tiled=True)
-    share_key, share_value, share_query = (
-        shares[i * wide : (i + 1) * wide] for i in range(3)
-    )
+    share_key, share_out = shares_first[0, :wide].astype(F32), shares_first[0, wide:].astype(F32)
+    share_value, share_query = shares[0, :wide].astype(F32), shares[0, wide:].astype(F32)
 
     tiny = jnp.sum(tiny, axis=0)
     divisor = tiny[2 * wide + 3] * width

time: 946 us -> 933 us (0.986)
  local copies, waits for them, and re-layouts: 137 us -> 123 us
  starting transfers between devices: 81.9 us -> 71.1 us
    all_gather x1, waiting for transfers between devices: 107 us -> 70.2 us  [shards(): weights = lax.all_gather(weights, ALL, axis=0, tiled=True)]
    all_to_all x1, waiting for transfers between devices: 36.8 us -> 1.42 us  [shards(): grad_pair = lax.all_to_all(grad_pair, GROUP, 0, 0, tiled=True)]
    ppermute x34, waiting for transfers between devices: 107 us -> 141 us  [swap(): lax.ppermute(a, axis, [(i, i ^ step) for i in range(lax.axis_size(axis))])]
    all_to_all x1, starting transfers between devices: 19.1 us -> 2.57 us  [shards(): lax.all_to_all(jnp.broadcast_to(small[None], (devices, small.shape[0])),...]
    optimization_barrier x11 -> x5, local copies, waits for them, and re-layouts: 20.3 us -> 4.76 us  [together(): return lax.optimization_barrier(values)]
    ppermute x4, waiting for transfers between devices: 36.3 us -> 51.7 us  [shift(): lax.ppermute(a, axis, [(i, i + step) for i in range(n) if 0 <= i + step <...]
    all_to_all x1, waiting for transfers between devices: 13.7 us -> 25.3 us  [shards(): pair = lax.all_to_all(pair, GROUP, 0, 0, tiled=True)]
    reduce_scatter x1, starting transfers between devices: 0.04 us -> 10.6 us  [shards(): lax.psum_scatter(grad_pair, 'z', scatter_dimension=0, tiled=True)]
  transfers between devices with their start and end apart: 49 -> 49, of which waited for: 25 -> 30; matrix products, arithmetic and copies ran while one was open for 18% -> 18% of each run, Pallas kernels for 26% -> 28%
where the time goes in v3:
time: 933 us; the launch traced here: 922 us
  waiting for transfers between devices  344 us (37%)
  Pallas kernels  281 us (30%)
  local copies, waits for them, and re-layouts  123 us (13%)
  other arithmetic  81.3 us (9%)
  starting transfers between devices  71.1 us (8%)
  between operations  21.9 us (2%)
    ppermute x34, waiting for transfers between devices, swap(): lax.ppermute(a, axis, [(i, i ^ step) for i in range(lax.axis_size(axis))])  141 us
    all_gather x1, waiting for transfers between devices, shards(): weights = lax.all_gather(weights, ALL, axis=0, tiled=True)  70.2 us
    pallas_call x2, Pallas kernels, feed(): pl.pallas_call(functools.partial(feed_kernel, spans=level_spans(width, de...  54.2 us
    pallas_call x8, Pallas kernels, weight_grad(): pl.pallas_call(functools.partial(weight_grad_kernel, parts=parts), grid=(...  52.2 us
    pallas_call x4, Pallas kernels, project_back(): pl.pallas_call(functools.partial(project_back_kernel, count=count), grid=...  52 us
    ppermute x4, waiting for transfers between devices, shift(): lax.ppermute(a, axis, [(i, i + step) for i in range(n) if 0 <= i + step <...  51.7 us
    unnamed x172, local copies, waits for them, and re-layouts  45.8 us
    pallas_call x3, Pallas kernels, project(): pl.pallas_call(project_kernel, grid=(cols // tile,), in_specs=[pl.BlockSp...  44.2 us
  transfers between devices with their start and end apart: 49, of which 30 were waited for; matrix products, arithmetic and copies ran while one was open for 18% of the time, Pallas kernels for 28%

profile of v3, /device:TPU:0, one launch (start us, length us, event | category | flops | bytes accessed | tf_op | source)
XLA Modules:
  0.0 922.5 jit_solution(18076762268326845826)
XLA Ops:
  31.3 19.8 %collective-permute-done.refs_2_ = bf16[256,2048]{1,0:T(8,128)(2,1)} collective-permute-done((bf16[256,2048]{1,0:T(8,128)(2,1)}, bf16[256,2048]{1,0:T(8,128)(2,1)}, u32[]{:S(2)}, u32[]{:S(2)}) %collective-permute-start) | collective-permute-done | bytes 1048608 | tf_op jit(solution)/shard_map/ppermute | solution.py:39
  51.1 22.3 %collective-permute-done.2 = bf16[256,2048]{1,0:T(8,128)(2,1)} collective-permute-done((bf16[256,2048]{1,0:T(8,128)(2,1)S(1)}, bf16[256,2048]{1,0:T(8,128)(2,1)}, u32[]{:S(2)}, u32[]{:S(2)}) %collective-permute-start.2) | collective-permute-done | bytes 1048608 | tf_op jit(solution)/shard_map/ppermute | solution.py:34
  88.7 25.3 %all-to-all-done = bf16[8,128,688]{1,2,0:T(8,128)(2,1)S(1)} async-done(((bf16[8,128,688]{1,2,0:T(8,128)(2,1)}), bf16[8,128,688]{1,2,0:T(8,128)(2,1)S(1)}, u32[]{:S(2)}, u32[]{:S(2)}) %all-to-all-start) | async-done | bytes 1409056 | tf_op jit(solution)/shard_map/all_to_all | solution.py:566
  139.0 15.9 %collective-permute-done.5.refs_5_ = bf16[256,2048]{1,0:T(8,128)(2,1)} collective-permute-done((bf16[256,2048]{1,0:T(8,128)(2,1)}, bf16[256,2048]{1,0:T(8,128)(2,1)}, u32[]{:S(2)}, u32[]{:S(2)}) %collective-permute-start.5) | collective-permute-done | bytes 1048608 | tf_op jit(solution)/shard_map/ppermute | solution.py:34
  183.7 70.2 %all-gather.7.cloned.1.call-done.refs_1_.refs_2_.refs_3_ = bf16[2048,8192]{1,0:T(8,128)(2,1)} async-done(((bf16[64,8192]{1,0:T(8,128)(2,1)}), bf16[2048,8192]{1,0:T(8,128)(2,1)}) %all-gather.7.cloned.1.call-update) | async-done | bytes 33554448 | tf_op jit(solution)/shard_map/all_gather | solution.py:549
  265.6 32.9 %project.4.k_ref.v_ref = bf16[1536,4096]{1,0:T(8,128)(2,1)} custom-call(bf16[1536,2048]{1,0:T(8,128)(2,1)} %join.1.refs_0_, bf16[2048,8192]{1,0:T(8,128)(2,1)} %all-gather.7.cloned.1.call-done.refs_1_.refs_2_.refs_3_), custom_call_target="tpu_custom_call" | custom-call | flops 25769803776 | bytes 35651584 | tf_op jit(solution)/shard_map/project/pallas_call | solution.py:166
  302.8 15.9 %attend_forward.1 = (f32[256,2048]{1,0:T(8,128)S(1)}, bf16[256,2048]{1,0:T(8,128)(2,1)S(1)}) custom-call(s32[256,8]{1,0:T(8,128)S(1)} %copy.78.query_ref, s32[8,1536]{1,0:T(8,128)S(1)} %stack.96.key_ref, bf16[256,2048]{1,0:T(8,128)(2,1)S(1)} %project.3.q_ref, bf16[1536,4096]{1,0:T(8,128)(2,1)} %project.4.k_ref.v_ref, bf16[1536,4096]{1,0:T(8,128)(2,1)} %project.4.k_ref.v_ref), custom_call_target="tpu_custom_call" | custom-call | flops 3221225472 | bytes 16777216 | tf_op jit(solution)/shard_map/attend_forward/pallas_call | solution.py:453
  334.1 11.1 %collective-permute-done.7 = bf16[256,1024]{1,0:T(8,128)(2,1)S(1)} collective-permute-done((bf16[256,1024]{1,0:T(8,128)(2,1)S(1)}, bf16[256,1024]{1,0:T(8,128)(2,1)S(1)}, u32[]{:S(2)}, u32[]{:S(2)}) %collective-permute-start.7) | collective-permute-done | bytes 524320 | tf_op jit(solution)/shard_map/ppermute | solution.py:34
  347.5 14.6 %all-gather.9.cloned.1.call-done = bf16[5504,512]{1,0:T(8,128)(2,1)} async-done(((bf16[1376,512]{1,0:T(8,128)(2,1)}), bf16[5504,512]{1,0:T(8,128)(2,1)}) %all-gather.9.cloned.1.call-update) | async-done | bytes 5636112 | tf_op jit(solution)/shard_map/all_gather | solution.py:613
  369.8 10.6 %reduce-scatter.5.cloned.1.call-start = ((), (), s32[]{:S(2)}) async-start(), calls=%async_computation.9 | async-start | bytes 7045120 | tf_op jit(solution)/shard_map/reduce_scatter | solution.py:663
  380.4 9.7 %collective-permute-done.10 = bf16[2,256,1024]{2,1,0:T(8,128)(2,1)} collective-permute-done((bf16[2,256,1024]{2,1,0:T(8,128)(2,1)}, bf16[2,256,1024]{2,1,0:T(8,128)(2,1)}, u32[]{:S(2)}, u32[]{:S(2)}) %collective-permute-start.10) | collective-permute-done | bytes 1048608 | tf_op jit(solution)/shard_map/ppermute | solution.py:34
  396.3 29.3 %all-gather.11.cloned.1.call-done = bf16[4,172,2048]{2,1,0:T(8,128)(2,1)} async-done(((bf16[1,172,2048]{2,1,0:T(8,128)(2,1)}), bf16[4,172,2048]{2,1,0:T(8,128)(2,1)}) %all-gather.11.cloned.1.call-update) | async-done | bytes 2818064 | tf_op jit(solution)/shard_map/all_gather | solution.py:635
  428.8 25.8 %feed.1 = (bf16[1024,2048]{1,0:T(8,128)(2,1)}, bf16[1024,2048]{1,0:T(8,128)(2,1)}, bf16[688,1024]{1,0:T(8,128)(2,1)}, bf16[1376,1024]{1,0:T(8,128)(2,1)}) custom-call(bf16[1024,2048]{1,0:T(8,128)(2,1)} %collective-permute-done.12.x_ref.refs_4_, bf16[1024,2048]{1,0:T(8,128)(2,1)} %collective-permute-done.9.cot_ref.refs_5_, bf16[4,1376,512]{2,1,0:T(8,128)(2,1)} %bitcast.193, ...), custom_call_target="tpu_custom_call" | custom-call | flops 17314086912 | bytes 29458432 | tf_op jit(solution)/shard_map/feed/pallas_call | solution.py:298
  462.1 28.4 %feed_sum.1 = (bf16[1024,2048]{1,0:T(8,128)(2,1)}, bf16[688,1024]{1,0:T(8,128)(2,1)}, bf16[1376,1024]{1,0:T(8,128)(2,1)}, bf16[2,256,1024]{2,1,0:T(8,128)(2,1)},...) custom-call(bf16[1024,2048]{1,0:T(8,128)(2,1)} %bitcast.35.x_ref.refs_0_, ...), custom_call_target="tpu_custom_call" | custom-call | flops 17314086912 | bytes 29458432 | tf_op jit(solution)/shard_map/feed_sum/pallas_call | solution.py:298
  494.8 23.5 %feed_weights.1 = (bf16[4,1376,512]{2,1,0:T(8,128)(2,1)}, bf16[4,172,2048]{2,1,0:T(8,128)(2,1)}) custom-call(bf16[1024,2048]{1,0:T(8,128)(2,1)} %bitcast.35.x_ref.refs_0_, bf16[1024,2048]{1,0:T(8,128)(2,1)} %copy-done.55, bf16[688,1024]{1,0:T(8,128)(2,1)S(1)} %copy-done.22, bf16[1376,1024]{1,0:T(8,128)(2,1)} %get-tuple-element.205.refs_3_, ...), custom_call_target="tpu_custom_call" | custom-call | flops 17314086912 | bytes 33685504 | tf_op jit(solution)/shard_map/feed_weights/pallas_call | solution.py:351
  522.1 12.5 %collective-permute-done.18 = bf16[256,1024]{1,0:T(8,128)(2,1)} collective-permute-done((bf16[256,1024]{1,0:T(8,128)(2,1)}, bf16[256,1024]{1,0:T(8,128)(2,1)}, u32[]{:S(2)}, u32[]{:S(2)}) %collective-permute-start.18) | collective-permute-done | bytes 524320 | tf_op jit(solution)/shard_map/ppermute | solution.py:34
  558.8 25.8 %attend_backward.1 = (bf16[256,2048]{1,0:T(8,128)(2,1)S(1)}, bf16[1536,2048]{1,0:T(8,128)(2,1)}, bf16[1536,2048]{1,0:T(8,128)(2,1)}) custom-call(s32[256,8]{1,0:T(8,128)S(1)} %copy.78.query_ref, s32[8,1536]{1,0:T(8,128)S(1)} %stack.96.key_ref, bf16[256,2048]{1,0:T(8,128)(2,1)S(1)} %project.3.q_ref, bf16[1536,4096]{1,0:T(8,128)(2,1)} %project.4.k_ref.v_ref, ...), custom_call_target="tpu_custom_call" | custom-call | flops 8053063680 | bytes 31457280 | tf_op jit(solution)/shard_map/attend_backward/pallas_call | solution.py:483
  626.9 9.7 %weight_grad.12 = (bf16[512,2048]{1,0:T(8,128)(2,1)S(1)}, bf16[512,2048]{1,0:T(8,128)(2,1)}) custom-call(bf16[1024,1536]{1,0:T(8,128)(2,1)S(1)} %copy-done.7, bf16[1536,2048]{1,0:T(8,128)(2,1)} %get-tuple-element.255.refs_1_.refs_0_, bf16[1024,2048]{1,0:T(8,128)(2,1)S(1)} %copy-done.18), custom_call_target="tpu_custom_call" | custom-call | flops 6442450944 | bytes 17825792 | tf_op jit(solution)/shard_map/weight_grad/pallas_call | solution.py:117
  657.9 14.0 %project_back.6 = bf16[512,2048]{1,0:T(8,128)(2,1)} custom-call(bf16[1536,2048]{1,0:T(8,128)(2,1)} %get-tuple-element.255.refs_1_.refs_0_, bf16[1536,2048]{1,0:T(8,128)(2,1)} %get-tuple-element.256.refs_1_, bf16[2048,8192]{1,0:T(8,128)(2,1)} %all-gather.7.cloned.1.call-done.refs_1_.refs_2_.refs_3_, ...), custom_call_target="tpu_custom_call" | custom-call | flops 8589934592 | bytes 25165824 | tf_op jit(solution)/shard_map/project_back/pallas_call | solution.py:197
  694.3 24.0 %project_back.5 = bf16[1024,2048]{1,0:T(8,128)(2,1)} custom-call(bf16[1536,2048]{1,0:T(8,128)(2,1)} %get-tuple-element.255.refs_1_.refs_0_, bf16[1536,2048]{1,0:T(8,128)(2,1)} %get-tuple-element.256.refs_1_, bf16[2048,8192]{1,0:T(8,128)(2,1)} %all-gather.7.cloned.1.call-done.refs_1_.refs_2_.refs_3_, ...), custom_call_target="tpu_custom_call" | custom-call | flops 17179869184 | bytes 33554432 | tf_op jit(solution)/shard_map/project_back/pallas_call | solution.py:197
  719.8 18.8 %collective-permute-done.26 = bf16[512,2048]{1,0:T(8,128)(2,1)} collective-permute-done((bf16[512,2048]{1,0:T(8,128)(2,1)}, bf16[512,2048]{1,0:T(8,128)(2,1)}, u32[]{:S(2)}, u32[]{:S(2)}) %collective-permute-start.26) | collective-permute-done | bytes 2097184 | tf_op jit(solution)/shard_map/ppermute | solution.py:39
  768.7 17.7 %collective-permute-done.27 = bf16[512,2048]{1,0:T(8,128)(2,1)} collective-permute-done((bf16[512,2048]{1,0:T(8,128)(2,1)}, bf16[512,2048]{1,0:T(8,128)(2,1)}, u32[]{:S(2)}, u32[]{:S(2)}) %collective-permute-start.27) | collective-permute-done | bytes 2097184 | tf_op jit(solution)/shard_map/ppermute | solution.py:34
  786.4 11.6 %collective-permute-done.30 = bf16[512,2048]{1,0:T(8,128)(2,1)} collective-permute-done((bf16[512,2048]{1,0:T(8,128)(2,1)}, bf16[512,2048]{1,0:T(8,128)(2,1)}, u32[]{:S(2)}, u32[]{:S(2)}) %collective-permute-start.30) | collective-permute-done | bytes 2097184 | tf_op jit(solution)/shard_map/ppermute | solution.py:39
  869.7 11.7 %collective-permute-done.36 = bf16[256,1024]{1,0:T(8,128)(2,1)} collective-permute-done((bf16[256,1024]{1,0:T(8,128)(2,1)}, bf16[256,1024]{1,0:T(8,128)(2,1)}, u32[]{:S(2)}, u32[]{:S(2)}) %collective-permute-start.36) | collective-permute-done | bytes 524320 | tf_op jit(solution)/shard_map/ppermute | solution.py:34
  (409 shorter events, 399.4 us)
Async XLA Ops:
  7.2 246.7 %all-gather.7.cloned.1.call-start = ((), (), s32[]{:S(2)}) async-start(), calls=%async_computation.8 | async-start | bytes 34603008 | tf_op jit(solution)/shard_map/all_gather | solution.py:549
  9.6 41.5 %collective-permute-start = (bf16[256,2048]{1,0:T(8,128)(2,1)}, bf16[256,2048]{1,0:T(8,128)(2,1)}, u32[]{:S(2)}, u32[]{:S(2)}) collective-permute-start(bf16[256,2048]{1,0:T(8,128)(2,1)} %refs_0_), channel_id=1, source_target_pairs={{0,2},{2,4},{4,6},{1,3},{3,5},{5,7},{8,10},{10,12},{12,14},{9,11},... | collective-permute-start | bytes 3145736 | tf_op jit(solution)/shard_map/ppermute | solution.py:39
  17.1 56.2 %collective-permute-start.2 = (bf16[256,2048]{1,0:T(8,128)(2,1)S(1)}, bf16[256,2048]{1,0:T(8,128)(2,1)}, u32[]{:S(2)}, u32[]{:S(2)}) collective-permute-start(bf16[256,2048]{1,0:T(8,128)(2,1)S(1)} %copy-done.46), channel_id=1, source_target_pairs={{0,1},{1,0},{2,3},{3,2},{4,5},{5,4},{6,7},{7,6},{8,9},{9,8},{10,11... | collective-permute-start | bytes 3145736 | tf_op jit(solution)/shard_map/ppermute | solution.py:34
  75.9 38.1 %all-to-all-start = ((bf16[8,128,688]{1,2,0:T(8,128)(2,1)}), bf16[8,128,688]{1,2,0:T(8,128)(2,1)S(1)}, u32[]{:S(2)}, u32[]{:S(2)}) async-start(bf16[8,128,688]{1,2,0:T(8,128)(2,1)} %copy.70), calls=%async_computation | async-start | bytes 2818048 | tf_op jit(solution)/shard_map/all_to_all | solution.py:566
  80.6 42.8 %collective-permute-start.3 = (bf16[256,2048]{1,0:T(8,128)(2,1)}, bf16[256,2048]{1,0:T(8,128)(2,1)}, u32[]{:S(2)}, u32[]{:S(2)}) collective-permute-start(bf16[256,2048]{1,0:T(8,128)(2,1)} %collective-permute-done.refs_2_), channel_id=1, source_target_pairs={{0,1},{1,0},{2,3},{3,2},{4,5},{5,4},{6,7},{7,6},{8,9},{9,8},{10,11... | collective-permute-start | bytes 3145736 | tf_op jit(solution)/shard_map/ppermute | solution.py:34
  82.7 42.2 %collective-permute-start.4 = (bf16[256,2048]{1,0:T(8,128)(2,1)}, bf16[256,2048]{1,0:T(8,128)(2,1)}, u32[]{:S(2)}, u32[]{:S(2)}) collective-permute-start(bf16[256,2048]{1,0:T(8,128)(2,1)} %collective-permute-done.refs_2_), channel_id=1, source_target_pairs={{0,2},{2,4},{4,6},{1,3},{3,5},{5,7},{8,10},{10,12},{12,14},{9,11},... | collective-permute-start | bytes 3145736 | tf_op jit(solution)/shard_map/ppermute | solution.py:39
  117.3 244.7 %all-gather.9.cloned.1.call-start = ((), (), s32[]{:S(2)}) async-start(), calls=%async_computation.13 | async-start | bytes 7045120 | tf_op jit(solution)/shard_map/all_gather | solution.py:613
  253.9 48.9 %collective-permute-start.6 = (bf16[512,2048]{1,0:T(8,128)(2,1)}, bf16[512,2048]{1,0:T(8,128)(2,1)}, u32[]{:S(2)}, u32[]{:S(2)}) collective-permute-start(bf16[512,2048]{1,0:T(8,128)(2,1)} %pad_maximum_fusion.1), channel_id=1, source_target_pairs={{0,16},{16,0},{1,17},{17,1},{2,18},{18,2},{3,19},{19,3},{4,20},{20... | collective-permute-start | bytes 6291464 | tf_op jit(solution)/shard_map/ppermute | solution.py:34
  259.8 165.8 %all-gather.11.cloned.1.call-start = ((), (), s32[]{:S(2)}) async-start(), calls=%async_computation.14 | async-start | bytes 3604480 | tf_op jit(solution)/shard_map/all_gather | solution.py:635
  369.8 251.3 %reduce-scatter.5.cloned.1.call-start = ((), (), s32[]{:S(2)}) async-start(), calls=%async_computation.9 | async-start | bytes 7045120 | tf_op jit(solution)/shard_map/reduce_scatter | solution.py:663
  454.6 66.2 %collective-permute-start.16 = (bf16[1024,2048]{1,0:T(8,128)(2,1)}, bf16[1024,2048]{1,0:T(8,128)(2,1)}, u32[]{:S(2)}, u32[]{:S(2)}) collective-permute-start(bf16[1024,2048]{1,0:T(8,128)(2,1)} %get-tuple-element.211), channel_id=1, source_target_pairs={{0,8},{8,0},{1,9},{9,1},{2,10},{10,2},{3,11},{11,3},{4,12},{12,4},... | collective-permute-start | bytes 12582920 | tf_op jit(solution)/shard_map/ppermute | solution.py:34
  522.0 196.3 %reduce-scatter.7.cloned.1.call-start = ((), (), s32[]{:S(2)}) async-start(), calls=%async_computation.10 | async-start | bytes 3604480 | tf_op jit(solution)/shard_map/reduce_scatter | solution.py:664
  558.3 48.0 %collective-permute-start.20 = (bf16[512,2048]{1,0:T(8,128)(2,1)}, bf16[512,2048]{1,0:T(8,128)(2,1)}, u32[]{:S(2)}, u32[]{:S(2)}) collective-permute-start(bf16[512,2048]{1,0:T(8,128)(2,1)} %get-tuple-element.220), channel_id=1, source_target_pairs={{0,16},{16,0},{1,17},{17,1},{2,18},{18,2},{3,19},{19,3},{4,20},{20... | collective-permute-start | bytes 6291464 | tf_op jit(solution)/shard_map/ppermute | solution.py:34
  653.6 66.2 %collective-permute-start.24 = (bf16[512,2048]{1,0:T(8,128)(2,1)}, bf16[512,2048]{1,0:T(8,128)(2,1)}, u32[]{:S(2)}, u32[]{:S(2)}) collective-permute-start(bf16[512,2048]{1,0:T(8,128)(2,1)} %get-tuple-element.248), channel_id=1, source_target_pairs={{0,16},{16,0},{1,17},{17,1},{2,18},{18,2},{3,19},{19,3},{4,20},{20... | collective-permute-start | bytes 6291464 | tf_op jit(solution)/shard_map/ppermute | solution.py:34
  656.5 63.3 %collective-permute-start.25 = (bf16[2,4,64,2048]{3,2,1,0:T(8,128)(2,1)}, bf16[2,4,64,2048]{3,2,1,0:T(8,128)(2,1)}, u32[]{:S(2)}, u32[]{:S(2)}) collective-permute-start(bf16[2,4,64,2048]{3,2,1,0:T(8,128)(2,1)} %dynamic-slice_bitcast_fusion), channel_id=1, source_target_pairs={{0,1},{1,0},{2,3},{3,2},{4,5},{5,4},{6,7},{7,6},{8,9},{9,8},{10,11... | collective-permute-start | bytes 6291464 | tf_op jit(solution)/shard_map/ppermute | solution.py:34
  672.0 66.6 %collective-permute-start.26 = (bf16[512,2048]{1,0:T(8,128)(2,1)}, bf16[512,2048]{1,0:T(8,128)(2,1)}, u32[]{:S(2)}, u32[]{:S(2)}) collective-permute-start(bf16[512,2048]{1,0:T(8,128)(2,1)} %project_back.6), channel_id=1, source_target_pairs={{2,0},{4,2},{6,4},{3,1},{5,3},{7,5},{10,8},{12,10},{14,12},{11,9},... | collective-permute-start | bytes 6291464 | tf_op jit(solution)/shard_map/ppermute | solution.py:39
  681.1 38.7 %all-to-all-start.2 = ((bf16[8,64,1376]{2,1,0:T(8,128)(2,1)}), bf16[8,64,1376]{2,1,0:T(8,128)(2,1)}, u32[]{:S(2)}, u32[]{:S(2)}) async-start(bf16[8,64,1376]{2,1,0:T(8,128)(2,1)} %bitcast.170), calls=%async_computation.3 | async-start | bytes 2883584 | tf_op jit(solution)/shard_map/all_to_all | solution.py:718
  685.4 222.2 %reduce-scatter.11.cloned.1.call-start = ((), (), s32[]{:S(2)}) async-start(), calls=%async_computation.12 | async-start | bytes 2621440 | tf_op jit(solution)/shard_map/reduce_scatter | solution.py:745
  685.5 82.8 %collective-permute-start.29 = (bf16[4,64,2048]{2,1,0:T(8,128)(2,1)}, bf16[4,64,2048]{2,1,0:T(8,128)(2,1)}, u32[]{:S(2)}, u32[]{:S(2)}) collective-permute-start(bf16[4,64,2048]{2,1,0:T(8,128)(2,1)} %get-tuple-element.264), channel_id=1, source_target_pairs={{0,1},{1,0},{2,3},{3,2},{4,5},{5,4},{6,7},{7,6},{8,9},{9,8},{10,11... | collective-permute-start | bytes 3145736 | tf_op jit(solution)/shard_map/ppermute | solution.py:34
  738.6 47.8 %collective-permute-start.27 = (bf16[512,2048]{1,0:T(8,128)(2,1)}, bf16[512,2048]{1,0:T(8,128)(2,1)}, u32[]{:S(2)}, u32[]{:S(2)}) collective-permute-start(bf16[512,2048]{1,0:T(8,128)(2,1)} %copy-done.20), channel_id=1, source_target_pairs={{0,16},{16,0},{1,17},{17,1},{2,18},{18,2},{3,19},{19,3},{4,20},{20... | collective-permute-start | bytes 6291464 | tf_op jit(solution)/shard_map/ppermute | solution.py:34
  748.9 49.1 %collective-permute-start.30 = (bf16[512,2048]{1,0:T(8,128)(2,1)}, bf16[512,2048]{1,0:T(8,128)(2,1)}, u32[]{:S(2)}, u32[]{:S(2)}) collective-permute-start(bf16[512,2048]{1,0:T(8,128)(2,1)} %add_convert_fusion.3), channel_id=1, source_target_pairs={{2,0},{4,2},{6,4},{3,1},{5,3},{7,5},{10,8},{12,10},{14,12},{11,9},... | collective-permute-start | bytes 6291464 | tf_op jit(solution)/shard_map/ppermute | solution.py:39
  801.4 44.7 %collective-permute-start.31 = (bf16[4,64,2048]{2,1,0:T(8,128)(2,1)}, bf16[4,64,2048]{2,1,0:T(8,128)(2,1)}, u32[]{:S(2)}, u32[]{:S(2)}) collective-permute-start(bf16[4,64,2048]{2,1,0:T(8,128)(2,1)} %dynamic-slice_bitcast_fusion.1), channel_id=1, source_target_pairs={{0,1},{1,0},{2,3},{3,2},{4,5},{5,4},{6,7},{7,6},{8,9},{9,8},{10,11... | collective-permute-start | bytes 3145736 | tf_op jit(solution)/shard_map/ppermute | solution.py:34
  808.1 101.7 %reduce-scatter.9.cloned.1.call-start = ((), (), s32[]{:S(2)}) async-start(), calls=%async_computation.11 | async-start | bytes 2621440 | tf_op jit(solution)/shard_map/reduce_scatter | solution.py:762
  810.6 44.9 %collective-permute-start.34 = (bf16[2,256,1024]{2,1,0:T(8,128)(2,1)}, bf16[2,256,1024]{2,1,0:T(8,128)(2,1)}, u32[]{:S(2)}, u32[]{:S(2)}) collective-permute-start(bf16[2,256,1024]{2,1,0:T(8,128)(2,1)} %get-tuple-element.278), channel_id=1, source_target_pairs={{0,16},{16,0},{1,17},{17,1},{2,18},{18,2},{3,19},{19,3},{4,20},{20... | collective-permute-start | bytes 3145736 | tf_op jit(solution)/shard_map/ppermute | solution.py:34
  (100 other events, 1207.8 us)
Sparse Core Ops, SparseCore 0:
  11.6 242.2 all-gather.6
  259.9 102.1 all-gather.8
  369.9 55.6 all-gather.10
  522.2 98.8 reduce-scatter.4
  638.7 71.0 reduce-scatter.6
  808.2 42.2 reduce-scatter.10
  862.5 43.2 reduce-scatter.8

commit v4 on v3

--- a/solution.py
+++ b/solution.py
@@ -698,16 +698,13 @@
 
     got_value = swap(far_value, "core")
     key_home, key_away = weight_grad(halo_near, grad_keys, got_key, 2)
-    far_query = weight_grad(normed1_far, grad_queries)
-    got_value, key_home, key_away, far_query, grad_keys, grad_values, grad_queries = together(
-        got_value, key_home, key_away, far_query, grad_keys, grad_values, grad_queries
-    )
-
-    got_query = swap(far_query, "core")
+    got_value, key_home, key_away, grad_keys, grad_values, grad_queries = together(
+        got_value, key_home, key_away, grad_keys, grad_values, grad_queries
+    )
+
     value_near = weight_grad(halo_near, grad_values, got_value)
-    out_away, out_home = split_y(by_owner(add(out_home, out_x)))
-    got_query, value_near, key_away, out_away, out_home, grad_keys, grad_values = together(
-        got_query, value_near, key_away, out_away, out_home, grad_keys, grad_values
+    value_near, key_away, grad_keys, grad_values, grad_queries = together(
+        value_near, key_away, grad_keys, grad_values, grad_queries
     )
 
     key_x = swap(key_away, "x")
@@ -720,12 +717,14 @@
     back = project_back(halves, weights, [0, 1], BF16, reach, 2 * rows)
     back = shift(back, "z", -1)
     grad_halo = project_back(halves, weights, [0, 1], BF16, 0, reach * 2 * rows)
+    got_query = swap(weight_grad(normed1_far, grad_queries), "core")
     query_home, query_away = weight_grad(normed1_near, grad_queries, got_query, 2)
     key_x, value_y, query_home, query_away, grad_halo, back, grad_queries, *held = together(
         key_x, value_y, query_home, query_away, grad_halo, back, grad_queries, grad_pair, out_near, out_got,
-        grad_down,
-    )
-    grad_pair, out_near, out_got, grad_down = held
+        grad_down, out_home, out_x,
+    )
+    grad_pair, out_near, out_got, grad_down, out_home, out_x = held
+    out_away, out_home = split_y(by_owner(add(out_home, out_x)))
     share_down = grad_down.reshape(hidden, width).astype(F32)
 
     key_away, key_home = split_y(by_owner(add(key_home, key_x)))

time: 933 us -> 923 us (0.989)
  waiting for transfers between devices: 344 us -> 331 us
    ppermute x4, waiting for transfers between devices: 51.7 us -> 38 us  [shift(): lax.ppermute(a, axis, [(i, i + step) for i in range(n) if 0 <= i + step <...]
    unnamed x172 -> x178, local copies, waits for them, and re-layouts: 45.8 us -> 47.9 us
  transfers between devices with their start and end apart: 49 -> 49, of which waited for: 30 -> 28; matrix products, arithmetic and copies ran while one was open for 18% -> 18% of each run, Pallas kernels for 28% -> 28%
where the time goes in v4:
time: 923 us; the launch traced here: 912 us
  waiting for transfers between devices  331 us (36%)
  Pallas kernels  282 us (31%)
  local copies, waits for them, and re-layouts  126 us (14%)
  other arithmetic  81.4 us (9%)
  starting transfers between devices  70.5 us (8%)
  between operations  21.9 us (2%)
    ppermute x34, waiting for transfers between devices, swap(): lax.ppermute(a, axis, [(i, i ^ step) for i in range(lax.axis_size(axis))])  142 us
    all_gather x1, waiting for transfers between devices, shards(): weights = lax.all_gather(weights, ALL, axis=0, tiled=True)  70.1 us
    pallas_call x2, Pallas kernels, feed(): pl.pallas_call(functools.partial(feed_kernel, spans=level_spans(width, de...  54.2 us
    pallas_call x8, Pallas kernels, weight_grad(): pl.pallas_call(functools.partial(weight_grad_kernel, parts=parts), grid=(...  52.5 us
    pallas_call x4, Pallas kernels, project_back(): pl.pallas_call(functools.partial(project_back_kernel, count=count), grid=...  51.9 us
    unnamed x178, local copies, waits for them, and re-layouts  47.9 us
    pallas_call x3, Pallas kernels, project(): pl.pallas_call(project_kernel, grid=(cols // tile,), in_specs=[pl.BlockSp...  44.3 us
    ppermute x4, waiting for transfers between devices, shift(): lax.ppermute(a, axis, [(i, i + step) for i in range(n) if 0 <= i + step <...  38 us
  transfers between devices with their start and end apart: 49, of which 28 were waited for; matrix products, arithmetic and copies ran while one was open for 18% of the time, Pallas kernels for 28%

profile of v4, /device:TPU:0, one launch (start us, length us, event | category | flops | bytes accessed | tf_op | source)
XLA Modules:
  0.0 912.4 jit_solution(7932322983179966910)
XLA Ops:
  31.3 19.8 %collective-permute-done.refs_2_ = bf16[256,2048]{1,0:T(8,128)(2,1)} collective-permute-done((bf16[256,2048]{1,0:T(8,128)(2,1)}, bf16[256,2048]{1,0:T(8,128)(2,1)}, u32[]{:S(2)}, u32[]{:S(2)}) %collective-permute-start) | collective-permute-done | bytes 1048608 | tf_op jit(solution)/shard_map/ppermute | solution.py:39
  51.1 22.3 %collective-permute-done.2 = bf16[256,2048]{1,0:T(8,128)(2,1)} collective-permute-done((bf16[256,2048]{1,0:T(8,128)(2,1)S(1)}, bf16[256,2048]{1,0:T(8,128)(2,1)}, u32[]{:S(2)}, u32[]{:S(2)}) %collective-permute-start.2) | collective-permute-done | bytes 1048608 | tf_op jit(solution)/shard_map/ppermute | solution.py:34
  88.7 25.3 %all-to-all-done = bf16[8,128,688]{1,2,0:T(8,128)(2,1)S(1)} async-done(((bf16[8,128,688]{1,2,0:T(8,128)(2,1)}), bf16[8,128,688]{1,2,0:T(8,128)(2,1)S(1)}, u32[]{:S(2)}, u32[]{:S(2)}) %all-to-all-start) | async-done | bytes 1409056 | tf_op jit(solution)/shard_map/all_to_all | solution.py:566
  139.0 16.0 %collective-permute-done.5.refs_5_ = bf16[256,2048]{1,0:T(8,128)(2,1)} collective-permute-done((bf16[256,2048]{1,0:T(8,128)(2,1)}, bf16[256,2048]{1,0:T(8,128)(2,1)}, u32[]{:S(2)}, u32[]{:S(2)}) %collective-permute-start.5) | collective-permute-done | bytes 1048608 | tf_op jit(solution)/shard_map/ppermute | solution.py:34
  183.8 70.1 %all-gather.7.cloned.1.call-done.refs_1_.refs_2_.refs_3_ = bf16[2048,8192]{1,0:T(8,128)(2,1)} async-done(((bf16[64,8192]{1,0:T(8,128)(2,1)}), bf16[2048,8192]{1,0:T(8,128)(2,1)}) %all-gather.7.cloned.1.call-update) | async-done | bytes 33554448 | tf_op jit(solution)/shard_map/all_gather | solution.py:549
  265.6 32.9 %project.4.k_ref.v_ref = bf16[1536,4096]{1,0:T(8,128)(2,1)} custom-call(bf16[1536,2048]{1,0:T(8,128)(2,1)} %join.1.refs_0_, bf16[2048,8192]{1,0:T(8,128)(2,1)} %all-gather.7.cloned.1.call-done.refs_1_.refs_2_.refs_3_), custom_call_target="tpu_custom_call" | custom-call | flops 25769803776 | bytes 35651584 | tf_op jit(solution)/shard_map/project/pallas_call | solution.py:166
  302.8 15.9 %attend_forward.1 = (f32[256,2048]{1,0:T(8,128)S(1)}, bf16[256,2048]{1,0:T(8,128)(2,1)S(1)}) custom-call(s32[256,8]{1,0:T(8,128)S(1)} %copy.80.query_ref, s32[8,1536]{1,0:T(8,128)S(1)} %stack.96.key_ref, bf16[256,2048]{1,0:T(8,128)(2,1)S(1)} %project.3.q_ref, bf16[1536,4096]{1,0:T(8,128)(2,1)} %project.4.k_ref.v_ref, bf16[1536,4096]{1,0:T(8,128)(2,1)} %project.4.k_ref.v_ref), custom_call_target="tpu_custom_call" | custom-call | flops 3221225472 | bytes 16777216 | tf_op jit(solution)/shard_map/attend_forward/pallas_call | solution.py:453
  334.1 11.1 %collective-permute-done.7 = bf16[256,1024]{1,0:T(8,128)(2,1)S(1)} collective-permute-done((bf16[256,1024]{1,0:T(8,128)(2,1)S(1)}, bf16[256,1024]{1,0:T(8,128)(2,1)S(1)}, u32[]{:S(2)}, u32[]{:S(2)}) %collective-permute-start.7) | collective-permute-done | bytes 524320 | tf_op jit(solution)/shard_map/ppermute | solution.py:34
  347.5 14.6 %all-gather.9.cloned.1.call-done = bf16[5504,512]{1,0:T(8,128)(2,1)} async-done(((bf16[1376,512]{1,0:T(8,128)(2,1)}), bf16[5504,512]{1,0:T(8,128)(2,1)}) %all-gather.9.cloned.1.call-update) | async-done | bytes 5636112 | tf_op jit(solution)/shard_map/all_gather | solution.py:613
  369.8 10.6 %reduce-scatter.5.cloned.1.call-start = ((), (), s32[]{:S(2)}) async-start(), calls=%async_computation.9 | async-start | bytes 7045120 | tf_op jit(solution)/shard_map/reduce_scatter | solution.py:663
  380.4 9.7 %collective-permute-done.10 = bf16[2,256,1024]{2,1,0:T(8,128)(2,1)} collective-permute-done((bf16[2,256,1024]{2,1,0:T(8,128)(2,1)}, bf16[2,256,1024]{2,1,0:T(8,128)(2,1)}, u32[]{:S(2)}, u32[]{:S(2)}) %collective-permute-start.10) | collective-permute-done | bytes 1048608 | tf_op jit(solution)/shard_map/ppermute | solution.py:34
  396.3 29.3 %all-gather.11.cloned.1.call-done = bf16[4,172,2048]{2,1,0:T(8,128)(2,1)} async-done(((bf16[1,172,2048]{2,1,0:T(8,128)(2,1)}), bf16[4,172,2048]{2,1,0:T(8,128)(2,1)}) %all-gather.11.cloned.1.call-update) | async-done | bytes 2818064 | tf_op jit(solution)/shard_map/all_gather | solution.py:635
  428.8 25.8 %feed.1 = (bf16[1024,2048]{1,0:T(8,128)(2,1)}, bf16[1024,2048]{1,0:T(8,128)(2,1)}, bf16[688,1024]{1,0:T(8,128)(2,1)}, bf16[1376,1024]{1,0:T(8,128)(2,1)}) custom-call(bf16[1024,2048]{1,0:T(8,128)(2,1)} %collective-permute-done.12.x_ref.refs_4_, bf16[1024,2048]{1,0:T(8,128)(2,1)} %collective-permute-done.9.cot_ref.refs_5_, bf16[4,1376,512]{2,1,0:T(8,128)(2,1)} %bitcast.197, ...), custom_call_target="tpu_custom_call" | custom-call | flops 17314086912 | bytes 29458432 | tf_op jit(solution)/shard_map/feed/pallas_call | solution.py:298
  462.1 28.4 %feed_sum.1 = (bf16[1024,2048]{1,0:T(8,128)(2,1)}, bf16[688,1024]{1,0:T(8,128)(2,1)}, bf16[1376,1024]{1,0:T(8,128)(2,1)}, bf16[2,256,1024]{2,1,0:T(8,128)(2,1)},...) custom-call(bf16[1024,2048]{1,0:T(8,128)(2,1)} %bitcast.35.x_ref.refs_0_, ...), custom_call_target="tpu_custom_call" | custom-call | flops 17314086912 | bytes 29458432 | tf_op jit(solution)/shard_map/feed_sum/pallas_call | solution.py:298
  494.8 23.5 %feed_weights.1 = (bf16[4,1376,512]{2,1,0:T(8,128)(2,1)}, bf16[4,172,2048]{2,1,0:T(8,128)(2,1)}) custom-call(bf16[1024,2048]{1,0:T(8,128)(2,1)} %bitcast.35.x_ref.refs_0_, bf16[1024,2048]{1,0:T(8,128)(2,1)} %copy-done.58, bf16[688,1024]{1,0:T(8,128)(2,1)S(1)} %copy-done.23, bf16[1376,1024]{1,0:T(8,128)(2,1)} %get-tuple-element.205.refs_3_, ...), custom_call_target="tpu_custom_call" | custom-call | flops 17314086912 | bytes 33685504 | tf_op jit(solution)/shard_map/feed_weights/pallas_call | solution.py:351
  522.1 12.5 %collective-permute-done.18 = bf16[256,1024]{1,0:T(8,128)(2,1)} collective-permute-done((bf16[256,1024]{1,0:T(8,128)(2,1)}, bf16[256,1024]{1,0:T(8,128)(2,1)}, u32[]{:S(2)}, u32[]{:S(2)}) %collective-permute-start.18) | collective-permute-done | bytes 524320 | tf_op jit(solution)/shard_map/ppermute | solution.py:34
  558.9 25.9 %attend_backward.1 = (bf16[256,2048]{1,0:T(8,128)(2,1)S(1)}, bf16[1536,2048]{1,0:T(8,128)(2,1)}, bf16[1536,2048]{1,0:T(8,128)(2,1)}) custom-call(s32[256,8]{1,0:T(8,128)S(1)} %copy.80.query_ref, s32[8,1536]{1,0:T(8,128)S(1)} %stack.96.key_ref, bf16[256,2048]{1,0:T(8,128)(2,1)S(1)} %project.3.q_ref, bf16[1536,4096]{1,0:T(8,128)(2,1)} %project.4.k_ref.v_ref, ...), custom_call_target="tpu_custom_call" | custom-call | flops 8053063680 | bytes 31457280 | tf_op jit(solution)/shard_map/attend_backward/pallas_call | solution.py:483
  596.7 9.7 %collective-permute-done.20 = bf16[512,2048]{1,0:T(8,128)(2,1)} collective-permute-done((bf16[512,2048]{1,0:T(8,128)(2,1)}, bf16[512,2048]{1,0:T(8,128)(2,1)}, u32[]{:S(2)}, u32[]{:S(2)}) %collective-permute-start.20) | collective-permute-done | bytes 2097184 | tf_op jit(solution)/shard_map/ppermute | solution.py:34
  635.9 10.0 %weight_grad.13 = bf16[1024,2048]{1,0:T(8,128)(2,1)S(1)} custom-call(bf16[1024,1536]{1,0:T(8,128)(2,1)S(1)} %copy-done.8, bf16[1536,2048]{1,0:T(8,128)(2,1)} %get-tuple-element.252.refs_1_, bf16[1024,2048]{1,0:T(8,128)(2,1)} %collective-permute-done.22.refs_2_), custom_call_target="tpu_custom_call" | custom-call | flops 6442450944 | bytes 17825792 | tf_op jit(solution)/shard_map/weight_grad/pallas_call | solution.py:117
  658.0 13.9 %project_back.6 = bf16[512,2048]{1,0:T(8,128)(2,1)} custom-call(bf16[1536,2048]{1,0:T(8,128)(2,1)} %get-tuple-element.251.refs_1_.refs_0_, bf16[1536,2048]{1,0:T(8,128)(2,1)} %get-tuple-element.252.refs_1_, bf16[2048,8192]{1,0:T(8,128)(2,1)} %all-gather.7.cloned.1.call-done.refs_1_.refs_2_.refs_3_, ...), custom_call_target="tpu_custom_call" | custom-call | flops 8589934592 | bytes 25165824 | tf_op jit(solution)/shard_map/project_back/pallas_call | solution.py:197
  685.3 24.1 %project_back.5 = bf16[1024,2048]{1,0:T(8,128)(2,1)} custom-call(bf16[1536,2048]{1,0:T(8,128)(2,1)} %get-tuple-element.251.refs_1_.refs_0_, bf16[1536,2048]{1,0:T(8,128)(2,1)} %get-tuple-element.252.refs_1_, bf16[2048,8192]{1,0:T(8,128)(2,1)} %all-gather.7.cloned.1.call-done.refs_1_.refs_2_.refs_3_, ...), custom_call_target="tpu_custom_call" | custom-call | flops 17179869184 | bytes 33554432 | tf_op jit(solution)/shard_map/project_back/pallas_call | solution.py:197
  758.3 17.6 %collective-permute-done.29 = bf16[4,64,2048]{2,1,0:T(8,128)(2,1)} collective-permute-done((bf16[4,64,2048]{2,1,0:T(8,128)(2,1)}, bf16[4,64,2048]{2,1,0:T(8,128)(2,1)}, u32[]{:S(2)}, u32[]{:S(2)}) %collective-permute-start.29) | collective-permute-done | bytes 1048608 | tf_op jit(solution)/shard_map/ppermute | solution.py:34
  775.9 12.1 %collective-permute-done.30 = bf16[512,2048]{1,0:T(8,128)(2,1)} collective-permute-done((bf16[512,2048]{1,0:T(8,128)(2,1)}, bf16[512,2048]{1,0:T(8,128)(2,1)}, u32[]{:S(2)}, u32[]{:S(2)}) %collective-permute-start.30) | collective-permute-done | bytes 2097184 | tf_op jit(solution)/shard_map/ppermute | solution.py:39
  859.4 11.6 %collective-permute-done.36 = bf16[256,1024]{1,0:T(8,128)(2,1)} collective-permute-done((bf16[256,1024]{1,0:T(8,128)(2,1)}, bf16[256,1024]{1,0:T(8,128)(2,1)}, u32[]{:S(2)}, u32[]{:S(2)}) %collective-permute-start.36) | collective-permute-done | bytes 524320 | tf_op jit(solution)/shard_map/ppermute | solution.py:34
  (415 shorter events, 397.7 us)
Async XLA Ops:
  7.2 246.7 %all-gather.7.cloned.1.call-start = ((), (), s32[]{:S(2)}) async-start(), calls=%async_computation.8 | async-start | bytes 34603008 | tf_op jit(solution)/shard_map/all_gather | solution.py:549
  9.6 41.5 %collective-permute-start = (bf16[256,2048]{1,0:T(8,128)(2,1)}, bf16[256,2048]{1,0:T(8,128)(2,1)}, u32[]{:S(2)}, u32[]{:S(2)}) collective-permute-start(bf16[256,2048]{1,0:T(8,128)(2,1)} %refs_0_), channel_id=1, source_target_pairs={{0,2},{2,4},{4,6},{1,3},{3,5},{5,7},{8,10},{10,12},{12,14},{9,11},... | collective-permute-start | bytes 3145736 | tf_op jit(solution)/shard_map/ppermute | solution.py:39
  17.1 56.3 %collective-permute-start.2 = (bf16[256,2048]{1,0:T(8,128)(2,1)S(1)}, bf16[256,2048]{1,0:T(8,128)(2,1)}, u32[]{:S(2)}, u32[]{:S(2)}) collective-permute-start(bf16[256,2048]{1,0:T(8,128)(2,1)S(1)} %copy-done.49), channel_id=1, source_target_pairs={{0,1},{1,0},{2,3},{3,2},{4,5},{5,4},{6,7},{7,6},{8,9},{9,8},{10,11... | collective-permute-start | bytes 3145736 | tf_op jit(solution)/shard_map/ppermute | solution.py:34
  75.9 38.1 %all-to-all-start = ((bf16[8,128,688]{1,2,0:T(8,128)(2,1)}), bf16[8,128,688]{1,2,0:T(8,128)(2,1)S(1)}, u32[]{:S(2)}, u32[]{:S(2)}) async-start(bf16[8,128,688]{1,2,0:T(8,128)(2,1)} %copy.72), calls=%async_computation | async-start | bytes 2818048 | tf_op jit(solution)/shard_map/all_to_all | solution.py:566
  80.7 42.8 %collective-permute-start.3 = (bf16[256,2048]{1,0:T(8,128)(2,1)}, bf16[256,2048]{1,0:T(8,128)(2,1)}, u32[]{:S(2)}, u32[]{:S(2)}) collective-permute-start(bf16[256,2048]{1,0:T(8,128)(2,1)} %collective-permute-done.refs_2_), channel_id=1, source_target_pairs={{0,1},{1,0},{2,3},{3,2},{4,5},{5,4},{6,7},{7,6},{8,9},{9,8},{10,11... | collective-permute-start | bytes 3145736 | tf_op jit(solution)/shard_map/ppermute | solution.py:34
  82.7 42.2 %collective-permute-start.4 = (bf16[256,2048]{1,0:T(8,128)(2,1)}, bf16[256,2048]{1,0:T(8,128)(2,1)}, u32[]{:S(2)}, u32[]{:S(2)}) collective-permute-start(bf16[256,2048]{1,0:T(8,128)(2,1)} %collective-permute-done.refs_2_), channel_id=1, source_target_pairs={{0,2},{2,4},{4,6},{1,3},{3,5},{5,7},{8,10},{10,12},{12,14},{9,11},... | collective-permute-start | bytes 3145736 | tf_op jit(solution)/shard_map/ppermute | solution.py:39
  117.3 244.7 %all-gather.9.cloned.1.call-start = ((), (), s32[]{:S(2)}) async-start(), calls=%async_computation.13 | async-start | bytes 7045120 | tf_op jit(solution)/shard_map/all_gather | solution.py:613
  253.9 48.9 %collective-permute-start.6 = (bf16[512,2048]{1,0:T(8,128)(2,1)}, bf16[512,2048]{1,0:T(8,128)(2,1)}, u32[]{:S(2)}, u32[]{:S(2)}) collective-permute-start(bf16[512,2048]{1,0:T(8,128)(2,1)} %pad_maximum_fusion.1), channel_id=1, source_target_pairs={{0,16},{16,0},{1,17},{17,1},{2,18},{18,2},{3,19},{19,3},{4,20},{20... | collective-permute-start | bytes 6291464 | tf_op jit(solution)/shard_map/ppermute | solution.py:34
  259.8 165.8 %all-gather.11.cloned.1.call-start = ((), (), s32[]{:S(2)}) async-start(), calls=%async_computation.14 | async-start | bytes 3604480 | tf_op jit(solution)/shard_map/all_gather | solution.py:635
  369.8 251.3 %reduce-scatter.5.cloned.1.call-start = ((), (), s32[]{:S(2)}) async-start(), calls=%async_computation.9 | async-start | bytes 7045120 | tf_op jit(solution)/shard_map/reduce_scatter | solution.py:663
  454.7 66.3 %collective-permute-start.16 = (bf16[1024,2048]{1,0:T(8,128)(2,1)}, bf16[1024,2048]{1,0:T(8,128)(2,1)}, u32[]{:S(2)}, u32[]{:S(2)}) collective-permute-start(bf16[1024,2048]{1,0:T(8,128)(2,1)} %get-tuple-element.211), channel_id=1, source_target_pairs={{0,8},{8,0},{1,9},{9,1},{2,10},{10,2},{3,11},{11,3},{4,12},{12,4},... | collective-permute-start | bytes 12582920 | tf_op jit(solution)/shard_map/ppermute | solution.py:34
  522.1 194.2 %reduce-scatter.7.cloned.1.call-start = ((), (), s32[]{:S(2)}) async-start(), calls=%async_computation.10 | async-start | bytes 3604480 | tf_op jit(solution)/shard_map/reduce_scatter | solution.py:664
  558.4 48.0 %collective-permute-start.20 = (bf16[512,2048]{1,0:T(8,128)(2,1)}, bf16[512,2048]{1,0:T(8,128)(2,1)}, u32[]{:S(2)}, u32[]{:S(2)}) collective-permute-start(bf16[512,2048]{1,0:T(8,128)(2,1)} %get-tuple-element.220), channel_id=1, source_target_pairs={{0,16},{16,0},{1,17},{17,1},{2,18},{18,2},{3,19},{19,3},{4,20},{20... | collective-permute-start | bytes 6291464 | tf_op jit(solution)/shard_map/ppermute | solution.py:34
  651.3 58.1 %collective-permute-start.25 = (bf16[1024,2048]{1,0:T(8,128)(2,1)}, bf16[1024,2048]{1,0:T(8,128)(2,1)}, u32[]{:S(2)}, u32[]{:S(2)}) collective-permute-start(bf16[1024,2048]{1,0:T(8,128)(2,1)} %weight_grad.14), channel_id=1, source_target_pairs={{0,8},{8,0},{1,9},{9,1},{2,10},{10,2},{3,11},{11,3},{4,12},{12,4},... | collective-permute-start | bytes 12582920 | tf_op jit(solution)/shard_map/ppermute | solution.py:34
  651.8 66.7 %collective-permute-start.23 = (bf16[512,2048]{1,0:T(8,128)(2,1)}, bf16[512,2048]{1,0:T(8,128)(2,1)}, u32[]{:S(2)}, u32[]{:S(2)}) collective-permute-start(bf16[512,2048]{1,0:T(8,128)(2,1)} %copy-done.20), channel_id=1, source_target_pairs={{0,16},{16,0},{1,17},{17,1},{2,18},{18,2},{3,19},{19,3},{4,20},{20... | collective-permute-start | bytes 6291464 | tf_op jit(solution)/shard_map/ppermute | solution.py:34
  656.5 62.0 %collective-permute-start.24 = (bf16[2,4,64,2048]{3,2,1,0:T(8,128)(2,1)}, bf16[2,4,64,2048]{3,2,1,0:T(8,128)(2,1)}, u32[]{:S(2)}, u32[]{:S(2)}) collective-permute-start(bf16[2,4,64,2048]{3,2,1,0:T(8,128)(2,1)} %dynamic-slice_bitcast_fusion), channel_id=1, source_target_pairs={{0,1},{1,0},{2,3},{3,2},{4,5},{5,4},{6,7},{7,6},{8,9},{9,8},{10,11... | collective-permute-start | bytes 6291464 | tf_op jit(solution)/shard_map/ppermute | solution.py:34
  671.9 51.2 %collective-permute-start.26 = (bf16[512,2048]{1,0:T(8,128)(2,1)}, bf16[512,2048]{1,0:T(8,128)(2,1)}, u32[]{:S(2)}, u32[]{:S(2)}) collective-permute-start(bf16[512,2048]{1,0:T(8,128)(2,1)} %project_back.6), channel_id=1, source_target_pairs={{2,0},{4,2},{6,4},{3,1},{5,3},{7,5},{10,8},{12,10},{14,12},{11,9},... | collective-permute-start | bytes 6291464 | tf_op jit(solution)/shard_map/ppermute | solution.py:39
  685.3 212.2 %reduce-scatter.11.cloned.1.call-start = ((), (), s32[]{:S(2)}) async-start(), calls=%async_computation.12 | async-start | bytes 2621440 | tf_op jit(solution)/shard_map/reduce_scatter | solution.py:744
  723.1 52.8 %collective-permute-start.27 = (bf16[512,2048]{1,0:T(8,128)(2,1)}, bf16[512,2048]{1,0:T(8,128)(2,1)}, u32[]{:S(2)}, u32[]{:S(2)}) collective-permute-start(bf16[512,2048]{1,0:T(8,128)(2,1)} %copy-done.21), channel_id=1, source_target_pairs={{0,16},{16,0},{1,17},{17,1},{2,18},{18,2},{3,19},{19,3},{4,20},{20... | collective-permute-start | bytes 6291464 | tf_op jit(solution)/shard_map/ppermute | solution.py:34
  734.0 41.8 %collective-permute-start.29 = (bf16[4,64,2048]{2,1,0:T(8,128)(2,1)}, bf16[4,64,2048]{2,1,0:T(8,128)(2,1)}, u32[]{:S(2)}, u32[]{:S(2)}) collective-permute-start(bf16[4,64,2048]{2,1,0:T(8,128)(2,1)} %dynamic-slice_bitcast_fusion.2), channel_id=1, source_target_pairs={{0,1},{1,0},{2,3},{3,2},{4,5},{5,4},{6,7},{7,6},{8,9},{9,8},{10,11... | collective-permute-start | bytes 3145736 | tf_op jit(solution)/shard_map/ppermute | solution.py:34
  739.0 49.0 %collective-permute-start.30 = (bf16[512,2048]{1,0:T(8,128)(2,1)}, bf16[512,2048]{1,0:T(8,128)(2,1)}, u32[]{:S(2)}, u32[]{:S(2)}) collective-permute-start(bf16[512,2048]{1,0:T(8,128)(2,1)} %add_convert_fusion.3), channel_id=1, source_target_pairs={{2,0},{4,2},{6,4},{3,1},{5,3},{7,5},{10,8},{12,10},{14,12},{11,9},... | collective-permute-start | bytes 6291464 | tf_op jit(solution)/shard_map/ppermute | solution.py:39
  791.5 44.5 %collective-permute-start.31 = (bf16[4,64,2048]{2,1,0:T(8,128)(2,1)}, bf16[4,64,2048]{2,1,0:T(8,128)(2,1)}, u32[]{:S(2)}, u32[]{:S(2)}) collective-permute-start(bf16[4,64,2048]{2,1,0:T(8,128)(2,1)} %dynamic-slice_bitcast_fusion.1), channel_id=1, source_target_pairs={{0,1},{1,0},{2,3},{3,2},{4,5},{5,4},{6,7},{7,6},{8,9},{9,8},{10,11... | collective-permute-start | bytes 3145736 | tf_op jit(solution)/shard_map/ppermute | solution.py:34
  798.0 101.6 %reduce-scatter.9.cloned.1.call-start = ((), (), s32[]{:S(2)}) async-start(), calls=%async_computation.11 | async-start | bytes 2621440 | tf_op jit(solution)/shard_map/reduce_scatter | solution.py:761
  800.4 45.0 %collective-permute-start.34 = (bf16[2,256,1024]{2,1,0:T(8,128)(2,1)}, bf16[2,256,1024]{2,1,0:T(8,128)(2,1)}, u32[]{:S(2)}, u32[]{:S(2)}) collective-permute-start(bf16[2,256,1024]{2,1,0:T(8,128)(2,1)} %get-tuple-element.277), channel_id=1, source_target_pairs={{0,16},{16,0},{1,17},{17,1},{2,18},{18,2},{3,19},{19,3},{4,20},{20... | collective-permute-start | bytes 3145736 | tf_op jit(solution)/shard_map/ppermute | solution.py:34
  (103 other events, 1247.0 us)
Sparse Core Ops, SparseCore 0:
  11.6 242.2 all-gather.6
  259.9 102.1 all-gather.8
  369.9 55.6 all-gather.10
  522.2 98.7 reduce-scatter.4
  623.2 56.7 reduce-scatter.6
  798.1 42.4 reduce-scatter.10
  852.1 43.5 reduce-scatter.8
